TPU v7x, 32 devices: a whole 2x2x4 slice. The times are simulated.
32 devices in a mesh: px: 4 (over z), py: 8 (over y, x, core).
Axes of the slice: x: 2, y: 2, z: 4, core: 2. Of those that a mesh axis runs over, the one named last changes fastest.
Arguments:
- wind_east: bfloat16 [64, 128, 256], P('px', 'py'), may hold values from -4 to 4
- wind_north: bfloat16 [64, 128, 256], P('px', 'py'), may hold values from -4 to 4
- wind_up: bfloat16 [64, 128, 256], P('px', 'py'), may hold values from -4 to 4
Outputs:
- pressure: float32 [64, 128, 256], P('px', 'py')
All inputs are finite; a program needn't handle non-finite values.
Results may differ from a plain program's by a relative error of at most 0.0003.
Values may be sent and summed in bfloat16 or wider, within the bound.
No kernel may reach another device: no remote copies, remote signals or barrier semaphores. Data moves between devices by JAX's collectives and lax.ppermute only.
A program may use at most 64 MiB of HBM per device.

v0:
```python
import functools
import math

import jax
import jax.numpy as jnp
import numpy as np
from jax import lax
from jax.experimental import pallas as pl
from jax.experimental.pallas import tpu as pltpu
from jax.sharding import PartitionSpec as P

NU_BASE = 0.01
SMAGORINSKY = 0.16
STRAIN_FLOOR = 1.0
TIME_STEP = 0.25
HALO = 3
F32 = jnp.float32


def cosine_basis(levels):
    level = np.arange(levels, dtype=np.int64)[:, None]
    mode = np.arange(levels, dtype=np.int64)[None, :]
    radians = math.pi / (2.0 * levels) * ((2 * level + 1) * mode % (4 * levels))
    weight = np.where(mode == 0, math.sqrt(1.0 / levels), math.sqrt(2.0 / levels))
    return (weight * np.cos(radians)).astype(np.float32)


def fourier_basis(length):
    cell = np.arange(length)
    half = length // 2
    columns = [np.full(length, math.sqrt(1.0 / length))]
    waves = [0]
    for wave in range(1, half):
        angle = 2.0 * math.pi * (cell * wave % length) / length
        columns += [math.sqrt(2.0 / length) * np.cos(angle), math.sqrt(2.0 / length) * np.sin(angle)]
        waves += [wave, wave]
    columns.append(math.sqrt(1.0 / length) * (1.0 - 2.0 * (cell % 2)))
    waves.append(half)
    eigen = 4.0 * np.sin(math.pi / length * np.array(waves)) ** 2
    return np.stack(columns, axis=1).astype(np.float32), eigen.astype(np.float32)


def mode_eigen(levels):
    return (4.0 * np.sin(math.pi / (2.0 * levels) * np.arange(levels)) ** 2).astype(np.float32)


def high_dot(left, right, contract):
    return lax.dot_general(
        left, right, (contract, ((), ())), precision=lax.Precision.HIGHEST, preferred_element_type=F32
    )


def with_halo(stacked):
    width = HALO
    pad = -(stacked.shape[2] + 2 * width) % 8
    for axis, dim in (("py", 2), ("px", 1)):
        size, length = lax.axis_size(axis), stacked.shape[dim]
        up = [(i, (i + 1) % size) for i in range(size)]
        down = [(j, i) for i, j in up]
        last = lax.slice_in_dim(stacked, length - width, length, axis=dim)
        leading = lax.slice_in_dim(stacked, 0, width, axis=dim)
        before = lax.ppermute(last, axis, up)
        after = lax.ppermute(leading, axis, down)
        if dim == 2:
            shape = list(stacked.shape)
            shape[2] = pad
            pieces = [stacked, after, jnp.zeros(shape, stacked.dtype), before]
        else:
            pieces = [before, stacked, after]
        stacked = jnp.concatenate(pieces, axis=dim)
    return stacked


def source_kernel(cells_x, cells_y, rim_ref, basis_ref, out_ref, wind, visc, east, part, source):
    rows = wind.shape[2]
    levels = wind.shape[3]
    planes = cells_x + 2 * HALO
    lane = lax.broadcasted_iota(jnp.int32, (rows, levels), 1)
    bottom = lane == 0
    top = lane == levels - 1

    def y_next(values):
        return pltpu.roll(values, rows - 1, 0)

    def y_prev(values):
        return pltpu.roll(values, 1, 0)

    def z_next(values, edge=0.0):
        return jnp.where(top, edge, pltpu.roll(values, levels - 1, 1))

    def z_prev(values, edge=0.0):
        return jnp.where(bottom, edge, pltpu.roll(values, 1, 1))

    def eddy(total):
        return NU_BASE + SMAGORINSKY * jnp.sqrt(total + STRAIN_FLOOR)

    def load(x, carry):
        for c in range(3):
            wind[c, x] = rim_ref[c, x].astype(F32)
        return carry

    lax.fori_loop(0, planes, load, 0)

    def viscosity(x, carry):
        centre = [wind[c, x] for c in range(3)]
        along_x = [wind[c, x + 1] - wind[c, x - 1] for c in range(3)]
        along_y = [y_next(u) - y_prev(u) for u in centre]
        along_z = [z_next(u) - z_prev(u) for u in centre]
        normal = along_x[0] * along_x[0] + along_y[1] * along_y[1] + along_z[2] * along_z[2]
        xy = along_x[1] + along_y[0]
        xz = along_x[2] + along_z[0]
        yz = along_y[2] + along_z[1]
        visc[x] = eddy(0.5 * normal + 0.25 * (xy * xy + xz * xz + yz * yz))
        return carry

    lax.fori_loop(1, planes - 1, viscosity, 0)

    def provisional(x, carry):
        centre = [wind[c, x] for c in range(3)]
        nu = visc[x]
        beyond = eddy(
            0.5 * centre[2] * centre[2] + 0.25 * (centre[0] * centre[0] + centre[1] * centre[1])
        )
        sum_xn = nu + visc[x + 1]
        sum_xp = nu + visc[x - 1]
        sum_yn = nu + y_next(nu)
        sum_yp = nu + y_prev(nu)
        sum_zn = nu + z_next(nu, beyond)
        sum_zp = nu + z_prev(nu, beyond)
        whole = (sum_xn + sum_xp) + (sum_yn + sum_yp) + (sum_zn + sum_zp)
        coef = (
            sum_xn - centre[0],
            sum_xp + centre[0],
            sum_yn - centre[1],
            sum_yp + centre[1],
            sum_zn - centre[2],
            sum_zp + centre[2],
        )

        def one(c):
            u = centre[c]
            total = coef[0] * wind[c, x + 1] + coef[1] * wind[c, x - 1]
            total = total + coef[2] * y_next(u) + coef[3] * y_prev(u)
            total = total + coef[4] * z_next(u) + coef[5] * z_prev(u)
            return u + (0.5 * TIME_STEP) * (total - whole * u)

        east[x] = one(0)
        north = one(1)
        up = one(2)
        up_edge_top = (0.5 * TIME_STEP) * (sum_zn * centre[2])
        up_edge_bottom = (0.5 * TIME_STEP) * (sum_zp * centre[2])
        part[x] = (y_next(north) - y_prev(north)) + (
            z_next(up, up_edge_top) - z_prev(up, up_edge_bottom)
        )
        return carry

    lax.fori_loop(2, planes - 2, provisional, 0)

    def collect(x, carry):
        value = 0.5 * (part[x] + (east[x + 1] - east[x - 1]))
        source[x - HALO] = value[:cells_y]
        return carry

    lax.fori_loop(HALO, planes - HALO, collect, 0)
    flat = source[...].reshape(cells_x * cells_y, levels)
    out_ref[...] = high_dot(basis_ref[...], flat, ((1,), (1,)))


def source_modes(rim, basis_rows, cells_x, cells_y):
    planes, rows, levels = rim.shape[1:]
    return pl.pallas_call(
        functools.partial(source_kernel, cells_x, cells_y),
        out_shape=jax.ShapeDtypeStruct((levels, cells_x * cells_y), F32),
        in_specs=[pl.BlockSpec(memory_space=pltpu.VMEM)] * 2,
        out_specs=pl.BlockSpec(memory_space=pltpu.VMEM),
        scratch_shapes=[
            pltpu.VMEM((3, planes, rows, levels), F32),
            pltpu.VMEM((planes, rows, levels), F32),
            pltpu.VMEM((planes, rows, levels), F32),
            pltpu.VMEM((planes, rows, levels), F32),
            pltpu.VMEM((cells_x, cells_y, levels), F32),
        ],
        name="source_modes",
    )(rim, basis_rows)


def block_transpose(values, width):
    count = len(values)
    values = list(values)
    lane = lax.broadcasted_iota(jnp.int32, values[0].shape, 1) // width
    step = 1
    while step < count:
        odd = (lane & step) != 0
        for i in range(count):
            if i & step:
                continue
            low, high = values[i], values[i + step]
            shift = width * step
            values[i] = jnp.where(odd, pltpu.roll(high, shift, 1), low)
            values[i + step] = jnp.where(odd, high, pltpu.roll(low, low.shape[1] - shift, 1))
        step *= 2
    return values


def solve_kernel(
    east_count, north_count, cells_x, cells_y,
    in_ref, qx_ref, qxt_ref, qy_ref, qyt_ref, ex_ref, ey_ref, em_ref, rank_ref, out_ref, work,
):
    total_x = east_count * cells_x
    total_y = north_count * cells_y
    block = in_ref.shape[1]
    groups = cells_x // north_count
    for a in range(east_count):
        for g in range(groups):
            lanes = slice(g * total_y, (g + 1) * total_y)
            pieces = [in_ref[a * north_count + b, :, lanes] for b in range(north_count)]
            for i, piece in enumerate(block_transpose(pieces, cells_y)):
                row = (a * cells_x + g * north_count + i) * block
                work[row : row + block, :] = piece
    work[...] = high_dot(work[...], qy_ref[...], ((1,), (0,)))
    planes = [work[pl.ds(i, total_x, stride=block), :] for i in range(block)]
    waves = high_dot(qxt_ref[...], jnp.concatenate(planes, axis=1), ((1,), (0,)))
    eigen = ex_ref[...] + ey_ref[0:1, :]
    first = rank_ref[0] * block
    solved = []
    for i in range(block):
        value = eigen + em_ref[first + i]
        empty = value == 0.0
        factor = jnp.where(empty, 0.0, -1.0 / jnp.where(empty, 1.0, value))
        solved.append(waves[:, i * total_y : (i + 1) * total_y] * factor)
    back = high_dot(qx_ref[...], jnp.concatenate(solved, axis=1), ((1,), (0,)))
    for i in range(block):
        work[pl.ds(i, total_x, stride=block), :] = back[:, i * total_y : (i + 1) * total_y]
    work[...] = high_dot(work[...], qyt_ref[...], ((1,), (0,)))
    for a in range(east_count):
        for g in range(groups):
            lanes = slice(g * total_y, (g + 1) * total_y)
            rows = [(a * cells_x + g * north_count + i) * block for i in range(north_count)]
            pieces = [work[row : row + block, :] for row in rows]
            for b, piece in enumerate(block_transpose(pieces, cells_y)):
                out_ref[a * north_count + b, :, lanes] = piece


def solve_planes(blocks, rank, east_count, north_count, cells_x, cells_y, levels):
    total_x = east_count * cells_x
    total_y = north_count * cells_y
    qx, ex = fourier_basis(total_x)
    qy, ey = fourier_basis(total_y)
    vmem = pl.BlockSpec(memory_space=pltpu.VMEM)
    smem = pl.BlockSpec(memory_space=pltpu.SMEM)
    return pl.pallas_call(
        functools.partial(solve_kernel, east_count, north_count, cells_x, cells_y),
        out_shape=jax.ShapeDtypeStruct(blocks.shape, F32),
        in_specs=[vmem] * 7 + [smem] * 2,
        out_specs=vmem,
        scratch_shapes=[pltpu.VMEM((total_x * blocks.shape[1], total_y), F32)],
        name="solve_planes",
    )(
        blocks, qx, np.ascontiguousarray(qx.T), qy, np.ascontiguousarray(qy.T),
        np.ascontiguousarray(np.broadcast_to(ex[:, None], (total_x, total_y))),
        np.ascontiguousarray(np.broadcast_to(ey[None, :], (8, total_y))),
        mode_eigen(levels), rank,
    )


def pressure_kernel(modes_ref, basis_ref, out_ref):
    out_ref[...] = high_dot(modes_ref[...], basis_ref[...], ((0,), (0,)))


def pressure_cells(modes, basis_rows):
    return pl.pallas_call(
        pressure_kernel,
        out_shape=jax.ShapeDtypeStruct((modes.shape[1], basis_rows.shape[1]), F32),
        in_specs=[pl.BlockSpec(memory_space=pltpu.VMEM)] * 2,
        out_specs=pl.BlockSpec(memory_space=pltpu.VMEM),
        name="pressure_cells",
    )(modes, basis_rows)


def rotation(row_count, col_count, length, direction):
    product = (
        lax.broadcasted_iota(jnp.int32, (row_count, col_count), 0)
        * lax.broadcasted_iota(jnp.int32, (row_count, col_count), 1)
        % length
    )
    radians = 2.0 * math.pi / length * product.astype(jnp.float32)
    return (jnp.cos(radians), direction * jnp.sin(radians))


def matmul(table, operand):
    return jnp.dot(
        table, operand, precision=lax.Precision.HIGHEST, preferred_element_type=jnp.float32
    )


def contract(formula, table, operand):
    return jnp.einsum(
        formula, table, operand, precision=lax.Precision.HIGHEST, preferred_element_type=jnp.float32
    )


def transform_rows(real_part, imag_part, direction):
    length = real_part.shape[0]
    width = real_part.shape[1]
    factor_low = 1
    for candidate in range(1, math.isqrt(length) + 1):
        if length % candidate == 0:
            factor_low = candidate
    factor_high = length // factor_low
    cos_high, sin_high = rotation(factor_high, factor_high, factor_high, direction)
    grid_real = real_part.reshape(factor_high, factor_low * width)
    grid_imag = imag_part.reshape(factor_high, factor_low * width)
    section_real = (matmul(cos_high, grid_real) - matmul(sin_high, grid_imag)).reshape(
        factor_high, factor_low, width
    )
    section_imag = (matmul(cos_high, grid_imag) + matmul(sin_high, grid_real)).reshape(
        factor_high, factor_low, width
    )
    turn_cos, turn_sin = rotation(factor_high, factor_low, length, direction)
    turn_cos = turn_cos[:, :, None]
    turn_sin = turn_sin[:, :, None]
    turned_real = section_real * turn_cos - section_imag * turn_sin
    turned_imag = section_real * turn_sin + section_imag * turn_cos
    cos_low, sin_low = rotation(factor_low, factor_low, factor_low, direction)
    out_real = contract("ca,kar->ckr", cos_low, turned_real) - contract(
        "ca,kar->ckr", sin_low, turned_imag
    )
    out_imag = contract("ca,kar->ckr", cos_low, turned_imag) + contract(
        "ca,kar->ckr", sin_low, turned_real
    )
    return (out_real.reshape(length, width), out_imag.reshape(length, width))


def first_forward(flat, high_count, second_cells, level_count):
    total = flat.shape[0]
    width = flat.shape[1]
    low_length = total // high_count
    grid = flat.reshape(low_length, high_count * width)
    cos_low, sin_low = rotation(low_length, low_length, low_length, -1.0)
    section_real = matmul(cos_low, grid).reshape(low_length, high_count, second_cells, level_count)
    section_imag = matmul(sin_low, grid).reshape(low_length, high_count, second_cells, level_count)
    turn_cos, turn_sin = rotation(low_length, high_count, total, -1.0)
    turn_cos = turn_cos[:, :, None, None]
    turn_sin = turn_sin[:, :, None, None]
    turned_real = section_real * turn_cos - section_imag * turn_sin
    turned_imag = section_real * turn_sin + section_imag * turn_cos
    cos_high, sin_high = rotation(high_count, high_count, high_count, -1.0)
    out_real = contract("ca,kaym->cykm", cos_high, turned_real) - contract(
        "ca,kaym->cykm", sin_high, turned_imag
    )
    out_imag = contract("ca,kaym->cykm", cos_high, turned_imag) + contract(
        "ca,kaym->cykm", sin_high, turned_real
    )
    merged = low_length * level_count
    return (
        out_real.reshape(high_count, second_cells, merged),
        out_imag.reshape(high_count, second_cells, merged),
    )


def first_inverse(real_part, imag_part, level_count):
    high_count = real_part.shape[0]
    second_cells = real_part.shape[1]
    low_length = real_part.shape[2] // level_count
    total = high_count * low_length
    data_real = real_part.reshape(high_count, second_cells, low_length, level_count)
    data_imag = imag_part.reshape(high_count, second_cells, low_length, level_count)
    cos_high, sin_high = rotation(high_count, high_count, high_count, 1.0)
    section_real = contract("ac,cykm->kaym", cos_high, data_real) - contract(
        "ac,cykm->kaym", sin_high, data_imag
    )
    section_imag = contract("ac,cykm->kaym", cos_high, data_imag) + contract(
        "ac,cykm->kaym", sin_high, data_real
    )
    turn_cos, turn_sin = rotation(low_length, high_count, total, 1.0)
    turn_cos = turn_cos[:, :, None, None]
    turn_sin = turn_sin[:, :, None, None]
    turned_real = section_real * turn_cos - section_imag * turn_sin
    turned_imag = section_real * turn_sin + section_imag * turn_cos
    cos_low, sin_low = rotation(low_length, low_length, low_length, 1.0)
    flat = matmul(cos_low, turned_real.reshape(low_length, -1)) - matmul(
        sin_low, turned_imag.reshape(low_length, -1)
    )
    return flat.reshape(total, second_cells * level_count)


def solve_modes(
    real_part, imag_part, first_rank, second_rank, first_total, second_total, levels, level_count
):
    low_length = real_part.shape[1] // level_count
    shape_full = (second_total, low_length, level_count)
    wave_second = lax.broadcasted_iota(jnp.int32, shape_full, 0)
    wave_first = second_rank * low_length + lax.broadcasted_iota(jnp.int32, shape_full, 1)
    mode_index = first_rank * level_count + lax.broadcasted_iota(jnp.int32, shape_full, 2)
    eigen = 4.0 * jnp.sin(math.pi / first_total * wave_first.astype(jnp.float32)) ** 2
    eigen = eigen + 4.0 * jnp.sin(math.pi / second_total * wave_second.astype(jnp.float32)) ** 2
    eigen = eigen + 4.0 * jnp.sin(math.pi / (2.0 * levels) * mode_index.astype(jnp.float32)) ** 2
    empty = (wave_first == 0) & (wave_second == 0) & (mode_index == 0)
    factor = jnp.where(empty, 0.0, -1.0 / jnp.where(empty, 1.0, eigen)) / (
        first_total * second_total
    )
    factor = factor.reshape(second_total, low_length * level_count)
    return (real_part * factor, imag_part * factor)


def fold_half(real_part, imag_part, level_count):
    high_count = real_part.shape[0]
    second_cells = real_part.shape[1]
    low_length = real_part.shape[2] // level_count
    half_high = high_count // 2
    half_low = low_length // 2
    nyquist = real_part[half_high, :, :level_count]

    def halve(values):
        kept = values[:half_high].reshape(half_high, second_cells, 2, half_low * level_count)
        return kept.transpose(0, 2, 1, 3).reshape(high_count, second_cells, half_low * level_count)

    kept_real = halve(real_part)
    kept_imag = halve(imag_part).at[0, :, :level_count].set(nyquist)
    return (kept_real, kept_imag)


def solve_half(
    real_part, imag_part, first_rank, second_rank, first_total, second_total, levels, level_count
):
    packed_real = real_part[:, :level_count]
    packed_imag = imag_part[:, :level_count]
    mirror_real = jnp.roll(packed_real[::-1], 1, axis=0)
    mirror_imag = jnp.roll(packed_imag[::-1], 1, axis=0)
    zero_real = 0.5 * (packed_real + mirror_real)
    zero_imag = 0.5 * (packed_imag - mirror_imag)
    nyquist_real = 0.5 * (packed_imag + mirror_imag)
    nyquist_imag = -0.5 * (packed_real - mirror_real)
    first_block = second_rank == 0
    real_part = jnp.where(first_block, real_part.at[:, :level_count].set(zero_real), real_part)
    imag_part = jnp.where(first_block, imag_part.at[:, :level_count].set(zero_imag), imag_part)
    solved_real, solved_imag = solve_modes(
        real_part,
        imag_part,
        first_rank,
        second_rank,
        first_total,
        second_total,
        levels,
        level_count,
    )
    wave_second = lax.broadcasted_iota(jnp.int32, (second_total, level_count), 0)
    mode_index = first_rank * level_count + lax.broadcasted_iota(
        jnp.int32, (second_total, level_count), 1
    )
    eigen = 4.0 + 4.0 * jnp.sin(math.pi / second_total * wave_second.astype(jnp.float32)) ** 2
    eigen = eigen + 4.0 * jnp.sin(math.pi / (2.0 * levels) * mode_index.astype(jnp.float32)) ** 2
    nyquist_factor = -1.0 / eigen / (first_total * second_total)
    solved_nyquist_real = nyquist_real * nyquist_factor
    solved_nyquist_imag = nyquist_imag * nyquist_factor
    joined_real = solved_real[:, :level_count] - solved_nyquist_imag
    joined_imag = solved_imag[:, :level_count] + solved_nyquist_real
    solved_real = jnp.where(
        first_block, solved_real.at[:, :level_count].set(joined_real), solved_real
    )
    solved_imag = jnp.where(
        first_block, solved_imag.at[:, :level_count].set(joined_imag), solved_imag
    )
    return (solved_real, solved_imag)


def unfold_half(real_part, imag_part, level_count):
    high_count = real_part.shape[0]
    second_cells = real_part.shape[1]
    half_low = real_part.shape[2] // level_count
    half_high = high_count // 2
    low_length = 2 * half_low

    def unhalve(values):
        shaped = values.reshape(half_high, 2, second_cells, half_low * level_count)
        return shaped.transpose(0, 2, 1, 3).reshape(
            half_high, second_cells, low_length * level_count
        )

    lower_real = unhalve(real_part)
    lower_imag = unhalve(imag_part)
    zero_line = lower_real[0, :, :level_count]
    nyquist_line = lower_imag[0, :, :level_count]
    upper = jnp.zeros((high_count - half_high, second_cells, low_length * level_count), jnp.float32)
    full_real = jnp.concatenate([2.0 * lower_real, upper], axis=0)
    full_imag = jnp.concatenate([2.0 * lower_imag, upper], axis=0)
    full_real = (
        full_real.at[0, :, :level_count]
        .set(zero_line)
        .at[half_high, :, :level_count]
        .set(nyquist_line)
    )
    full_imag = full_imag.at[0, :, :level_count].set(0.0)
    return (full_real, full_imag)


def spectral(
    modes,
    first_rank,
    second_rank,
    second_count,
    levels,
    send_out,
    send_across,
    bring_back,
    bring_home,
):
    first_count = modes.shape[0]
    first_cells = modes.shape[1]
    merged = modes.shape[2]
    level_count = levels // first_count
    second_cells = merged // level_count
    first_total = first_count * first_cells
    second_total = second_count * second_cells
    pencil = send_out(modes).reshape(first_total, merged)
    line_real, line_imag = first_forward(pencil, second_count, second_cells, level_count)
    line_real, line_imag = fold_half(line_real, line_imag, level_count)
    across_real, across_imag = send_across(line_real, line_imag)
    across_real = across_real.reshape(second_total, -1)
    across_imag = across_imag.reshape(second_total, -1)
    wave_real, wave_imag = transform_rows(across_real, across_imag, -1.0)
    wave_real, wave_imag = solve_half(
        wave_real,
        wave_imag,
        first_rank,
        second_rank,
        first_total,
        second_total,
        levels,
        level_count,
    )
    back_real, back_imag = transform_rows(wave_real, wave_imag, 1.0)
    home_real, home_imag = bring_back(
        back_real.reshape(1, second_total, -1), back_imag.reshape(1, second_total, -1)
    )
    home_real, home_imag = unfold_half(home_real, home_imag, level_count)
    flat = first_inverse(home_real, home_imag, level_count)
    return bring_home(flat.reshape(1, first_total, merged))


def staged(modes, east_count, north_count, cells_x, cells_y):
    levels = modes.shape[0]
    level_count = levels // east_count

    def send_out(values):
        return lax.all_to_all(values, "px", split_axis=0, concat_axis=1, tiled=True)

    def send_across(real_part, imag_part):
        return (
            lax.all_to_all(real_part, "py", split_axis=0, concat_axis=1, tiled=True),
            lax.all_to_all(imag_part, "py", split_axis=0, concat_axis=1, tiled=True),
        )

    def bring_back(real_part, imag_part):
        return (
            lax.all_to_all(real_part, "py", split_axis=1, concat_axis=0, tiled=True),
            lax.all_to_all(imag_part, "py", split_axis=1, concat_axis=0, tiled=True),
        )

    def bring_home(values):
        return lax.all_to_all(values, "px", split_axis=1, concat_axis=0, tiled=True)

    shaped = modes.reshape(east_count, level_count, cells_x, cells_y).transpose(0, 2, 3, 1)
    result = spectral(
        shaped.reshape(east_count, cells_x, cells_y * level_count),
        lax.axis_index("px"),
        lax.axis_index("py"),
        north_count,
        levels,
        send_out,
        send_across,
        bring_back,
        bring_home,
    )
    result = result.reshape(east_count, cells_x, cells_y, level_count).transpose(0, 3, 1, 2)
    return result.reshape(levels, cells_x * cells_y)


def shards(wind_east, wind_north, wind_up):
    cells_x, cells_y, levels = wind_east.shape
    east_count = lax.axis_size("px")
    north_count = lax.axis_size("py")
    devices = east_count * north_count
    basis_rows = np.ascontiguousarray(cosine_basis(levels).T)
    rim = with_halo(jnp.stack((wind_east, wind_north, wind_up)))
    modes = source_modes(rim, basis_rows, cells_x, cells_y)
    if levels == 8 * devices and north_count * cells_y == 128 and cells_x % north_count == 0:
        blocks = modes.reshape(devices, levels // devices, cells_x * cells_y)
        blocks = lax.all_to_all(blocks, ("px", "py"), split_axis=0, concat_axis=0, tiled=True)
        rank = (lax.axis_index("px") * north_count + lax.axis_index("py")).reshape(1)
        blocks = solve_planes(blocks, rank, east_count, north_count, cells_x, cells_y, levels)
        blocks = lax.all_to_all(blocks, ("px", "py"), split_axis=0, concat_axis=0, tiled=True)
        modes = blocks.reshape(levels, cells_x * cells_y)
    else:
        modes = staged(modes, east_count, north_count, cells_x, cells_y)
    return pressure_cells(modes, basis_rows).reshape(cells_x, cells_y, levels)


def solution(mesh):
    return jax.shard_map(
        shards,
        mesh=mesh,
        in_specs=(P("px", "py", None), P("px", "py", None), P("px", "py", None)),
        out_specs=P("px", "py", None),
        check_vma=False,
    )
```

profile of v0, /device:TPU:0, one launch (start us, length us, event | category | flops | bytes accessed | tf_op | source)
XLA Modules:
  0.0 62.5 jit_solution(9250420982915526970)
XLA Ops:
  0.0 0.0 copy-start.2
  0.0 0.0 copy-start.1
  0.0 0.0 copy-start
  0.0 1.1 %pad_maximum_fusion.9 = (bf16[3,16,3,256]{3,2,1,0:T(4,128)(2,1)S(1)}, bf16[3,16,3,256]{3,2,1,0:T(4,128)(2,1)S(1)}) fusion(bf16[1,16,16,256]{3,2,1,0:T(8,128)(2,1)} %bitcast.7, bf16[1,16,16,256]{3,2,1,0:T(8,128)(2,1)} %bitcast.10, bf16[1,16,16,256]{3,2,1,0:T(8,128)(2,1)} %bitcast.13), kind=kLoop, calls=%fused_computation.9 | loop fusion | flops 442368 | bytes 540672 | tf_op jit(solution)/shard_map/slice | solution.py:61
  1.1 3.4 %collective-permute-start = (bf16[3,16,3,256]{3,2,1,0:T(4,128)(2,1)S(1)}, bf16[3,16,3,256]{3,2,1,0:T(4,128)(2,1)S(1)}, u32[]{:S(2)}, u32[]{:S(2)}) collective-permute-start(bf16[3,16,3,256]{3,2,1,0:T(4,128)(2,1)S(1)} %get-tuple-element.7), channel_id=1, source_target_pairs={{1,0},{2,1},{3,2},{4,3},{5,4},{6,5},{7,6},{0,7},{9,8},{10,9},{11,1... | collective-permute-start | bytes 221192 | tf_op jit(solution)/shard_map/ppermute | solution.py:63
  4.6 0.0 collective-permute-start.1
  4.6 2.3 %collective-permute-done = bf16[3,16,3,256]{3,2,1,0:T(4,128)(2,1)S(1)} collective-permute-done((bf16[3,16,3,256]{3,2,1,0:T(4,128)(2,1)S(1)}, bf16[3,16,3,256]{3,2,1,0:T(4,128)(2,1)S(1)}, u32[]{:S(2)}, u32[]{:S(2)}) %collective-permute-start) | collective-permute-done | bytes 73760 | tf_op jit(solution)/shard_map/ppermute | solution.py:63
  6.8 2.7 %collective-permute-done.1 = bf16[3,16,3,256]{3,2,1,0:T(4,128)(2,1)S(1)} collective-permute-done((bf16[3,16,3,256]{3,2,1,0:T(4,128)(2,1)S(1)}, bf16[3,16,3,256]{3,2,1,0:T(4,128)(2,1)S(1)}, u32[]{:S(2)}, u32[]{:S(2)}) %collective-permute-start.1) | collective-permute-done | bytes 73760 | tf_op jit(solution)/shard_map/ppermute | solution.py:62
  9.5 0.9 %pad_maximum_fusion.6 = (bf16[3,3,24,256]{3,2,1,0:T(8,128)(2,1)S(1)}, bf16[3,3,24,256]{3,2,1,0:T(8,128)(2,1)S(1)}) fusion(bf16[3,16,3,256]{3,2,1,0:T(4,128)(2,1)S(1)} %collective-permute-done.1, bf16[3,16,2,256]{3,2,1,0:T(2,128)(2,1)S(1)} %broadcast_in_dim.3, bf16[3,16,3,256]{3,2,1,0:T(4,128)(2,1)S(1)} %collective-permute-done, ...), kind=kLoop, calls=%fused_computation.6 | loop fusion | flops 1327104 | bytes 811008 | tf_op jit(solution)/shard_map/slice | solution.py:60
  10.4 1.6 %collective-permute-start.2 = (bf16[3,3,24,256]{3,2,1,0:T(8,128)(2,1)S(1)}, bf16[3,3,24,256]{3,2,1,0:T(8,128)(2,1)S(1)}, u32[]{:S(2)}, u32[]{:S(2)}) collective-permute-start(bf16[3,3,24,256]{3,2,1,0:T(8,128)(2,1)S(1)} %get-tuple-element.5), channel_id=1, source_target_pairs={{0,8},{8,16},{16,24},{24,0},{1,9},{9,17},{17,25},{25,1},{2,10},{10... | collective-permute-start | bytes 331784 | tf_op jit(solution)/shard_map/ppermute | solution.py:62
  12.1 2.2 %collective-permute-start.3 = (bf16[3,3,24,256]{3,2,1,0:T(8,128)(2,1)S(1)}, bf16[3,3,24,256]{3,2,1,0:T(8,128)(2,1)S(1)}, u32[]{:S(2)}, u32[]{:S(2)}) collective-permute-start(bf16[3,3,24,256]{3,2,1,0:T(8,128)(2,1)S(1)} %get-tuple-element.6), channel_id=1, source_target_pairs={{8,0},{16,8},{24,16},{0,24},{9,1},{17,9},{25,17},{1,25},{10,2},{18... | collective-permute-start | bytes 331784 | tf_op jit(solution)/shard_map/ppermute | solution.py:63
  14.3 2.8 %collective-permute-done.2 = bf16[3,3,24,256]{3,2,1,0:T(8,128)(2,1)S(1)} collective-permute-done((bf16[3,3,24,256]{3,2,1,0:T(8,128)(2,1)S(1)}, bf16[3,3,24,256]{3,2,1,0:T(8,128)(2,1)S(1)}, u32[]{:S(2)}, u32[]{:S(2)}) %collective-permute-start.2) | collective-permute-done | bytes 110624 | tf_op jit(solution)/shard_map/ppermute | solution.py:62
  17.1 0.9 %collective-permute-done.3 = bf16[3,3,24,256]{3,2,1,0:T(8,128)(2,1)S(1)} collective-permute-done((bf16[3,3,24,256]{3,2,1,0:T(8,128)(2,1)S(1)}, bf16[3,3,24,256]{3,2,1,0:T(8,128)(2,1)S(1)}, u32[]{:S(2)}, u32[]{:S(2)}) %collective-permute-start.3) | collective-permute-done | bytes 110624 | tf_op jit(solution)/shard_map/ppermute | solution.py:63
  18.0 0.0 copy-done.2
  18.0 0.0 copy-done.1
  18.0 0.0 copy-done
  18.0 1.1 %pad_maximum_fusion.rim_ref = bf16[3,22,24,256]{3,2,1,0:T(8,128)(2,1)} fusion(bf16[3,3,24,256]{3,2,1,0:T(8,128)(2,1)S(1)} %collective-permute-done.3, bf16[3,16,3,256]{3,2,1,0:T(4,128)(2,1)S(1)} %collective-permute-done.1, bf16[3,16,2,256]{3,2,1,0:T(2,128)(2,1)S(1)} %broadcast_in_dim.3, bf16[3,16,3,256]{3,2,1,0:T(4,128)(2,1)S(1)} %collective-permute-done, ...), kind=kLoop, calls=%fused_computation | loop fusion | flops 6488064 | bytes 1622016 | tf_op jit(solution)/shard_map/concatenate | solution.py:70
  19.1 8.5 %source_modes.1 = f32[256,256]{1,0:T(8,128)} custom-call(bf16[3,22,24,256]{3,2,1,0:T(8,128)(2,1)} %pad_maximum_fusion.rim_ref, f32[256,256]{1,0:T(8,128)} %constant.28.clone.basis_ref), custom_call_target="tpu_custom_call" | custom-call | tf_op jit(solution)/shard_map/source_modes/pallas_call | solution.py:171
  27.6 3.8 %all-to-all-start = ((f32[32,8,256]{2,1,0:T(8,128)}), f32[32,8,256]{2,1,0:T(8,128)S(1)}, u32[]{:S(2)}, u32[]{:S(2)}) async-start(f32[32,8,256]{2,1,0:T(8,128)} %bitcast.17), calls=%async_computation | async-start | bytes 524288 | tf_op jit(solution)/shard_map/all_to_all | solution.py:589
  31.4 10.6 %all-to-all-done.in_ref = f32[32,8,256]{2,1,0:T(8,128)S(1)} async-done(((f32[32,8,256]{2,1,0:T(8,128)}), f32[32,8,256]{2,1,0:T(8,128)S(1)}, u32[]{:S(2)}, u32[]{:S(2)}) %all-to-all-start) | async-done | bytes 262176 | tf_op jit(solution)/shard_map/all_to_all | solution.py:589
  42.0 0.0 copy-start.3
  42.0 0.7 %copy-done.3 = f32[32,8,256]{2,1,0:T(8,128)} copy-done((f32[32,8,256]{2,1,0:T(8,128)}, f32[32,8,256]{2,1,0:T(8,128)S(1)}, u32[]{:S(2)}) %copy-start.3) | copy-done | bytes 262168
  42.7 3.8 %solve_planes.1 = f32[32,8,256]{2,1,0:T(8,128)} custom-call(f32[32,8,256]{2,1,0:T(8,128)} %copy-done.3, f32[64,64]{1,0:T(8,128)} %constant.29.clone.qx_ref, f32[64,64]{1,0:T(8,128)} %constant.30.clone.qxt_ref, f32[128,128]{1,0:T(8,128)} %constant.31.clone.qy_ref, f32[128,128]{1,0:T(8,128)} %constant.32.clone.qyt_ref, f32[64,128]{1,0:T(8,128)} %constant.33.clone.ex_ref, ...), custom_call_target="tpu_custom_call" | custom-call | tf_op jit(solution)/shard_map/solve_planes/pallas_call | solution.py:251
  46.5 13.8 %all_to_all.10 = f32[32,8,256]{2,1,0:T(8,128)} all-to-all(f32[32,8,256]{2,1,0:T(8,128)} %solve_planes.1), channel_id=1, replica_groups=mesh['px'=4,'py'=8] {'px','py'}, dimensions={0} | all-to-all | bytes 524288 | tf_op jit(solution)/shard_map/all_to_all | solution.py:592
  60.4 2.1 %pressure_cells.1 = f32[256,256]{1,0:T(8,128)} custom-call(f32[256,256]{1,0:T(8,128)} %bitcast.16, f32[256,256]{1,0:T(8,128)} %constant.28.clone.basis_ref), custom_call_target="tpu_custom_call" | custom-call | tf_op jit(solution)/shard_map/pressure_cells/pallas_call | solution.py:271
  (1 shorter events, 0.0 us)
Async XLA Ops:
  0.0 18.0 %copy-start.2 = (bf16[16,16,256]{2,1,0:T(8,128)(2,1)S(1)}, bf16[16,16,256]{2,1,0:T(8,128)(2,1)}, u32[]{:S(2)}) copy-start(bf16[16,16,256]{2,1,0:T(8,128)(2,1)} %param.11) | copy-start | bytes 393220
  0.0 18.0 %copy-start.1 = (bf16[16,16,256]{2,1,0:T(8,128)(2,1)S(1)}, bf16[16,16,256]{2,1,0:T(8,128)(2,1)}, u32[]{:S(2)}) copy-start(bf16[16,16,256]{2,1,0:T(8,128)(2,1)} %param.12) | copy-start | bytes 393220
  0.0 18.0 %copy-start = (bf16[16,16,256]{2,1,0:T(8,128)(2,1)S(1)}, bf16[16,16,256]{2,1,0:T(8,128)(2,1)}, u32[]{:S(2)}) copy-start(bf16[16,16,256]{2,1,0:T(8,128)(2,1)} %param.13) | copy-start | bytes 393220
  1.1 5.7 %collective-permute-start = (bf16[3,16,3,256]{3,2,1,0:T(4,128)(2,1)S(1)}, bf16[3,16,3,256]{3,2,1,0:T(4,128)(2,1)S(1)}, u32[]{:S(2)}, u32[]{:S(2)}) collective-permute-start(bf16[3,16,3,256]{3,2,1,0:T(4,128)(2,1)S(1)} %get-tuple-element.7), channel_id=1, source_target_pairs={{1,0},{2,1},{3,2},{4,3},{5,4},{6,5},{7,6},{0,7},{9,8},{10,9},{11,1... | collective-permute-start | bytes 221192 | tf_op jit(solution)/shard_map/ppermute | solution.py:63
  4.6 4.9 %collective-permute-start.1 = (bf16[3,16,3,256]{3,2,1,0:T(4,128)(2,1)S(1)}, bf16[3,16,3,256]{3,2,1,0:T(4,128)(2,1)S(1)}, u32[]{:S(2)}, u32[]{:S(2)}) collective-permute-start(bf16[3,16,3,256]{3,2,1,0:T(4,128)(2,1)S(1)} %get-tuple-element.8), channel_id=1, source_target_pairs={{0,1},{1,2},{2,3},{3,4},{4,5},{5,6},{6,7},{7,0},{8,9},{9,10},{10,1... | collective-permute-start | bytes 221192 | tf_op jit(solution)/shard_map/ppermute | solution.py:62
  10.4 6.7 %collective-permute-start.2 = (bf16[3,3,24,256]{3,2,1,0:T(8,128)(2,1)S(1)}, bf16[3,3,24,256]{3,2,1,0:T(8,128)(2,1)S(1)}, u32[]{:S(2)}, u32[]{:S(2)}) collective-permute-start(bf16[3,3,24,256]{3,2,1,0:T(8,128)(2,1)S(1)} %get-tuple-element.5), channel_id=1, source_target_pairs={{0,8},{8,16},{16,24},{24,0},{1,9},{9,17},{17,25},{25,1},{2,10},{10... | collective-permute-start | bytes 331784 | tf_op jit(solution)/shard_map/ppermute | solution.py:62
  12.1 5.9 %collective-permute-start.3 = (bf16[3,3,24,256]{3,2,1,0:T(8,128)(2,1)S(1)}, bf16[3,3,24,256]{3,2,1,0:T(8,128)(2,1)S(1)}, u32[]{:S(2)}, u32[]{:S(2)}) collective-permute-start(bf16[3,3,24,256]{3,2,1,0:T(8,128)(2,1)S(1)} %get-tuple-element.6), channel_id=1, source_target_pairs={{8,0},{16,8},{24,16},{0,24},{9,1},{17,9},{25,17},{1,25},{10,2},{18... | collective-permute-start | bytes 331784 | tf_op jit(solution)/shard_map/ppermute | solution.py:63
  27.6 14.4 %all-to-all-start = ((f32[32,8,256]{2,1,0:T(8,128)}), f32[32,8,256]{2,1,0:T(8,128)S(1)}, u32[]{:S(2)}, u32[]{:S(2)}) async-start(f32[32,8,256]{2,1,0:T(8,128)} %bitcast.17), calls=%async_computation | async-start | bytes 524288 | tf_op jit(solution)/shard_map/all_to_all | solution.py:589
  42.0 0.7 %copy-start.3 = (f32[32,8,256]{2,1,0:T(8,128)}, f32[32,8,256]{2,1,0:T(8,128)S(1)}, u32[]{:S(2)}) copy-start(f32[32,8,256]{2,1,0:T(8,128)S(1)} %all-to-all-done.in_ref) | copy-start | bytes 786436
where the time goes:
time: 62.9 us; the launch traced here: 62.5 us
  waiting for transfers between devices  19.2 us (31%)
  Pallas kernels  14.5 us (23%)
  blocking collectives  13.8 us (22%)
  starting transfers between devices  11.1 us (18%)
  other arithmetic  3.17 us (5%)
  local copies, waits for them, and re-layouts  0.74 us (1%)
    all_to_all x1, blocking collectives, shards(): lax.all_to_all(blocks, ('px', 'py'), split_axis=0, concat_axis=0, tiled=T...  13.8 us
    all_to_all x1, waiting for transfers between devices, shards(): lax.all_to_all(blocks, ('px', 'py'), split_axis=0, concat_axis=0, tiled=T...  10.6 us
    pallas_call x1, Pallas kernels, source_modes(): pl.pallas_call(functools.partial(source_kernel, cells_x, cells_y), out_sh...  8.48 us
    ppermute x2, starting transfers between devices, with_halo(): after = lax.ppermute(leading, axis, down)  5.67 us
    ppermute x2, waiting for transfers between devices, with_halo(): before = lax.ppermute(last, axis, up)  5.48 us
    pallas_call x1, Pallas kernels, solve_planes(): pl.pallas_call(functools.partial(solve_kernel, east_count, north_count, c...  3.85 us
    all_to_all x1, starting transfers between devices, shards(): lax.all_to_all(blocks, ('px', 'py'), split_axis=0, concat_axis=0, tiled=T...  3.79 us
    ppermute x2, waiting for transfers between devices, with_halo(): after = lax.ppermute(leading, axis, down)  3.14 us
  transfers between devices with their start and end apart: 5, of which 5 were waited for; matrix products, arithmetic and copies ran while one was open for 0% of the time, Pallas kernels for 0%

commit v1 on v0

--- a/solution.py
+++ b/solution.py
@@ -3,6 +3,7 @@
 
 import jax
 import jax.numpy as jnp
+import ml_dtypes
 import numpy as np
 from jax import lax
 from jax.experimental import pallas as pl
@@ -14,7 +15,12 @@
 STRAIN_FLOOR = 1.0
 TIME_STEP = 0.25
 HALO = 3
+LANES = 128
 F32 = jnp.float32
+BF16 = jnp.bfloat16
+FORWARD = 3
+INVERSE = 2
+KERNEL_VMEM = pltpu.CompilerParams(vmem_limit_bytes=24 * 2**20)
 
 
 def cosine_basis(levels):
@@ -44,144 +50,250 @@
     return (4.0 * np.sin(math.pi / (2.0 * levels) * np.arange(levels)) ** 2).astype(np.float32)
 
 
-def high_dot(left, right, contract):
-    return lax.dot_general(
-        left, right, (contract, ((), ())), precision=lax.Precision.HIGHEST, preferred_element_type=F32
-    )
-
-
-def with_halo(stacked):
-    width = HALO
-    pad = -(stacked.shape[2] + 2 * width) % 8
-    for axis, dim in (("py", 2), ("px", 1)):
-        size, length = lax.axis_size(axis), stacked.shape[dim]
-        up = [(i, (i + 1) % size) for i in range(size)]
-        down = [(j, i) for i, j in up]
-        last = lax.slice_in_dim(stacked, length - width, length, axis=dim)
-        leading = lax.slice_in_dim(stacked, 0, width, axis=dim)
-        before = lax.ppermute(last, axis, up)
-        after = lax.ppermute(leading, axis, down)
-        if dim == 2:
-            shape = list(stacked.shape)
-            shape[2] = pad
-            pieces = [stacked, after, jnp.zeros(shape, stacked.dtype), before]
-        else:
-            pieces = [before, stacked, after]
-        stacked = jnp.concatenate(pieces, axis=dim)
-    return stacked
-
-
-def source_kernel(cells_x, cells_y, rim_ref, basis_ref, out_ref, wind, visc, east, part, source):
+PAIRS = {2: ((0, 0), (0, 1), (1, 0)), 3: ((0, 0), (0, 1), (1, 0), (1, 1), (0, 2), (2, 0))}
+
+
+def parts_of(values, count, narrow):
+    parts = []
+    for _ in range(count):
+        parts.append(values.astype(narrow))
+        values = values - parts[-1].astype(values.dtype)
+    return parts
+
+
+def table_parts(table, axis, count):
+    parts = parts_of(table, count, ml_dtypes.bfloat16)
+    return np.ascontiguousarray(np.concatenate([parts[t] for t, _ in PAIRS[count]], axis=axis))
+
+
+def value_parts(values, axis, count):
+    parts = parts_of(values, count, BF16)
+    return jnp.concatenate([parts[v] for _, v in PAIRS[count]], axis=axis)
+
+
+def dot(left, right, contract):
+    return lax.dot_general(left, right, (contract, ((), ())), preferred_element_type=F32)
+
+
+def on_chip(values):
+    return pltpu.with_memory_space_constraint(values, pltpu.VMEM)
+
+
+def ring(axis):
+    size = lax.axis_size(axis)
+    up = [(i, (i + 1) % size) for i in range(size)]
+    return up, [(j, i) for i, j in up]
+
+
+def lane_blocks(values):
+    return [values[:, i : i + LANES] for i in range(0, values.shape[1], LANES)]
+
+
+def z_next(values, edge):
+    lane = lax.broadcasted_iota(jnp.int32, (values.shape[0], LANES), 1)
+    turned = [pltpu.roll(block, LANES - 1, 1) for block in lane_blocks(values)] + [edge]
+    last = lane == LANES - 1
+    pairs = zip(turned[1:], turned[:-1])
+    return jnp.concatenate([jnp.where(last, after, here) for after, here in pairs], axis=1)
+
+
+def z_prev(values, edge):
+    lane = lax.broadcasted_iota(jnp.int32, (values.shape[0], LANES), 1)
+    turned = [edge] + [pltpu.roll(block, 1, 1) for block in lane_blocks(values)]
+    pairs = zip(turned[:-1], turned[1:])
+    return jnp.concatenate([jnp.where(lane == 0, before, here) for before, here in pairs], axis=1)
+
+
+def y_next(values):
+    return pltpu.roll(values, values.shape[0] - 1, 0)
+
+
+def y_prev(values):
+    return pltpu.roll(values, 1, 0)
+
+
+def eddy(total):
+    root = total + 4.0 * STRAIN_FLOOR
+    return NU_BASE + (0.5 * SMAGORINSKY) * (root * lax.rsqrt(root))
+
+
+def visc_plane(x, wind, above, below, visc):
+    along_x = [wind[c, x + 1] - wind[c, x - 1] for c in range(3)]
+    along_y = [y_next(wind[c, x]) - y_prev(wind[c, x]) for c in range(3)]
+    along_z = [above[c, x] - below[c, x] for c in range(3)]
+    normal = along_x[0] * along_x[0] + along_y[1] * along_y[1] + along_z[2] * along_z[2]
+    xy = along_x[1] + along_y[0]
+    xz = along_x[2] + along_z[0]
+    yz = along_y[2] + along_z[1]
+    visc[x] = eddy((normal + normal) + (xy * xy + xz * xz + yz * yz))
+
+
+def wind_plane(x, wind, above, below, visc, east, part):
+    cells = east.shape[1]
+    centre = [wind[c, x] for c in range(3)]
+    nu = visc[x]
+    lane = lax.broadcasted_iota(jnp.int32, (nu.shape[0], LANES), 1)
+    ends = [jnp.where(lane < LANES // 2, u[:, :LANES], u[:, -LANES:]) for u in centre]
+    beyond = eddy(2.0 * (ends[2] * ends[2]) + (ends[0] * ends[0] + ends[1] * ends[1]))
+    sum_xn = nu + visc[x + 1]
+    sum_xp = nu + visc[x - 1]
+    sum_yn = nu + y_next(nu)
+    sum_yp = nu + y_prev(nu)
+    sum_zn = nu + z_next(nu, beyond)
+    sum_zp = nu + z_prev(nu, beyond)
+    whole = ((sum_xn + sum_xp) + (sum_yn + sum_yp)) + ((sum_zn + sum_zp) - 2.0 / TIME_STEP)
+    coef = (
+        sum_xn - centre[0],
+        sum_xp + centre[0],
+        sum_yn - centre[1],
+        sum_yp + centre[1],
+        sum_zn - centre[2],
+        sum_zp + centre[2],
+    )
+
+    def one(c, rows):
+        u = centre[c]
+        total = coef[0][:rows] * wind[c, x + 1, :rows] + coef[1][:rows] * wind[c, x - 1, :rows]
+        total += coef[2][:rows] * y_next(u)[:rows] + coef[3][:rows] * y_prev(u)[:rows]
+        total += coef[4][:rows] * above[c, x, :rows] + coef[5][:rows] * below[c, x, :rows]
+        return total - whole[:rows] * u[:rows]
+
+    east[x] = one(0, cells)
+    north = one(1, nu.shape[0])
+    up = one(2, cells)
+    edge = centre[2][:cells]
+    top = sum_zn[:cells, -LANES:] * edge[:, -LANES:]
+    bottom = sum_zp[:cells, :LANES] * edge[:, :LANES]
+    part[x] = (y_next(north) - y_prev(north))[:cells] + (z_next(up, top) - z_prev(up, bottom))
+
+
+def store_plane(c, x, plane, wind, above, below):
+    none = jnp.zeros((plane.shape[0], LANES), F32)
+    wind[c, x] = plane
+    above[c, x] = z_next(plane, none)
+    below[c, x] = z_prev(plane, none)
+
+
+def each(first, last, body, jump=0, skip=0):
+    def step(i, carry):
+        body(i + jnp.where(i >= first + jump, skip, 0) if skip else i)
+        return carry
+
+    lax.fori_loop(first, last, step, 0)
+
+
+def inner_kernel(winds_ref, before_ref, after_ref, wind, above, below, visc, east, part):
+    cells_x, cells_y, levels = winds_ref.shape[1:]
     rows = wind.shape[2]
-    levels = wind.shape[3]
+    gap = jnp.zeros((rows - cells_y - 2 * HALO, levels), F32)
+
+    def load(x):
+        for c in range(3):
+            pieces = [winds_ref[c, x], after_ref[c, x], before_ref[c, x]]
+            own, after, before = [piece.astype(F32) for piece in pieces]
+            plane = jnp.concatenate([own, after, gap, before], axis=0)
+            store_plane(c, x + HALO, plane, wind, above, below)
+
+    each(0, cells_x, load)
+    first, last = HALO, HALO + cells_x
+    each(first + 1, last - 1, lambda x: visc_plane(x, wind, above, below, visc))
+    each(first + 2, last - 2, lambda x: wind_plane(x, wind, above, below, visc, east, part))
+
+
+def outer_kernel(low_ref, high_ref, basis_ref, *refs):
+    wind, above, below, visc, east, part = refs[6:12]
+    out_ref, source = refs[12:]
+    cells_x, cells_y, levels = source.shape
+    skip = cells_x
+
+    def load(x):
+        for c in range(3):
+            for ref, start in ((low_ref, 0), (high_ref, HALO + cells_x)):
+                store_plane(c, x + start, ref[c, x].astype(F32), wind, above, below)
+
+    each(0, HALO, load)
+    each(1, 7, lambda x: visc_plane(x, wind, above, below, visc), 3, skip - 2)
+    each(2, 8, lambda x: wind_plane(x, wind, above, below, visc, east, part), 3, skip - 4)
+
+    def collect(x):
+        source[x] = part[x + HALO] + (east[x + HALO + 1] - east[x + HALO - 1])
+
+    each(0, cells_x, collect)
+    flat = source[...].reshape(cells_x * cells_y, levels)
+    out_ref[...] = dot(basis_ref[...], value_parts(flat, 1, FORWARD), ((1,), (1,)))
+
+
+def pack_kernel(east_ref, north_ref, up_ref, winds_ref, leading_ref, last_ref):
+    cells_x, cells_y, levels = east_ref.shape
+
+    def plane(x):
+        for c, ref in enumerate((east_ref, north_ref, up_ref)):
+            own = ref[x]
+            winds_ref[c, x] = own
+            wide = own.astype(F32)
+            leading_ref[c, x] = wide[:HALO].astype(BF16)
+            last_ref[c, x] = wide[cells_y - HALO :].astype(BF16)
+
+    each(0, cells_x, plane)
+
+
+def pack_winds(winds):
+    cells_x, cells_y, levels = winds[0].shape
+    vmem = pl.BlockSpec(memory_space=pltpu.VMEM)
+    edge = pltpu.VMEM((3, cells_x, HALO, levels), BF16)
+    return pl.pallas_call(
+        pack_kernel,
+        out_shape=[pltpu.VMEM((3, cells_x, cells_y, levels), BF16), edge, edge],
+        in_specs=[vmem] * 3,
+        out_specs=[vmem] * 3,
+        compiler_params=KERNEL_VMEM,
+        name="pack_winds",
+    )(*[pltpu.with_memory_space_constraint(wind, pltpu.HBM) for wind in winds])
+
+
+def source_modes(winds, basis_rows):
+    cells_x, cells_y, levels = winds[0].shape
     planes = cells_x + 2 * HALO
-    lane = lax.broadcasted_iota(jnp.int32, (rows, levels), 1)
-    bottom = lane == 0
-    top = lane == levels - 1
-
-    def y_next(values):
-        return pltpu.roll(values, rows - 1, 0)
-
-    def y_prev(values):
-        return pltpu.roll(values, 1, 0)
-
-    def z_next(values, edge=0.0):
-        return jnp.where(top, edge, pltpu.roll(values, levels - 1, 1))
-
-    def z_prev(values, edge=0.0):
-        return jnp.where(bottom, edge, pltpu.roll(values, 1, 1))
-
-    def eddy(total):
-        return NU_BASE + SMAGORINSKY * jnp.sqrt(total + STRAIN_FLOOR)
-
-    def load(x, carry):
-        for c in range(3):
-            wind[c, x] = rim_ref[c, x].astype(F32)
-        return carry
-
-    lax.fori_loop(0, planes, load, 0)
-
-    def viscosity(x, carry):
-        centre = [wind[c, x] for c in range(3)]
-        along_x = [wind[c, x + 1] - wind[c, x - 1] for c in range(3)]
-        along_y = [y_next(u) - y_prev(u) for u in centre]
-        along_z = [z_next(u) - z_prev(u) for u in centre]
-        normal = along_x[0] * along_x[0] + along_y[1] * along_y[1] + along_z[2] * along_z[2]
-        xy = along_x[1] + along_y[0]
-        xz = along_x[2] + along_z[0]
-        yz = along_y[2] + along_z[1]
-        visc[x] = eddy(0.5 * normal + 0.25 * (xy * xy + xz * xz + yz * yz))
-        return carry
-
-    lax.fori_loop(1, planes - 1, viscosity, 0)
-
-    def provisional(x, carry):
-        centre = [wind[c, x] for c in range(3)]
-        nu = visc[x]
-        beyond = eddy(
-            0.5 * centre[2] * centre[2] + 0.25 * (centre[0] * centre[0] + centre[1] * centre[1])
-        )
-        sum_xn = nu + visc[x + 1]
-        sum_xp = nu + visc[x - 1]
-        sum_yn = nu + y_next(nu)
-        sum_yp = nu + y_prev(nu)
-        sum_zn = nu + z_next(nu, beyond)
-        sum_zp = nu + z_prev(nu, beyond)
-        whole = (sum_xn + sum_xp) + (sum_yn + sum_yp) + (sum_zn + sum_zp)
-        coef = (
-            sum_xn - centre[0],
-            sum_xp + centre[0],
-            sum_yn - centre[1],
-            sum_yp + centre[1],
-            sum_zn - centre[2],
-            sum_zp + centre[2],
-        )
-
-        def one(c):
-            u = centre[c]
-            total = coef[0] * wind[c, x + 1] + coef[1] * wind[c, x - 1]
-            total = total + coef[2] * y_next(u) + coef[3] * y_prev(u)
-            total = total + coef[4] * z_next(u) + coef[5] * z_prev(u)
-            return u + (0.5 * TIME_STEP) * (total - whole * u)
-
-        east[x] = one(0)
-        north = one(1)
-        up = one(2)
-        up_edge_top = (0.5 * TIME_STEP) * (sum_zn * centre[2])
-        up_edge_bottom = (0.5 * TIME_STEP) * (sum_zp * centre[2])
-        part[x] = (y_next(north) - y_prev(north)) + (
-            z_next(up, up_edge_top) - z_prev(up, up_edge_bottom)
-        )
-        return carry
-
-    lax.fori_loop(2, planes - 2, provisional, 0)
-
-    def collect(x, carry):
-        value = 0.5 * (part[x] + (east[x + 1] - east[x - 1]))
-        source[x - HALO] = value[:cells_y]
-        return carry
-
-    lax.fori_loop(HALO, planes - HALO, collect, 0)
-    flat = source[...].reshape(cells_x * cells_y, levels)
-    out_ref[...] = high_dot(basis_ref[...], flat, ((1,), (1,)))
-
-
-def source_modes(rim, basis_rows, cells_x, cells_y):
-    planes, rows, levels = rim.shape[1:]
-    return pl.pallas_call(
-        functools.partial(source_kernel, cells_x, cells_y),
-        out_shape=jax.ShapeDtypeStruct((levels, cells_x * cells_y), F32),
-        in_specs=[pl.BlockSpec(memory_space=pltpu.VMEM)] * 2,
-        out_specs=pl.BlockSpec(memory_space=pltpu.VMEM),
-        scratch_shapes=[
-            pltpu.VMEM((3, planes, rows, levels), F32),
-            pltpu.VMEM((planes, rows, levels), F32),
-            pltpu.VMEM((planes, rows, levels), F32),
-            pltpu.VMEM((planes, rows, levels), F32),
-            pltpu.VMEM((cells_x, cells_y, levels), F32),
-        ],
-        name="source_modes",
-    )(rim, basis_rows)
+    gap = -(cells_y + 2 * HALO) % 8
+    rows = cells_y + 2 * HALO + gap
+    up, down = ring("py")
+    stacked, leading, last = pack_winds(winds)
+    before = lax.ppermute(last, "py", up)
+    after = lax.ppermute(leading, "py", down)
+    none = jnp.zeros((3, HALO, gap, levels), BF16)
+
+    def edge(first):
+        own = stacked[:, first : first + HALO]
+        span = slice(first, first + HALO)
+        return jnp.concatenate([own, after[:, span], none, before[:, span]], axis=2)
+
+    up, down = ring("px")
+    low = lax.ppermute(edge(cells_x - HALO), "px", up)
+    high = lax.ppermute(edge(0), "px", down)
+    vmem = pl.BlockSpec(memory_space=pltpu.VMEM)
+    shapes = [pltpu.VMEM((3, planes, rows, levels), F32)] * 3
+    shapes += [pltpu.VMEM((planes, rows, levels), F32)]
+    shapes += [pltpu.VMEM((planes, cells_y, levels), F32)] * 2
+    state = pl.pallas_call(
+        inner_kernel,
+        out_shape=shapes,
+        in_specs=[vmem] * 3,
+        out_specs=[vmem] * 6,
+        cost_estimate=pl.CostEstimate(flops=40_000_000, bytes_accessed=6_000_000, transcendentals=0),
+        compiler_params=KERNEL_VMEM,
+        name="inner_planes",
+    )(on_chip(stacked), on_chip(before), on_chip(after))
+    results = pl.pallas_call(
+        outer_kernel,
+        out_shape=shapes + [pltpu.VMEM((levels, cells_x * cells_y), F32)],
+        in_specs=[vmem] * 9,
+        out_specs=[vmem] * 7,
+        input_output_aliases={3 + i: i for i in range(6)},
+        scratch_shapes=[pltpu.VMEM((cells_x, cells_y, levels), F32)],
+        compiler_params=KERNEL_VMEM,
+        name="outer_planes",
+    )(on_chip(low), on_chip(high), on_chip(table_parts(basis_rows * np.float32(0.0625), 1, FORWARD)), *[on_chip(part) for part in state])
+    return results[6]
 
 
 def block_transpose(values, width):
@@ -217,9 +329,9 @@
             for i, piece in enumerate(block_transpose(pieces, cells_y)):
                 row = (a * cells_x + g * north_count + i) * block
                 work[row : row + block, :] = piece
-    work[...] = high_dot(work[...], qy_ref[...], ((1,), (0,)))
+    work[...] = dot(value_parts(work[...], 1, FORWARD), qy_ref[...], ((1,), (0,)))
     planes = [work[pl.ds(i, total_x, stride=block), :] for i in range(block)]
-    waves = high_dot(qxt_ref[...], jnp.concatenate(planes, axis=1), ((1,), (0,)))
+    waves = dot(qxt_ref[...], value_parts(jnp.concatenate(planes, axis=1), 0, FORWARD), ((1,), (0,)))
     eigen = ex_ref[...] + ey_ref[0:1, :]
     first = rank_ref[0] * block
     solved = []
@@ -228,10 +340,10 @@
         empty = value == 0.0
         factor = jnp.where(empty, 0.0, -1.0 / jnp.where(empty, 1.0, value))
         solved.append(waves[:, i * total_y : (i + 1) * total_y] * factor)
-    back = high_dot(qx_ref[...], jnp.concatenate(solved, axis=1), ((1,), (0,)))
+    back = dot(qx_ref[...], value_parts(jnp.concatenate(solved, axis=1), 0, INVERSE), ((1,), (0,)))
     for i in range(block):
         work[pl.ds(i, total_x, stride=block), :] = back[:, i * total_y : (i + 1) * total_y]
-    work[...] = high_dot(work[...], qyt_ref[...], ((1,), (0,)))
+    work[...] = dot(value_parts(work[...], 1, INVERSE), qyt_ref[...], ((1,), (0,)))
     for a in range(east_count):
         for g in range(groups):
             lanes = slice(g * total_y, (g + 1) * total_y)
@@ -246,25 +358,31 @@
     total_y = north_count * cells_y
     qx, ex = fourier_basis(total_x)
     qy, ey = fourier_basis(total_y)
+    tables = [
+        table_parts(qx, 1, INVERSE),
+        table_parts(qx.T, 1, FORWARD),
+        table_parts(qy, 0, FORWARD),
+        table_parts(qy.T, 0, INVERSE),
+    ]
+    tables += [
+        np.ascontiguousarray(np.broadcast_to(ex[:, None], (total_x, total_y))),
+        np.ascontiguousarray(np.broadcast_to(ey[None, :], (8, total_y))),
+    ]
     vmem = pl.BlockSpec(memory_space=pltpu.VMEM)
     smem = pl.BlockSpec(memory_space=pltpu.SMEM)
     return pl.pallas_call(
         functools.partial(solve_kernel, east_count, north_count, cells_x, cells_y),
-        out_shape=jax.ShapeDtypeStruct(blocks.shape, F32),
+        out_shape=pltpu.VMEM(blocks.shape, F32),
         in_specs=[vmem] * 7 + [smem] * 2,
         out_specs=vmem,
         scratch_shapes=[pltpu.VMEM((total_x * blocks.shape[1], total_y), F32)],
+        compiler_params=KERNEL_VMEM,
         name="solve_planes",
-    )(
-        blocks, qx, np.ascontiguousarray(qx.T), qy, np.ascontiguousarray(qy.T),
-        np.ascontiguousarray(np.broadcast_to(ex[:, None], (total_x, total_y))),
-        np.ascontiguousarray(np.broadcast_to(ey[None, :], (8, total_y))),
-        mode_eigen(levels), rank,
-    )
+    )(on_chip(blocks), *[on_chip(table) for table in tables], mode_eigen(levels), rank)
 
 
 def pressure_kernel(modes_ref, basis_ref, out_ref):
-    out_ref[...] = high_dot(modes_ref[...], basis_ref[...], ((0,), (0,)))
+    out_ref[...] = dot(value_parts(modes_ref[...], 0, INVERSE), basis_ref[...], ((0,), (0,)))
 
 
 def pressure_cells(modes, basis_rows):
@@ -273,8 +391,9 @@
         out_shape=jax.ShapeDtypeStruct((modes.shape[1], basis_rows.shape[1]), F32),
         in_specs=[pl.BlockSpec(memory_space=pltpu.VMEM)] * 2,
         out_specs=pl.BlockSpec(memory_space=pltpu.VMEM),
+        compiler_params=KERNEL_VMEM,
         name="pressure_cells",
-    )(modes, basis_rows)
+    )(on_chip(modes), on_chip(table_parts(basis_rows, 0, INVERSE)))
 
 
 def rotation(row_count, col_count, length, direction):
@@ -582,8 +701,7 @@
     north_count = lax.axis_size("py")
     devices = east_count * north_count
     basis_rows = np.ascontiguousarray(cosine_basis(levels).T)
-    rim = with_halo(jnp.stack((wind_east, wind_north, wind_up)))
-    modes = source_modes(rim, basis_rows, cells_x, cells_y)
+    modes = source_modes((wind_east, wind_north, wind_up), basis_rows)
     if levels == 8 * devices and north_count * cells_y == 128 and cells_x % north_count == 0:
         blocks = modes.reshape(devices, levels // devices, cells_x * cells_y)
         blocks = lax.all_to_all(blocks, ("px", "py"), split_axis=0, concat_axis=0, tiled=True)

time: 62.9 us -> 51.1 us (0.81)
  waiting for transfers between devices: 19.2 us -> 15.4 us
  other arithmetic: 3.17 us -> 0.12 us
  Pallas kernels: 14.5 us -> 11.8 us
  blocking collectives: 13.8 us -> 12.8 us
    ppermute x4, waiting for transfers between devices: 8.62 us -> 4.82 us  [the longest x1 2.64 us: source_modes(): before = lax.ppermute(last, 'py', up)]
    slice x2 -> x0, other arithmetic: 2.03 us -> none  [the longest x1 1.13 us: with_halo(): leading = lax.slice_in_dim(stacked, 0, width, axis=dim)]
    pallas_call x1, Pallas kernels: 3.85 us -> 2.35 us  [solve_planes(): pl.pallas_call(functools.partial(solve_kernel, east_count, north_count, c...]
    pallas_call x1, Pallas kernels: 2.15 us -> 1.01 us  [pressure_cells(): pl.pallas_call(pressure_kernel, out_shape=jax.ShapeDtypeStruct((modes.sha...]
    all_to_all x1, blocking collectives: 13.8 us -> 12.8 us  [shards(): lax.all_to_all(blocks, ('px', 'py'), split_axis=0, concat_axis=0, tiled=T...]
    concatenate x1, other arithmetic: 1.14 us -> 0.12 us  [edge(): return jnp.concatenate([own, after[:, span], none, before[:, span]], axis=2)]
    unnamed x8 -> x18, local copies, waits for them, and re-layouts: 0.71 us -> 0.06 us
    pallas_call x1 -> x3, Pallas kernels: 8.48 us -> 8.43 us  [the longest x1 4.26 us: source_modes(): pl.pallas_call(inner_kernel, out_shape=shapes, in_specs=[vmem] * 3, out_s...]
  transfers between devices with their start and end apart: 5 -> 5, of which waited for: 5 -> 3; matrix products, arithmetic and copies ran while one was open for 0% -> 0% of each run, Pallas kernels for 0% -> 8%
where the time goes in v1:
time: 51.1 us; the launch traced here: 50.9 us
  waiting for transfers between devices  15.4 us (30%)
  blocking collectives  12.8 us (25%)
  Pallas kernels  11.8 us (23%)
  starting transfers between devices  10.5 us (21%)
    all_to_all x1, blocking collectives, shards(): lax.all_to_all(blocks, ('px', 'py'), split_axis=0, concat_axis=0, tiled=T...  12.8 us
    all_to_all x1, waiting for transfers between devices, shards(): lax.all_to_all(blocks, ('px', 'py'), split_axis=0, concat_axis=0, tiled=T...  10.6 us
    pallas_call x1, Pallas kernels, source_modes(): pl.pallas_call(inner_kernel, out_shape=shapes, in_specs=[vmem] * 3, out_s...  4.26 us
    ppermute x1, starting transfers between devices, source_modes(): after = lax.ppermute(leading, 'py', down)  3.41 us
    all_to_all x1, starting transfers between devices, shards(): lax.all_to_all(blocks, ('px', 'py'), split_axis=0, concat_axis=0, tiled=T...  3.19 us
    pallas_call x1, Pallas kernels, source_modes(): pl.pallas_call(outer_kernel, out_shape=shapes + [pltpu.VMEM((levels, cell...  2.87 us
    ppermute x1, waiting for transfers between devices, source_modes(): before = lax.ppermute(last, 'py', up)  2.64 us
    pallas_call x1, Pallas kernels, solve_planes(): pl.pallas_call(functools.partial(solve_kernel, east_count, north_count, c...  2.35 us
  transfers between devices with their start and end apart: 5, of which 3 were waited for; matrix products, arithmetic and copies ran while one was open for 0% of the time, Pallas kernels for 8%

profile of v1, /device:TPU:0, one launch (start us, length us, event | category | flops | bytes accessed | tf_op | source)
XLA Modules:
  0.0 50.9 jit_solution(10323102349578371887)
XLA Ops:
  0.0 1.3 %pack_winds.1 = (bf16[3,16,16,256]{3,2,1,0:T(8,128)(2,1)S(1)}, bf16[3,16,3,256]{3,2,1,0:T(4,128)(2,1)S(1)}, bf16[3,16,3,256]{3,2,1,0:T(4,128)(2,1)S(1)}) custom-call(bf16[16,16,256]{2,1,0:T(8,128)(2,1)} %east_ref.1, bf16[16,16,256]{2,1,0:T(8,128)(2,1)} %north_ref.1, bf16[16,16,256]{2,1,0:T(8,128)(2,1)} %up_ref.1), custom_call_target="tpu_custom_call" | custom-call | tf_op jit(solution)/shard_map/pack_winds/pallas_call | solution.py:244
  1.3 3.4 %collective-permute-start = (bf16[3,16,3,256]{3,2,1,0:T(4,128)(2,1)S(1)}, bf16[3,16,3,256]{3,2,1,0:T(4,128)(2,1)S(1)}, u32[]{:S(2)}, u32[]{:S(2)}) collective-permute-start(bf16[3,16,3,256]{3,2,1,0:T(4,128)(2,1)S(1)} %get-tuple-element.16), channel_id=1, source_target_pairs={{1,0},{2,1},{3,2},{4,3},{5,4},{6,5},{7,6},{0,7},{9,8},{10,9},{11,1... | collective-permute-start | bytes 221192 | tf_op jit(solution)/shard_map/ppermute | solution.py:262
  4.7 0.0 collective-permute-start.1
  4.7 0.1 pad.6.clone
  4.8 2.2 %collective-permute-done.after_ref = bf16[3,16,3,256]{3,2,1,0:T(4,128)(2,1)S(1)} collective-permute-done((bf16[3,16,3,256]{3,2,1,0:T(4,128)(2,1)S(1)}, bf16[3,16,3,256]{3,2,1,0:T(4,128)(2,1)S(1)}, u32[]{:S(2)}, u32[]{:S(2)}) %collective-permute-start) | collective-permute-done | bytes 73760 | tf_op jit(solution)/shard_map/ppermute | solution.py:262
  7.0 2.6 %collective-permute-done.1.before_ref = bf16[3,16,3,256]{3,2,1,0:T(4,128)(2,1)S(1)} collective-permute-done((bf16[3,16,3,256]{3,2,1,0:T(4,128)(2,1)S(1)}, bf16[3,16,3,256]{3,2,1,0:T(4,128)(2,1)S(1)}, u32[]{:S(2)}, u32[]{:S(2)}) %collective-permute-start.1) | collective-permute-done | bytes 73760 | tf_op jit(solution)/shard_map/ppermute | solution.py:261
  9.7 0.1 pad_maximum_fusion.1
  9.8 1.6 %collective-permute-start.2 = (bf16[3,3,24,256]{3,2,1,0:T(8,128)(2,1)S(1)}, bf16[3,3,24,256]{3,2,1,0:T(8,128)(2,1)S(1)}, u32[]{:S(2)}, u32[]{:S(2)}) collective-permute-start(bf16[3,3,24,256]{3,2,1,0:T(8,128)(2,1)S(1)} %get-tuple-element.32), channel_id=1, source_target_pairs={{0,8},{8,16},{16,24},{24,0},{1,9},{9,17},{17,25},{25,1},{2,10},{10... | collective-permute-start | bytes 331784 | tf_op jit(solution)/shard_map/ppermute | solution.py:271
  11.4 2.2 %collective-permute-start.3 = (bf16[3,3,24,256]{3,2,1,0:T(8,128)(2,1)S(1)}, bf16[3,3,24,256]{3,2,1,0:T(8,128)(2,1)S(1)}, u32[]{:S(2)}, u32[]{:S(2)}) collective-permute-start(bf16[3,3,24,256]{3,2,1,0:T(8,128)(2,1)S(1)} %get-tuple-element.31), channel_id=1, source_target_pairs={{8,0},{16,8},{24,16},{0,24},{9,1},{17,9},{25,17},{1,25},{10,2},{18... | collective-permute-start | bytes 331784 | tf_op jit(solution)/shard_map/ppermute | solution.py:272
  13.7 4.3 %inner_planes.1 = (f32[3,22,24,256]{3,2,1,0:T(8,128)S(1)}, f32[3,22,24,256]{3,2,1,0:T(8,128)S(1)}, f32[3,22,24,256]{3,2,1,0:T(8,128)S(1)}, f32[22,24,256]{2,1,0:...) custom-call(bf16[3,16,16,256]{3,2,1,0:T(8,128)(2,1)S(1)} %get-tuple-element.15.winds_ref, ...), custom_call_target="tpu_custom_call" | custom-call | flops 40000000 | bytes 6000000 | tf_op jit(solution)/shard_map/inner_planes/pallas_call | solution.py:277
  17.9 0.0 collective-permute-done.2.low_ref
  17.9 0.0 collective-permute-done.3.high_ref
  18.0 0.0 copy-done
  18.0 0.0 copy-start.2
  18.0 0.0 copy-start.3
  18.0 0.0 copy-start.4
  18.0 0.0 copy-start.5
  18.0 0.0 copy-start.6
  18.0 0.0 copy-start.7
  18.0 0.0 copy-start.8
  18.1 2.9 %outer_planes.1 = (f32[3,22,24,256]{3,2,1,0:T(8,128)S(1)}, f32[3,22,24,256]{3,2,1,0:T(8,128)S(1)}, f32[3,22,24,256]{3,2,1,0:T(8,128)S(1)}, f32[22,24,256]{2,1,0:...) custom-call(bf16[3,3,24,256]{3,2,1,0:T(8,128)(2,1)S(1)} %collective-, ...), custom_call_target="tpu_custom_call", output_to_operand_aliasing={{0}: (3, {}), {1}: (4, {}), {2}: (5, {}), {3}: (6, {}), {4}... | custom-call | tf_op jit(solution)/shard_map/outer_planes/pallas_call | solution.py:286
  20.9 3.2 %all-to-all-start = ((f32[32,8,256]{2,1,0:T(8,128)}), f32[32,8,256]{2,1,0:T(8,128)S(1)}, u32[]{:S(2)}, u32[]{:S(2)}) async-start(f32[32,8,256]{2,1,0:T(8,128)} %bitcast), calls=%async_computation | async-start | bytes 524288 | tf_op jit(solution)/shard_map/all_to_all | solution.py:707
  24.1 10.6 %all-to-all-done.in_ref = f32[32,8,256]{2,1,0:T(8,128)S(1)} async-done(((f32[32,8,256]{2,1,0:T(8,128)}), f32[32,8,256]{2,1,0:T(8,128)S(1)}, u32[]{:S(2)}, u32[]{:S(2)}) %all-to-all-start) | async-done | bytes 262176 | tf_op jit(solution)/shard_map/all_to_all | solution.py:707
  34.7 0.0 copy-done.2
  34.7 0.0 copy-done.3
  34.7 0.0 copy-done.5
  34.7 0.0 copy-done.6
  34.7 0.0 copy-done.7
  34.8 0.0 copy-done.8
  34.8 2.3 %solve_planes.1 = f32[32,8,256]{2,1,0:T(8,128)S(1)} custom-call(f32[32,8,256]{2,1,0:T(8,128)S(1)} %all-to-all-done.in_ref, bf16[64,192]{1,0:T(8,128)(2,1)S(1)} %copy-done.5, bf16[64,384]{1,0:T(8,128)(2,1)S(1)} %copy-done.4, bf16[768,128]{1,0:T(8,128)(2,1)S(1)} %copy-done.2, bf16[384,128]{1,0:T(8,128)(2,1)S(1)} %copy-done.3, f32[64,128]{1,0:T(8,128)S(1)} %copy-done.6, ...), custom_call_target="tpu_custom_call" | custom-call | tf_op jit(solution)/shard_map/solve_planes/pallas_call | solution.py:373
  37.1 12.8 %all_to_all.10 = f32[32,8,256]{2,1,0:T(8,128)S(1)} all-to-all(f32[32,8,256]{2,1,0:T(8,128)S(1)} %solve_planes.1), channel_id=1, replica_groups=mesh['px'=4,'py'=8] {'px','py'}, dimensions={0} | all-to-all | bytes 524288 | tf_op jit(solution)/shard_map/all_to_all | solution.py:710
  49.9 1.0 %pressure_cells.1 = f32[256,256]{1,0:T(8,128)} custom-call(f32[256,256]{1,0:T(8,128)S(1)} %bitcast.4, bf16[768,256]{1,0:T(8,128)(2,1)S(1)} %copy-done.1), custom_call_target="tpu_custom_call" | custom-call | tf_op jit(solution)/shard_map/pressure_cells/pallas_call | solution.py:389
  (8 shorter events, 0.1 us)
Async XLA Ops:
  0.0 18.0 %copy-start = (bf16[256,1536]{1,0:T(8,128)(2,1)S(1)}, bf16[256,1536]{1,0:T(8,128)(2,1)}, u32[]{:S(2)}) copy-start(bf16[256,1536]{1,0:T(8,128)(2,1)} %constant.30.clone.basis_ref) | copy-start | bytes 2359300
  1.3 5.7 %collective-permute-start = (bf16[3,16,3,256]{3,2,1,0:T(4,128)(2,1)S(1)}, bf16[3,16,3,256]{3,2,1,0:T(4,128)(2,1)S(1)}, u32[]{:S(2)}, u32[]{:S(2)}) collective-permute-start(bf16[3,16,3,256]{3,2,1,0:T(4,128)(2,1)S(1)} %get-tuple-element.16), channel_id=1, source_target_pairs={{1,0},{2,1},{3,2},{4,3},{5,4},{6,5},{7,6},{0,7},{9,8},{10,9},{11,1... | collective-permute-start | bytes 221192 | tf_op jit(solution)/shard_map/ppermute | solution.py:262
  4.7 4.9 %collective-permute-start.1 = (bf16[3,16,3,256]{3,2,1,0:T(4,128)(2,1)S(1)}, bf16[3,16,3,256]{3,2,1,0:T(4,128)(2,1)S(1)}, u32[]{:S(2)}, u32[]{:S(2)}) collective-permute-start(bf16[3,16,3,256]{3,2,1,0:T(4,128)(2,1)S(1)} %get-tuple-element.17), channel_id=1, source_target_pairs={{0,1},{1,2},{2,3},{3,4},{4,5},{5,6},{6,7},{7,0},{8,9},{9,10},{10,1... | collective-permute-start | bytes 221192 | tf_op jit(solution)/shard_map/ppermute | solution.py:261
  9.8 8.1 %collective-permute-start.2 = (bf16[3,3,24,256]{3,2,1,0:T(8,128)(2,1)S(1)}, bf16[3,3,24,256]{3,2,1,0:T(8,128)(2,1)S(1)}, u32[]{:S(2)}, u32[]{:S(2)}) collective-permute-start(bf16[3,3,24,256]{3,2,1,0:T(8,128)(2,1)S(1)} %get-tuple-element.32), channel_id=1, source_target_pairs={{0,8},{8,16},{16,24},{24,0},{1,9},{9,17},{17,25},{25,1},{2,10},{10... | collective-permute-start | bytes 331784 | tf_op jit(solution)/shard_map/ppermute | solution.py:271
  11.4 6.5 %collective-permute-start.3 = (bf16[3,3,24,256]{3,2,1,0:T(8,128)(2,1)S(1)}, bf16[3,3,24,256]{3,2,1,0:T(8,128)(2,1)S(1)}, u32[]{:S(2)}, u32[]{:S(2)}) collective-permute-start(bf16[3,3,24,256]{3,2,1,0:T(8,128)(2,1)S(1)} %get-tuple-element.31), channel_id=1, source_target_pairs={{8,0},{16,8},{24,16},{0,24},{9,1},{17,9},{25,17},{1,25},{10,2},{18... | collective-permute-start | bytes 331784 | tf_op jit(solution)/shard_map/ppermute | solution.py:272
  18.0 16.7 %copy-start.2 = (bf16[768,128]{1,0:T(8,128)(2,1)S(1)}, bf16[768,128]{1,0:T(8,128)(2,1)}, u32[]{:S(2)}) copy-start(bf16[768,128]{1,0:T(8,128)(2,1)} %constant.33.clone.qy_ref) | copy-start | bytes 589828
  18.0 16.7 %copy-start.3 = (bf16[384,128]{1,0:T(8,128)(2,1)S(1)}, bf16[384,128]{1,0:T(8,128)(2,1)}, u32[]{:S(2)}) copy-start(bf16[384,128]{1,0:T(8,128)(2,1)} %constant.34.clone.qyt_ref) | copy-start | bytes 294916
  18.0 16.7 %copy-start.4 = (bf16[64,384]{1,0:T(8,128)(2,1)S(1)}, bf16[64,384]{1,0:T(8,128)(2,1)}, u32[]{:S(2)}) copy-start(bf16[64,384]{1,0:T(8,128)(2,1)} %constant.32.clone.qxt_ref) | copy-start | bytes 147460
  18.0 16.7 %copy-start.5 = (bf16[64,192]{1,0:T(8,128)(2,1)S(1)}, bf16[64,192]{1,0:T(8,128)(2,1)}, u32[]{:S(2)}) copy-start(bf16[64,192]{1,0:T(8,128)(2,1)} %constant.31.clone.qx_ref) | copy-start | bytes 73732
  18.0 16.7 %copy-start.6 = (f32[64,128]{1,0:T(8,128)S(1)}, f32[64,128]{1,0:T(8,128)}, u32[]{:S(2)}) copy-start(f32[64,128]{1,0:T(8,128)} %constant.35.clone.ex_ref) | copy-start | bytes 98308
  18.0 16.7 %copy-start.7 = (f32[8,128]{1,0:T(8,128)S(1)}, f32[8,128]{1,0:T(8,128)}, u32[]{:S(2)}) copy-start(f32[8,128]{1,0:T(8,128)} %constant.36.clone.ey_ref) | copy-start | bytes 12292
  18.0 16.7 %copy-start.8 = (f32[256]{0:T(256)S(1)}, f32[256]{0:T(256)}, u32[]{:S(2)}) copy-start(f32[256]{0:T(256)} %constant.37.clone.em_ref) | copy-start | bytes 3076
  20.9 29.0 %copy-start.1 = (bf16[768,256]{1,0:T(8,128)(2,1)S(1)}, bf16[768,256]{1,0:T(8,128)(2,1)}, u32[]{:S(2)}) copy-start(bf16[768,256]{1,0:T(8,128)(2,1)} %constant.38.clone.basis_ref) | copy-start | bytes 1179652
  20.9 13.8 %all-to-all-start = ((f32[32,8,256]{2,1,0:T(8,128)}), f32[32,8,256]{2,1,0:T(8,128)S(1)}, u32[]{:S(2)}, u32[]{:S(2)}) async-start(f32[32,8,256]{2,1,0:T(8,128)} %bitcast), calls=%async_computation | async-start | bytes 524288 | tf_op jit(solution)/shard_map/all_to_all | solution.py:707

commit v2 on v1

--- a/solution.py
+++ b/solution.py
@@ -15,10 +15,13 @@
 STRAIN_FLOOR = 1.0
 TIME_STEP = 0.25
 HALO = 3
+ROWS = 4
 LANES = 128
 F32 = jnp.float32
 BF16 = jnp.bfloat16
-FORWARD = 3
+DCT_PARTS = 3
+NORTH_PARTS = 3
+EAST_PARTS = 3
 INVERSE = 2
 KERNEL_VMEM = pltpu.CompilerParams(vmem_limit_bytes=24 * 2**20)
 
@@ -77,6 +80,13 @@
 
 def on_chip(values):
     return pltpu.with_memory_space_constraint(values, pltpu.VMEM)
+
+
+def swaps(axis):
+    size = lax.axis_size(axis)
+    inner = [(i, i ^ 1) for i in range(size)]
+    outer = [(i, (i - 1 if i % 2 == 0 else i + 1) % size) for i in range(size)]
+    return inner, outer
 
 
 def ring(axis):
@@ -174,125 +184,168 @@
     below[c, x] = z_prev(plane, none)
 
 
-def each(first, last, body, jump=0, skip=0):
+def by_parity(odd, body):
+    pl.when(odd == 1)(lambda: body(True))
+    pl.when(odd == 0)(lambda: body(False))
+
+
+def each(first, last, body, jump=0, skip=0, unroll=1):
     def step(i, carry):
         body(i + jnp.where(i >= first + jump, skip, 0) if skip else i)
         return carry
 
-    lax.fori_loop(first, last, step, 0)
-
-
-def inner_kernel(winds_ref, before_ref, after_ref, wind, above, below, visc, east, part):
+    lax.fori_loop(first, last, step, 0, unroll=unroll)
+
+
+def inner_kernel(odd_ref, winds_ref, near_ref, far_ref, wind, above, below, visc, east, part):
     cells_x, cells_y, levels = winds_ref.shape[1:]
-    rows = wind.shape[2]
-    gap = jnp.zeros((rows - cells_y - 2 * HALO, levels), F32)
-
-    def load(x):
-        for c in range(3):
-            pieces = [winds_ref[c, x], after_ref[c, x], before_ref[c, x]]
-            own, after, before = [piece.astype(F32) for piece in pieces]
-            plane = jnp.concatenate([own, after, gap, before], axis=0)
-            store_plane(c, x + HALO, plane, wind, above, below)
-
-    each(0, cells_x, load)
+
+    def load(odd):
+        after_ref, before_ref = (far_ref, near_ref) if odd else (near_ref, far_ref)
+
+        def plane(x):
+            for c in range(3):
+                pieces = [winds_ref[c, x], after_ref[c, x], before_ref[c, x]]
+                own, after, before = [piece.astype(F32) for piece in pieces]
+                whole = jnp.concatenate([own, after, before], axis=0)
+                store_plane(c, x + HALO, whole, wind, above, below)
+
+        each(0, cells_x, plane, unroll=4)
+
+    by_parity(odd_ref[0], load)
     first, last = HALO, HALO + cells_x
-    each(first + 1, last - 1, lambda x: visc_plane(x, wind, above, below, visc))
-    each(first + 2, last - 2, lambda x: wind_plane(x, wind, above, below, visc, east, part))
-
-
-def outer_kernel(low_ref, high_ref, basis_ref, *refs):
+    each(first + 1, last - 1, lambda x: visc_plane(x, wind, above, below, visc), unroll=2)
+    each(first + 2, last - 2, lambda x: wind_plane(x, wind, above, below, visc, east, part), unroll=2)
+
+
+def outer_kernel(low_ref, high_ref, low_corner_ref, high_corner_ref, basis_ref, *refs):
     wind, above, below, visc, east, part = refs[6:12]
     out_ref, source = refs[12:]
     cells_x, cells_y, levels = source.shape
     skip = cells_x
 
-    def load(x):
-        for c in range(3):
-            for ref, start in ((low_ref, 0), (high_ref, HALO + cells_x)):
-                store_plane(c, x + start, ref[c, x].astype(F32), wind, above, below)
-
-    each(0, HALO, load)
-    each(1, 7, lambda x: visc_plane(x, wind, above, below, visc), 3, skip - 2)
-    each(2, 8, lambda x: wind_plane(x, wind, above, below, visc, east, part), 3, skip - 4)
+
+    row = lax.broadcasted_iota(jnp.int32, (8, levels), 0)
+
+    def load(c):
+        for side, ref, corner_ref in ((0, low_ref, low_corner_ref), (1, high_ref, high_corner_ref)):
+            nearest = corner_ref[c].astype(F32)
+            second = jnp.where(row < 4, pltpu.roll(nearest, 6, 0), pltpu.roll(nearest, 2, 0))
+            for i, rest in enumerate((nearest, second, jnp.zeros_like(nearest))):
+                index = i if side else HALO - 1 - i
+                plane = jnp.concatenate([ref[c, index].astype(F32), rest], axis=0)
+                start = HALO + cells_x if side else 0
+                store_plane(c, start + index, plane, wind, above, below)
+
+    each(0, 3, load)
+    each(1, 7, lambda x: visc_plane(x, wind, above, below, visc), 3, skip - 2, unroll=2)
+    each(2, 8, lambda x: wind_plane(x, wind, above, below, visc, east, part), 3, skip - 4, unroll=2)
 
     def collect(x):
         source[x] = part[x + HALO] + (east[x + HALO + 1] - east[x + HALO - 1])
 
-    each(0, cells_x, collect)
+    each(0, cells_x, collect, unroll=4)
     flat = source[...].reshape(cells_x * cells_y, levels)
-    out_ref[...] = dot(basis_ref[...], value_parts(flat, 1, FORWARD), ((1,), (1,)))
-
-
-def pack_kernel(east_ref, north_ref, up_ref, winds_ref, leading_ref, last_ref):
-    cells_x, cells_y, levels = east_ref.shape
-
-    def plane(x):
-        for c, ref in enumerate((east_ref, north_ref, up_ref)):
-            own = ref[x]
-            winds_ref[c, x] = own
-            wide = own.astype(F32)
-            leading_ref[c, x] = wide[:HALO].astype(BF16)
-            last_ref[c, x] = wide[cells_y - HALO :].astype(BF16)
-
-    each(0, cells_x, plane)
-
-
-def pack_winds(winds):
+    out_ref[...] = dot(basis_ref[...], value_parts(flat, 1, DCT_PARTS), ((1,), (1,)))
+
+
+def pack_kernel(odd_ref, *refs):
+    winds = refs[:3]
+    winds_ref, inner_ref, outer_ref, down_ref, up_ref, sems = refs[3:]
+    cells_x, cells_y, levels = winds[0].shape
+
+    def pack(odd):
+        leading_ref, last_ref = (inner_ref, outer_ref) if odd else (outer_ref, inner_ref)
+        copies = []
+        for c, ref in enumerate(winds):
+            pairs = (
+                (ref.at[:, pl.ds(0, ROWS)], leading_ref.at[c]),
+                (ref.at[:, pl.ds(cells_y - ROWS, ROWS)], last_ref.at[c]),
+                (ref.at[pl.ds(0, HALO)], down_ref.at[c]),
+                (ref.at[pl.ds(cells_x - HALO, HALO)], up_ref.at[c]),
+                (ref, winds_ref.at[c]),
+            )
+            for i, (source, target) in enumerate(pairs):
+                copies.append(pltpu.make_async_copy(source, target, sems.at[5 * c + i]))
+        for copy in copies:
+            copy.start()
+        for copy in copies:
+            copy.wait()
+
+    by_parity(odd_ref[0], pack)
+
+
+def pack_winds(winds, odd):
     cells_x, cells_y, levels = winds[0].shape
     vmem = pl.BlockSpec(memory_space=pltpu.VMEM)
-    edge = pltpu.VMEM((3, cells_x, HALO, levels), BF16)
+    edge = pltpu.VMEM((3, cells_x, ROWS, levels), BF16)
+    side = pltpu.VMEM((3, HALO, cells_y, levels), BF16)
     return pl.pallas_call(
         pack_kernel,
-        out_shape=[pltpu.VMEM((3, cells_x, cells_y, levels), BF16), edge, edge],
-        in_specs=[vmem] * 3,
-        out_specs=[vmem] * 3,
+        out_shape=[pltpu.VMEM((3, cells_x, cells_y, levels), BF16), edge, edge, side, side],
+        in_specs=[pl.BlockSpec(memory_space=pltpu.SMEM)] + [pl.BlockSpec(memory_space=pl.ANY)] * 3,
+        out_specs=[vmem] * 5,
+        scratch_shapes=[pltpu.SemaphoreType.DMA((15,))],
         compiler_params=KERNEL_VMEM,
         name="pack_winds",
-    )(*[pltpu.with_memory_space_constraint(wind, pltpu.HBM) for wind in winds])
+    )(odd, *[pltpu.with_memory_space_constraint(wind, pltpu.HBM) for wind in winds])
 
 
 def source_modes(winds, basis_rows):
     cells_x, cells_y, levels = winds[0].shape
     planes = cells_x + 2 * HALO
-    gap = -(cells_y + 2 * HALO) % 8
-    rows = cells_y + 2 * HALO + gap
-    up, down = ring("py")
-    stacked, leading, last = pack_winds(winds)
-    before = lax.ppermute(last, "py", up)
-    after = lax.ppermute(leading, "py", down)
-    none = jnp.zeros((3, HALO, gap, levels), BF16)
-
-    def edge(first):
-        own = stacked[:, first : first + HALO]
-        span = slice(first, first + HALO)
-        return jnp.concatenate([own, after[:, span], none, before[:, span]], axis=2)
-
+    rows = cells_y + 2 * ROWS
+    odd_north = lax.axis_index("py") % 2
+    odd = odd_north.reshape(1)
+    stacked, inner_rows, outer_rows, leading, last = pack_winds(winds, odd)
+    inner, outer = swaps("py")
     up, down = ring("px")
-    low = lax.ppermute(edge(cells_x - HALO), "px", up)
-    high = lax.ppermute(edge(0), "px", down)
+    outer_got = lax.ppermute(outer_rows, "py", outer)
+    inner_got = lax.ppermute(inner_rows, "py", inner)
+    low = lax.ppermute(last, "px", up)
+    high = lax.ppermute(leading, "px", down)
+
+    def corner(first, second):
+        near, far = [[v[:, x] for x in (first, second)] for v in (inner_got, outer_got)]
+        after = [jnp.where(odd_north == 1, f, n) for n, f in zip(near, far)]
+        before = [jnp.where(odd_north == 1, n, f) for n, f in zip(near, far)]
+        none = jnp.zeros((3, 2, levels), BF16)
+        pieces = [after[0][:, :2], after[1][:, :1], none, before[1][:, 3:], before[0][:, 2:]]
+        return jnp.concatenate(pieces, axis=1)
+
+    low_corner = lax.ppermute(corner(cells_x - 1, cells_x - 2), "px", up)
+    high_corner = lax.ppermute(corner(0, 1), "px", down)
     vmem = pl.BlockSpec(memory_space=pltpu.VMEM)
+    smem = pl.BlockSpec(memory_space=pltpu.SMEM)
     shapes = [pltpu.VMEM((3, planes, rows, levels), F32)] * 3
     shapes += [pltpu.VMEM((planes, rows, levels), F32)]
     shapes += [pltpu.VMEM((planes, cells_y, levels), F32)] * 2
     state = pl.pallas_call(
         inner_kernel,
         out_shape=shapes,
-        in_specs=[vmem] * 3,
+        in_specs=[smem] + [vmem] * 3,
         out_specs=[vmem] * 6,
         cost_estimate=pl.CostEstimate(flops=40_000_000, bytes_accessed=6_000_000, transcendentals=0),
         compiler_params=KERNEL_VMEM,
         name="inner_planes",
-    )(on_chip(stacked), on_chip(before), on_chip(after))
+    )(odd, on_chip(stacked), on_chip(inner_got), on_chip(outer_got))
     results = pl.pallas_call(
         outer_kernel,
         out_shape=shapes + [pltpu.VMEM((levels, cells_x * cells_y), F32)],
-        in_specs=[vmem] * 9,
+        in_specs=[vmem] * 11,
         out_specs=[vmem] * 7,
-        input_output_aliases={3 + i: i for i in range(6)},
+        input_output_aliases={5 + i: i for i in range(6)},
         scratch_shapes=[pltpu.VMEM((cells_x, cells_y, levels), F32)],
         compiler_params=KERNEL_VMEM,
         name="outer_planes",
-    )(on_chip(low), on_chip(high), on_chip(table_parts(basis_rows * np.float32(0.0625), 1, FORWARD)), *[on_chip(part) for part in state])
+    )(
+        on_chip(low),
+        on_chip(high),
+        on_chip(low_corner),
+        on_chip(high_corner),
+        on_chip(table_parts(basis_rows * np.float32(0.0625), 1, DCT_PARTS)),
+        *[on_chip(part) for part in state],
+    )
     return results[6]
 
 
@@ -329,9 +382,9 @@
             for i, piece in enumerate(block_transpose(pieces, cells_y)):
                 row = (a * cells_x + g * north_count + i) * block
                 work[row : row + block, :] = piece
-    work[...] = dot(value_parts(work[...], 1, FORWARD), qy_ref[...], ((1,), (0,)))
+    work[...] = dot(value_parts(work[...], 1, NORTH_PARTS), qy_ref[...], ((1,), (0,)))
     planes = [work[pl.ds(i, total_x, stride=block), :] for i in range(block)]
-    waves = dot(qxt_ref[...], value_parts(jnp.concatenate(planes, axis=1), 0, FORWARD), ((1,), (0,)))
+    waves = dot(qxt_ref[...], value_parts(jnp.concatenate(planes, axis=1), 0, EAST_PARTS), ((1,), (0,)))
     eigen = ex_ref[...] + ey_ref[0:1, :]
     first = rank_ref[0] * block
     solved = []
@@ -360,8 +413,8 @@
     qy, ey = fourier_basis(total_y)
     tables = [
         table_parts(qx, 1, INVERSE),
-        table_parts(qx.T, 1, FORWARD),
-        table_parts(qy, 0, FORWARD),
+        table_parts(qx.T, 1, EAST_PARTS),
+        table_parts(qy, 0, NORTH_PARTS),
         table_parts(qy.T, 0, INVERSE),
     ]
     tables += [

time: 51.1 us -> 49.1 us (0.961)
  starting transfers between devices: 10.5 us -> 15.3 us
  waiting for transfers between devices: 15.4 us -> 10.6 us
  Pallas kernels: 11.8 us -> 9.57 us
    ppermute x4 -> x6, waiting for transfers between devices: 4.82 us -> 0.02 us  [the longest x1 0.01 us: source_modes(): inner_got = lax.ppermute(inner_rows, 'py', inner)]
    ppermute x4 -> x6, starting transfers between devices: 7.29 us -> 11.9 us  [the longest x1 3.61 us: source_modes(): outer_got = lax.ppermute(outer_rows, 'py', outer)]
    pallas_call x1, Pallas kernels: 4.26 us -> 2.44 us  [source_modes(): pl.pallas_call(inner_kernel, out_shape=shapes, in_specs=[smem] + [vmem] *...]
  transfers between devices with their start and end apart: 5 -> 7, of which waited for: 3 -> 1; matrix products, arithmetic and copies ran while one was open for 0% -> 1% of each run, Pallas kernels for 8% -> 5%
where the time goes in v2:
time: 49.1 us; the launch traced here: 48.8 us
  starting transfers between devices  15.3 us (31%)
  blocking collectives  12.8 us (26%)
  waiting for transfers between devices  10.6 us (22%)
  Pallas kernels  9.57 us (19%)
    all_to_all x1, blocking collectives, shards(): lax.all_to_all(blocks, ('px', 'py'), split_axis=0, concat_axis=0, tiled=T...  12.8 us
    all_to_all x1, waiting for transfers between devices, shards(): lax.all_to_all(blocks, ('px', 'py'), split_axis=0, concat_axis=0, tiled=T...  10.6 us
    ppermute x1, starting transfers between devices, source_modes(): outer_got = lax.ppermute(outer_rows, 'py', outer)  3.61 us
    ppermute x1, starting transfers between devices, source_modes(): high_corner = lax.ppermute(corner(0, 1), 'px', down)  3.41 us
    all_to_all x1, starting transfers between devices, shards(): lax.all_to_all(blocks, ('px', 'py'), split_axis=0, concat_axis=0, tiled=T...  3.34 us
    pallas_call x1, Pallas kernels, source_modes(): pl.pallas_call(inner_kernel, out_shape=shapes, in_specs=[smem] + [vmem] *...  2.44 us
    pallas_call x1, Pallas kernels, source_modes(): pl.pallas_call(outer_kernel, out_shape=shapes + [pltpu.VMEM((levels, cell...  2.38 us
    pallas_call x1, Pallas kernels, solve_planes(): pl.pallas_call(functools.partial(solve_kernel, east_count, north_count, c...  2.35 us
  transfers between devices with their start and end apart: 7, of which 1 were waited for; matrix products, arithmetic and copies ran while one was open for 1% of the time, Pallas kernels for 5%

profile of v2, /device:TPU:0, one launch (start us, length us, event | category | flops | bytes accessed | tf_op | source)
XLA Modules:
  0.0 48.8 jit_solution(14915550637444242520)
XLA Ops:
  0.0 1.4 %pack_winds.1 = (bf16[3,16,16,256]{3,2,1,0:T(8,128)(2,1)S(1)}, bf16[3,16,4,256]{3,2,1,0:T(4,128)(2,1)S(1)}, bf16[3,16,4,256]{3,2,1,0:T(4,128)(2,1)S(1)}, bf16[3,...) custom-call(s32[1]{0:T(128)} %bitcast.odd_ref, bf16[16,16,256]{2,1,0:T(8,128)(2,1)} %refs_0_.1, ...), custom_call_target="tpu_custom_call" | custom-call | tf_op jit(solution)/shard_map/pack_winds/pallas_call | solution.py:283
  1.5 0.6 %collective-permute-start.3 = (bf16[3,16,4,256]{3,2,0,1:T(4,128)(2,1)S(1)}, bf16[3,16,4,256]{3,2,0,1:T(4,128)(2,1)S(1)}, u32[]{:S(2)}, u32[]{:S(2)}) collective-permute-start(bf16[3,16,4,256]{3,2,0,1:T(4,128)(2,1)S(1)} %copy.20), channel_id=1, source_target_pairs={{0,1},{1,0},{2,3},{3,2},{4,5},{5,4},{6,7},{7,6},{8,9},{9,8},{10,11... | collective-permute-start | bytes 294920 | tf_op jit(solution)/shard_map/ppermute | solution.py:304
  2.0 3.6 %collective-permute-start.2 = (bf16[3,16,4,256]{3,2,0,1:T(4,128)(2,1)S(1)}, bf16[3,16,4,256]{3,2,0,1:T(4,128)(2,1)S(1)}, u32[]{:S(2)}, u32[]{:S(2)}) collective-permute-start(bf16[3,16,4,256]{3,2,0,1:T(4,128)(2,1)S(1)} %copy.19), channel_id=1, source_target_pairs={{0,7},{1,2},{2,1},{3,4},{4,3},{5,6},{6,5},{7,0},{8,15},{9,10},{10,... | collective-permute-start | bytes 294920 | tf_op jit(solution)/shard_map/ppermute | solution.py:303
  5.7 1.6 %collective-permute-start = (bf16[3,3,16,256]{3,2,1,0:T(8,128)(2,1)S(1)}, bf16[3,3,16,256]{3,2,1,0:T(8,128)(2,1)S(1)}, u32[]{:S(2)}, u32[]{:S(2)}) collective-permute-start(bf16[3,3,16,256]{3,2,1,0:T(8,128)(2,1)S(1)} %get-tuple-element.17), channel_id=1, source_target_pairs={{0,8},{8,16},{16,24},{24,0},{1,9},{9,17},{17,25},{25,1},{2,10},{10... | collective-permute-start | bytes 221192 | tf_op jit(solution)/shard_map/ppermute | solution.py:305
  7.2 2.2 %collective-permute-start.1 = (bf16[3,3,16,256]{3,2,1,0:T(8,128)(2,1)S(1)}, bf16[3,3,16,256]{3,2,1,0:T(8,128)(2,1)S(1)}, u32[]{:S(2)}, u32[]{:S(2)}) collective-permute-start(bf16[3,3,16,256]{3,2,1,0:T(8,128)(2,1)S(1)} %get-tuple-element.18), channel_id=1, source_target_pairs={{8,0},{16,8},{24,16},{0,24},{9,1},{17,9},{25,17},{1,25},{10,2},{18... | collective-permute-start | bytes 221192 | tf_op jit(solution)/shard_map/ppermute | solution.py:306
  9.5 0.0 collective-permute-done.3
  9.5 0.0 collective-permute-done.2
  9.7 0.5 %collective-permute-start.4 = (bf16[3,8,256]{2,1,0:T(8,128)(2,1)S(1)}, bf16[3,8,256]{2,1,0:T(8,128)(2,1)S(1)}, u32[]{:S(2)}, u32[]{:S(2)}) collective-permute-start(bf16[3,8,256]{2,1,0:T(8,128)(2,1)S(1)} %concatenate.6), channel_id=1, source_target_pairs={{0,8},{8,16},{16,24},{24,0},{1,9},{9,17},{17,25},{25,1},{2,10},{10... | collective-permute-start | bytes 36872 | tf_op jit(solution)/shard_map/ppermute | solution.py:316
  10.2 3.4 %collective-permute-start.5 = (bf16[3,8,256]{2,1,0:T(8,128)(2,1)S(1)}, bf16[3,8,256]{2,1,0:T(8,128)(2,1)S(1)}, u32[]{:S(2)}, u32[]{:S(2)}) collective-permute-start(bf16[3,8,256]{2,1,0:T(8,128)(2,1)S(1)} %concatenate.7), channel_id=1, source_target_pairs={{8,0},{16,8},{24,16},{0,24},{9,1},{17,9},{25,17},{1,25},{10,2},{18... | collective-permute-start | bytes 36872 | tf_op jit(solution)/shard_map/ppermute | solution.py:317
  13.7 2.4 %inner_planes.1 = (f32[3,22,24,256]{3,2,1,0:T(8,128)S(1)}, f32[3,22,24,256]{3,2,1,0:T(8,128)S(1)}, f32[3,22,24,256]{3,2,1,0:T(8,128)S(1)}, f32[22,24,256]{2,1,0:...) custom-call(s32[1]{0:T(128)} %bitcast.odd_ref, ...), custom_call_target="tpu_custom_call" | custom-call | flops 40000000 | bytes 6000000 | tf_op jit(solution)/shard_map/inner_planes/pallas_call | solution.py:323
  16.2 0.0 collective-permute-done.low_ref
  16.2 0.0 collective-permute-done.1.high_ref
  16.2 0.0 collective-permute-done.4.low_corner_ref
  16.2 0.0 collective-permute-done.5.high_corner_ref
  16.2 0.0 copy-done
  16.2 0.0 copy-start.2
  16.2 0.0 copy-start.3
  16.3 0.0 copy-start.4
  16.3 0.0 copy-start.5
  16.3 0.0 copy-start.6
  16.3 0.0 copy-start.7
  16.3 0.0 copy-start.8
  16.3 2.4 %outer_planes.1 = (f32[3,22,24,256]{3,2,1,0:T(8,128)S(1)}, f32[3,22,24,256]{3,2,1,0:T(8,128)S(1)}, f32[3,22,24,256]{3,2,1,0:T(8,128)S(1)}, f32[22,24,256]{2,1,0:...) custom-call(bf16[3,3,16,256]{3,2,1,0:T(8,128)(2,1)S(1)} %collective-, ...), custom_call_target="tpu_custom_call", output_to_operand_aliasing={{0}: (5, {}), {1}: (6, {}), {2}: (7, {}), {3}: (8, {}), {4}... | custom-call | tf_op jit(solution)/shard_map/outer_planes/pallas_call | solution.py:332
  18.7 3.3 %all-to-all-start = ((f32[32,8,256]{2,1,0:T(8,128)}), f32[32,8,256]{2,1,0:T(8,128)S(1)}, u32[]{:S(2)}, u32[]{:S(2)}) async-start(f32[32,8,256]{2,1,0:T(8,128)} %bitcast.9), calls=%async_computation | async-start | bytes 524288 | tf_op jit(solution)/shard_map/all_to_all | solution.py:760
  22.1 10.6 %all-to-all-done.in_ref = f32[32,8,256]{2,1,0:T(8,128)S(1)} async-done(((f32[32,8,256]{2,1,0:T(8,128)}), f32[32,8,256]{2,1,0:T(8,128)S(1)}, u32[]{:S(2)}, u32[]{:S(2)}) %all-to-all-start) | async-done | bytes 262176 | tf_op jit(solution)/shard_map/all_to_all | solution.py:760
  32.6 0.0 copy-done.2
  32.6 0.0 copy-done.3
  32.6 0.0 copy-done.4
  32.6 0.0 copy-done.5
  32.7 2.3 %solve_planes.1 = f32[32,8,256]{2,1,0:T(8,128)S(1)} custom-call(f32[32,8,256]{2,1,0:T(8,128)S(1)} %all-to-all-done.in_ref, bf16[64,192]{1,0:T(8,128)(2,1)S(1)} %copy-done.6, bf16[64,384]{1,0:T(8,128)(2,1)S(1)} %copy-done.4, bf16[768,128]{1,0:T(8,128)(2,1)S(1)} %copy-done.2, bf16[384,128]{1,0:T(8,128)(2,1)S(1)} %copy-done.3, f32[64,128]{1,0:T(8,128)S(1)} %copy-done.5, ...), custom_call_target="tpu_custom_call" | custom-call | tf_op jit(solution)/shard_map/solve_planes/pallas_call | solution.py:426
  35.0 12.8 %all_to_all.10 = f32[32,8,256]{2,1,0:T(8,128)S(1)} all-to-all(f32[32,8,256]{2,1,0:T(8,128)S(1)} %solve_planes.1), channel_id=1, replica_groups=mesh['px'=4,'py'=8] {'px','py'}, dimensions={0} | all-to-all | bytes 524288 | tf_op jit(solution)/shard_map/all_to_all | solution.py:763
  47.8 1.0 %pressure_cells.1 = f32[256,256]{1,0:T(8,128)} custom-call(f32[256,256]{1,0:T(8,128)S(1)} %bitcast.21, bf16[768,256]{1,0:T(8,128)(2,1)S(1)} %copy-done.1), custom_call_target="tpu_custom_call" | custom-call | tf_op jit(solution)/shard_map/pressure_cells/pallas_call | solution.py:442
  (22 shorter events, 0.3 us)
Async XLA Ops:
  0.0 16.2 %copy-start = (bf16[256,1536]{1,0:T(8,128)(2,1)S(1)}, bf16[256,1536]{1,0:T(8,128)(2,1)}, u32[]{:S(2)}) copy-start(bf16[256,1536]{1,0:T(8,128)(2,1)} %constant.44.clone.basis_ref) | copy-start | bytes 2359300
  1.5 8.0 %collective-permute-start.3 = (bf16[3,16,4,256]{3,2,0,1:T(4,128)(2,1)S(1)}, bf16[3,16,4,256]{3,2,0,1:T(4,128)(2,1)S(1)}, u32[]{:S(2)}, u32[]{:S(2)}) collective-permute-start(bf16[3,16,4,256]{3,2,0,1:T(4,128)(2,1)S(1)} %copy.20), channel_id=1, source_target_pairs={{0,1},{1,0},{2,3},{3,2},{4,5},{5,4},{6,7},{7,6},{8,9},{9,8},{10,11... | collective-permute-start | bytes 294920 | tf_op jit(solution)/shard_map/ppermute | solution.py:304
  2.0 7.4 %collective-permute-start.2 = (bf16[3,16,4,256]{3,2,0,1:T(4,128)(2,1)S(1)}, bf16[3,16,4,256]{3,2,0,1:T(4,128)(2,1)S(1)}, u32[]{:S(2)}, u32[]{:S(2)}) collective-permute-start(bf16[3,16,4,256]{3,2,0,1:T(4,128)(2,1)S(1)} %copy.19), channel_id=1, source_target_pairs={{0,7},{1,2},{2,1},{3,4},{4,3},{5,6},{6,5},{7,0},{8,15},{9,10},{10,... | collective-permute-start | bytes 294920 | tf_op jit(solution)/shard_map/ppermute | solution.py:303
  5.7 10.5 %collective-permute-start = (bf16[3,3,16,256]{3,2,1,0:T(8,128)(2,1)S(1)}, bf16[3,3,16,256]{3,2,1,0:T(8,128)(2,1)S(1)}, u32[]{:S(2)}, u32[]{:S(2)}) collective-permute-start(bf16[3,3,16,256]{3,2,1,0:T(8,128)(2,1)S(1)} %get-tuple-element.17), channel_id=1, source_target_pairs={{0,8},{8,16},{16,24},{24,0},{1,9},{9,17},{17,25},{25,1},{2,10},{10... | collective-permute-start | bytes 221192 | tf_op jit(solution)/shard_map/ppermute | solution.py:305
  7.2 9.0 %collective-permute-start.1 = (bf16[3,3,16,256]{3,2,1,0:T(8,128)(2,1)S(1)}, bf16[3,3,16,256]{3,2,1,0:T(8,128)(2,1)S(1)}, u32[]{:S(2)}, u32[]{:S(2)}) collective-permute-start(bf16[3,3,16,256]{3,2,1,0:T(8,128)(2,1)S(1)} %get-tuple-element.18), channel_id=1, source_target_pairs={{8,0},{16,8},{24,16},{0,24},{9,1},{17,9},{25,17},{1,25},{10,2},{18... | collective-permute-start | bytes 221192 | tf_op jit(solution)/shard_map/ppermute | solution.py:306
  9.7 6.5 %collective-permute-start.4 = (bf16[3,8,256]{2,1,0:T(8,128)(2,1)S(1)}, bf16[3,8,256]{2,1,0:T(8,128)(2,1)S(1)}, u32[]{:S(2)}, u32[]{:S(2)}) collective-permute-start(bf16[3,8,256]{2,1,0:T(8,128)(2,1)S(1)} %concatenate.6), channel_id=1, source_target_pairs={{0,8},{8,16},{16,24},{24,0},{1,9},{9,17},{17,25},{25,1},{2,10},{10... | collective-permute-start | bytes 36872 | tf_op jit(solution)/shard_map/ppermute | solution.py:316
  10.2 6.0 %collective-permute-start.5 = (bf16[3,8,256]{2,1,0:T(8,128)(2,1)S(1)}, bf16[3,8,256]{2,1,0:T(8,128)(2,1)S(1)}, u32[]{:S(2)}, u32[]{:S(2)}) collective-permute-start(bf16[3,8,256]{2,1,0:T(8,128)(2,1)S(1)} %concatenate.7), channel_id=1, source_target_pairs={{8,0},{16,8},{24,16},{0,24},{9,1},{17,9},{25,17},{1,25},{10,2},{18... | collective-permute-start | bytes 36872 | tf_op jit(solution)/shard_map/ppermute | solution.py:317
  16.2 16.4 %copy-start.2 = (bf16[768,128]{1,0:T(8,128)(2,1)S(1)}, bf16[768,128]{1,0:T(8,128)(2,1)}, u32[]{:S(2)}) copy-start(bf16[768,128]{1,0:T(8,128)(2,1)} %constant.47.clone.qy_ref) | copy-start | bytes 589828
  16.2 16.4 %copy-start.3 = (bf16[384,128]{1,0:T(8,128)(2,1)S(1)}, bf16[384,128]{1,0:T(8,128)(2,1)}, u32[]{:S(2)}) copy-start(bf16[384,128]{1,0:T(8,128)(2,1)} %constant.48.clone.qyt_ref) | copy-start | bytes 294916
  16.3 16.4 %copy-start.4 = (bf16[64,384]{1,0:T(8,128)(2,1)S(1)}, bf16[64,384]{1,0:T(8,128)(2,1)}, u32[]{:S(2)}) copy-start(bf16[64,384]{1,0:T(8,128)(2,1)} %constant.46.clone.qxt_ref) | copy-start | bytes 147460
  16.3 16.4 %copy-start.5 = (f32[64,128]{1,0:T(8,128)S(1)}, f32[64,128]{1,0:T(8,128)}, u32[]{:S(2)}) copy-start(f32[64,128]{1,0:T(8,128)} %constant.49.clone.ex_ref) | copy-start | bytes 98308
  16.3 16.4 %copy-start.6 = (bf16[64,192]{1,0:T(8,128)(2,1)S(1)}, bf16[64,192]{1,0:T(8,128)(2,1)}, u32[]{:S(2)}) copy-start(bf16[64,192]{1,0:T(8,128)(2,1)} %constant.45.clone.qx_ref) | copy-start | bytes 73732
  16.3 16.4 %copy-start.7 = (f32[8,128]{1,0:T(8,128)S(1)}, f32[8,128]{1,0:T(8,128)}, u32[]{:S(2)}) copy-start(f32[8,128]{1,0:T(8,128)} %constant.50.clone.ey_ref) | copy-start | bytes 12292
  16.3 16.4 %copy-start.8 = (f32[256]{0:T(256)S(1)}, f32[256]{0:T(256)}, u32[]{:S(2)}) copy-start(f32[256]{0:T(256)} %constant.51.clone.em_ref) | copy-start | bytes 3076
  18.7 29.1 %copy-start.1 = (bf16[768,256]{1,0:T(8,128)(2,1)S(1)}, bf16[768,256]{1,0:T(8,128)(2,1)}, u32[]{:S(2)}) copy-start(bf16[768,256]{1,0:T(8,128)(2,1)} %constant.52.clone.basis_ref) | copy-start | bytes 1179652
  18.7 13.9 %all-to-all-start = ((f32[32,8,256]{2,1,0:T(8,128)}), f32[32,8,256]{2,1,0:T(8,128)S(1)}, u32[]{:S(2)}, u32[]{:S(2)}) async-start(f32[32,8,256]{2,1,0:T(8,128)} %bitcast.9), calls=%async_computation | async-start | bytes 524288 | tf_op jit(solution)/shard_map/all_to_all | solution.py:760

commit v3 on v2

--- a/solution.py
+++ b/solution.py
@@ -16,6 +16,8 @@
 TIME_STEP = 0.25
 HALO = 3
 ROWS = 4
+EARLY = 4
+CHUNKS = 2
 LANES = 128
 F32 = jnp.float32
 BF16 = jnp.bfloat16
@@ -197,7 +199,19 @@
     lax.fori_loop(first, last, step, 0, unroll=unroll)
 
 
-def inner_kernel(odd_ref, winds_ref, near_ref, far_ref, wind, above, below, visc, east, part):
+def half_modes(first, source, east, part, basis_ref, modes, half):
+    count, cells_y, levels = source.shape
+    for i in range(count):
+        x = (first + i) % (2 * count) + HALO
+        source[i] = part[x] + (east[x + 1] - east[x - 1])
+    width = count * cells_y
+    flat = source[...].reshape(width, levels)
+    result = dot(basis_ref[...], value_parts(flat, 1, DCT_PARTS), ((1,), (1,)))
+    modes[:, half * width : (half + 1) * width] = result
+
+
+def inner_kernel(place_ref, winds_ref, near_ref, far_ref, basis_ref, *refs):
+    wind, above, below, visc, east, part, modes, source = refs
     cells_x, cells_y, levels = winds_ref.shape[1:]
 
     def load(odd):
@@ -212,19 +226,17 @@
 
         each(0, cells_x, plane, unroll=4)
 
-    by_parity(odd_ref[0], load)
+    by_parity(place_ref[0] % 2, load)
     first, last = HALO, HALO + cells_x
     each(first + 1, last - 1, lambda x: visc_plane(x, wind, above, below, visc), unroll=2)
     each(first + 2, last - 2, lambda x: wind_plane(x, wind, above, below, visc, east, part), unroll=2)
+    half_modes(EARLY, source, east, part, basis_ref, modes, 0)
 
 
 def outer_kernel(low_ref, high_ref, low_corner_ref, high_corner_ref, basis_ref, *refs):
-    wind, above, below, visc, east, part = refs[6:12]
-    out_ref, source = refs[12:]
-    cells_x, cells_y, levels = source.shape
-    skip = cells_x
-
-
+    wind, above, below, visc, east, part, modes, source = refs[7:]
+    levels = wind.shape[3]
+    cells_x = skip = wind.shape[1] - 2 * HALO
     row = lax.broadcasted_iota(jnp.int32, (8, levels), 0)
 
     def load(c):
@@ -241,41 +253,35 @@
     each(1, 7, lambda x: visc_plane(x, wind, above, below, visc), 3, skip - 2, unroll=2)
     each(2, 8, lambda x: wind_plane(x, wind, above, below, visc, east, part), 3, skip - 4, unroll=2)
 
-    def collect(x):
-        source[x] = part[x + HALO] + (east[x + HALO + 1] - east[x + HALO - 1])
-
-    each(0, cells_x, collect, unroll=4)
-    flat = source[...].reshape(cells_x * cells_y, levels)
-    out_ref[...] = dot(basis_ref[...], value_parts(flat, 1, DCT_PARTS), ((1,), (1,)))
-
-
-def pack_kernel(odd_ref, *refs):
+    half_modes(cells_x - EARLY, source, east, part, basis_ref, modes, 1)
+
+
+def pack_kernel(place_ref, *refs):
     winds = refs[:3]
     winds_ref, inner_ref, outer_ref, down_ref, up_ref, sems = refs[3:]
     cells_x, cells_y, levels = winds[0].shape
+    copies = [
+        pltpu.make_async_copy(ref, winds_ref.at[c], sems.at[c]) for c, ref in enumerate(winds)
+    ]
+    for copy in copies:
+        copy.start()
+    for copy in copies:
+        copy.wait()
 
     def pack(odd):
         leading_ref, last_ref = (inner_ref, outer_ref) if odd else (outer_ref, inner_ref)
-        copies = []
-        for c, ref in enumerate(winds):
-            pairs = (
-                (ref.at[:, pl.ds(0, ROWS)], leading_ref.at[c]),
-                (ref.at[:, pl.ds(cells_y - ROWS, ROWS)], last_ref.at[c]),
-                (ref.at[pl.ds(0, HALO)], down_ref.at[c]),
-                (ref.at[pl.ds(cells_x - HALO, HALO)], up_ref.at[c]),
-                (ref, winds_ref.at[c]),
-            )
-            for i, (source, target) in enumerate(pairs):
-                copies.append(pltpu.make_async_copy(source, target, sems.at[5 * c + i]))
-        for copy in copies:
-            copy.start()
-        for copy in copies:
-            copy.wait()
-
-    by_parity(odd_ref[0], pack)
-
-
-def pack_winds(winds, odd):
+        for c in range(3):
+            for x in range(cells_x):
+                own = winds_ref[c, x]
+                leading_ref[c, x] = own[:ROWS]
+                last_ref[c, x] = own[cells_y - ROWS :]
+
+    by_parity(place_ref[0] % 2, pack)
+    down_ref[...] = winds_ref[:, :HALO]
+    up_ref[...] = winds_ref[:, cells_x - HALO :]
+
+
+def pack_winds(winds, place):
     cells_x, cells_y, levels = winds[0].shape
     vmem = pl.BlockSpec(memory_space=pltpu.VMEM)
     edge = pltpu.VMEM((3, cells_x, ROWS, levels), BF16)
@@ -285,19 +291,19 @@
         out_shape=[pltpu.VMEM((3, cells_x, cells_y, levels), BF16), edge, edge, side, side],
         in_specs=[pl.BlockSpec(memory_space=pltpu.SMEM)] + [pl.BlockSpec(memory_space=pl.ANY)] * 3,
         out_specs=[vmem] * 5,
-        scratch_shapes=[pltpu.SemaphoreType.DMA((15,))],
+        scratch_shapes=[pltpu.SemaphoreType.DMA((3,))],
         compiler_params=KERNEL_VMEM,
         name="pack_winds",
-    )(odd, *[pltpu.with_memory_space_constraint(wind, pltpu.HBM) for wind in winds])
-
-
-def source_modes(winds, basis_rows):
+    )(place, *[pltpu.with_memory_space_constraint(wind, pltpu.HBM) for wind in winds])
+
+
+def source_modes(winds, place, basis_rows):
     cells_x, cells_y, levels = winds[0].shape
     planes = cells_x + 2 * HALO
     rows = cells_y + 2 * ROWS
-    odd_north = lax.axis_index("py") % 2
-    odd = odd_north.reshape(1)
-    stacked, inner_rows, outer_rows, leading, last = pack_winds(winds, odd)
+    odd_north = place % 2
+    place = place.reshape(1)
+    stacked, inner_rows, outer_rows, leading, last = pack_winds(winds, place)
     inner, outer = swaps("py")
     up, down = ring("px")
     outer_got = lax.ppermute(outer_rows, "py", outer)
@@ -320,22 +326,26 @@
     shapes = [pltpu.VMEM((3, planes, rows, levels), F32)] * 3
     shapes += [pltpu.VMEM((planes, rows, levels), F32)]
     shapes += [pltpu.VMEM((planes, cells_y, levels), F32)] * 2
+    shapes += [pltpu.VMEM((levels, cells_x * cells_y), F32)]
+    scratch = [pltpu.VMEM((cells_x // 2, cells_y, levels), F32)]
+    basis = on_chip(table_parts(basis_rows * np.float32(0.0625), 1, DCT_PARTS))
     state = pl.pallas_call(
         inner_kernel,
         out_shape=shapes,
-        in_specs=[smem] + [vmem] * 3,
-        out_specs=[vmem] * 6,
+        in_specs=[smem] + [vmem] * 4,
+        out_specs=[vmem] * 7,
+        scratch_shapes=scratch,
         cost_estimate=pl.CostEstimate(flops=40_000_000, bytes_accessed=6_000_000, transcendentals=0),
         compiler_params=KERNEL_VMEM,
         name="inner_planes",
-    )(odd, on_chip(stacked), on_chip(inner_got), on_chip(outer_got))
+    )(place, on_chip(stacked), on_chip(inner_got), on_chip(outer_got), basis)
     results = pl.pallas_call(
         outer_kernel,
-        out_shape=shapes + [pltpu.VMEM((levels, cells_x * cells_y), F32)],
-        in_specs=[vmem] * 11,
+        out_shape=shapes,
+        in_specs=[vmem] * 12,
         out_specs=[vmem] * 7,
-        input_output_aliases={5 + i: i for i in range(6)},
-        scratch_shapes=[pltpu.VMEM((cells_x, cells_y, levels), F32)],
+        input_output_aliases={5 + i: i for i in range(7)},
+        scratch_shapes=scratch,
         compiler_params=KERNEL_VMEM,
         name="outer_planes",
     )(
@@ -343,7 +353,7 @@
         on_chip(high),
         on_chip(low_corner),
         on_chip(high_corner),
-        on_chip(table_parts(basis_rows * np.float32(0.0625), 1, DCT_PARTS)),
+        basis,
         *[on_chip(part) for part in state],
     )
     return results[6]
@@ -369,24 +379,26 @@
 
 def solve_kernel(
     east_count, north_count, cells_x, cells_y,
-    in_ref, qx_ref, qxt_ref, qy_ref, qyt_ref, ex_ref, ey_ref, em_ref, rank_ref, out_ref, work,
+    in_ref, qx_ref, qxt_ref, qy_ref, qyt_ref, ex_ref, ey_ref, em_ref, place_ref, out_ref, work,
 ):
     total_x = east_count * cells_x
     total_y = north_count * cells_y
     block = in_ref.shape[1]
     groups = cells_x // north_count
-    for a in range(east_count):
-        for g in range(groups):
-            lanes = slice(g * total_y, (g + 1) * total_y)
-            pieces = [in_ref[a * north_count + b, :, lanes] for b in range(north_count)]
-            for i, piece in enumerate(block_transpose(pieces, cells_y)):
-                row = (a * cells_x + g * north_count + i) * block
-                work[row : row + block, :] = piece
-    work[...] = dot(value_parts(work[...], 1, NORTH_PARTS), qy_ref[...], ((1,), (0,)))
+    chunk = total_x * block // CHUNKS
+    for h in range(CHUNKS):
+        pieces = []
+        for a in range(h * east_count // CHUNKS, (h + 1) * east_count // CHUNKS):
+            for g in range(groups):
+                lanes = slice(g * total_y, (g + 1) * total_y)
+                got = [in_ref[a * north_count + b, :, lanes] for b in range(north_count)]
+                pieces += block_transpose(got, cells_y)
+        lines = value_parts(jnp.concatenate(pieces, axis=0), 1, NORTH_PARTS)
+        work[h * chunk : (h + 1) * chunk, :] = dot(lines, qy_ref[...], ((1,), (0,)))
     planes = [work[pl.ds(i, total_x, stride=block), :] for i in range(block)]
     waves = dot(qxt_ref[...], value_parts(jnp.concatenate(planes, axis=1), 0, EAST_PARTS), ((1,), (0,)))
     eigen = ex_ref[...] + ey_ref[0:1, :]
-    first = rank_ref[0] * block
+    first = place_ref[0] * block
     solved = []
     for i in range(block):
         value = eigen + em_ref[first + i]
@@ -396,21 +408,25 @@
     back = dot(qx_ref[...], value_parts(jnp.concatenate(solved, axis=1), 0, INVERSE), ((1,), (0,)))
     for i in range(block):
         work[pl.ds(i, total_x, stride=block), :] = back[:, i * total_y : (i + 1) * total_y]
-    work[...] = dot(value_parts(work[...], 1, INVERSE), qyt_ref[...], ((1,), (0,)))
-    for a in range(east_count):
-        for g in range(groups):
-            lanes = slice(g * total_y, (g + 1) * total_y)
-            rows = [(a * cells_x + g * north_count + i) * block for i in range(north_count)]
-            pieces = [work[row : row + block, :] for row in rows]
-            for b, piece in enumerate(block_transpose(pieces, cells_y)):
-                out_ref[a * north_count + b, :, lanes] = piece
-
-
-def solve_planes(blocks, rank, east_count, north_count, cells_x, cells_y, levels):
+    for h in range(CHUNKS):
+        lines = value_parts(work[h * chunk : (h + 1) * chunk, :], 1, INVERSE)
+        lines = dot(lines, qyt_ref[...], ((1,), (0,)))
+        row = 0
+        for a in range(h * east_count // CHUNKS, (h + 1) * east_count // CHUNKS):
+            for g in range(groups):
+                lanes = slice(g * total_y, (g + 1) * total_y)
+                pieces = [lines[row + i * block : row + (i + 1) * block] for i in range(north_count)]
+                row += north_count * block
+                for b, piece in enumerate(block_transpose(pieces, cells_y)):
+                    out_ref[a * north_count + b, :, lanes] = piece
+
+
+def solve_planes(blocks, place, east_count, north_count, cells_x, cells_y, levels):
     total_x = east_count * cells_x
     total_y = north_count * cells_y
     qx, ex = fourier_basis(total_x)
     qy, ey = fourier_basis(total_y)
+    qx = np.roll(qx.reshape(east_count, cells_x, total_x), -EARLY, axis=1).reshape(total_x, total_x)
     tables = [
         table_parts(qx, 1, INVERSE),
         table_parts(qx.T, 1, EAST_PARTS),
@@ -431,19 +447,40 @@
         scratch_shapes=[pltpu.VMEM((total_x * blocks.shape[1], total_y), F32)],
         compiler_params=KERNEL_VMEM,
         name="solve_planes",
-    )(on_chip(blocks), *[on_chip(table) for table in tables], mode_eigen(levels), rank)
-
-
-def pressure_kernel(modes_ref, basis_ref, out_ref):
-    out_ref[...] = dot(value_parts(modes_ref[...], 0, INVERSE), basis_ref[...], ((0,), (0,)))
-
-
-def pressure_cells(modes, basis_rows):
+    )(on_chip(blocks), *[on_chip(table) for table in tables], mode_eigen(levels), place.reshape(1))
+
+
+def pressure_kernel(shift, modes_ref, basis_ref, out_ref, cells, sems):
+    total = cells.shape[0]
+    half = total // 2
+    copies = []
+
+    def send(first, count):
+        target = out_ref.at[pl.ds((first + shift) % total, count)]
+        copy = pltpu.make_async_copy(cells.at[pl.ds(first, count)], target, sems.at[len(copies)])
+        copy.start()
+        copies.append(copy)
+
+    for first in (0, half):
+        part = value_parts(modes_ref[:, first : first + half], 0, INVERSE)
+        cells[first : first + half, :] = dot(part, basis_ref[...], ((0,), (0,)))
+        if first:
+            send(first, half - shift)
+            send(total - shift, shift)
+        else:
+            send(first, half)
+    for copy in copies:
+        copy.wait()
+
+
+def pressure_cells(modes, basis_rows, shift):
+    shape = (modes.shape[1], basis_rows.shape[1])
     return pl.pallas_call(
-        pressure_kernel,
-        out_shape=jax.ShapeDtypeStruct((modes.shape[1], basis_rows.shape[1]), F32),
+        functools.partial(pressure_kernel, shift),
+        out_shape=jax.ShapeDtypeStruct(shape, F32),
         in_specs=[pl.BlockSpec(memory_space=pltpu.VMEM)] * 2,
-        out_specs=pl.BlockSpec(memory_space=pltpu.VMEM),
+        out_specs=pl.BlockSpec(memory_space=pl.ANY),
+        scratch_shapes=[pltpu.VMEM(shape, F32), pltpu.SemaphoreType.DMA((3,))],
         compiler_params=KERNEL_VMEM,
         name="pressure_cells",
     )(on_chip(modes), on_chip(table_parts(basis_rows, 0, INVERSE)))
@@ -733,6 +770,7 @@
         return lax.all_to_all(values, "px", split_axis=1, concat_axis=0, tiled=True)
 
     shaped = modes.reshape(east_count, level_count, cells_x, cells_y).transpose(0, 2, 3, 1)
+    shaped = jnp.roll(shaped, EARLY, axis=1)
     result = spectral(
         shaped.reshape(east_count, cells_x, cells_y * level_count),
         lax.axis_index("px"),
@@ -744,7 +782,8 @@
         bring_back,
         bring_home,
     )
-    result = result.reshape(east_count, cells_x, cells_y, level_count).transpose(0, 3, 1, 2)
+    result = jnp.roll(result.reshape(east_count, cells_x, cells_y, level_count), -EARLY, axis=1)
+    result = result.transpose(0, 3, 1, 2)
     return result.reshape(levels, cells_x * cells_y)
 
 
@@ -754,17 +793,18 @@
     north_count = lax.axis_size("py")
     devices = east_count * north_count
     basis_rows = np.ascontiguousarray(cosine_basis(levels).T)
-    modes = source_modes((wind_east, wind_north, wind_up), basis_rows)
+    north_rank = lax.axis_index("py")
+    place = lax.axis_index("px") * north_count + north_rank
+    modes = source_modes((wind_east, wind_north, wind_up), place, basis_rows)
     if levels == 8 * devices and north_count * cells_y == 128 and cells_x % north_count == 0:
         blocks = modes.reshape(devices, levels // devices, cells_x * cells_y)
         blocks = lax.all_to_all(blocks, ("px", "py"), split_axis=0, concat_axis=0, tiled=True)
-        rank = (lax.axis_index("px") * north_count + lax.axis_index("py")).reshape(1)
-        blocks = solve_planes(blocks, rank, east_count, north_count, cells_x, cells_y, levels)
+        blocks = solve_planes(blocks, place, east_count, north_count, cells_x, cells_y, levels)
         blocks = lax.all_to_all(blocks, ("px", "py"), split_axis=0, concat_axis=0, tiled=True)
         modes = blocks.reshape(levels, cells_x * cells_y)
     else:
         modes = staged(modes, east_count, north_count, cells_x, cells_y)
-    return pressure_cells(modes, basis_rows).reshape(cells_x, cells_y, levels)
+    return pressure_cells(modes, basis_rows, EARLY * cells_y).reshape(cells_x, cells_y, levels)
 
 
 def solution(mesh):

time: 49.1 us -> 47.5 us (0.967)
  blocking collectives: 12.8 us -> 26.2 us
  waiting for transfers between devices: 10.6 us -> 0.02 us
  starting transfers between devices: 15.3 us -> 11.9 us
  Pallas kernels: 9.57 us -> 8.54 us
    all_to_all x1 -> x2, blocking collectives: 12.8 us -> 26.2 us  [shards(): lax.all_to_all(blocks, ('px', 'py'), split_axis=0, concat_axis=0, tiled=T...]
    all_to_all x1 -> x0, waiting for transfers between devices: 10.6 us -> none  [shards(): lax.all_to_all(blocks, ('px', 'py'), split_axis=0, concat_axis=0, tiled=T...]
    all_to_all x1 -> x0, starting transfers between devices: 3.34 us -> none  [shards(): lax.all_to_all(blocks, ('px', 'py'), split_axis=0, concat_axis=0, tiled=T...]
    pallas_call x2, Pallas kernels: 3.39 us -> 2.56 us  [the longest x1 1.55 us: source_modes(): pl.pallas_call(outer_kernel, out_shape=shapes, in_specs=[vmem] * 12, out_...]
  transfers between devices with their start and end apart: 7 -> 6, of which waited for: 1 -> 0; matrix products, arithmetic and copies ran while one was open for 1% -> 1% of each run, Pallas kernels for 5% -> 6%
where the time goes in v3:
time: 47.5 us; the launch traced here: 47.3 us
  blocking collectives  26.2 us (55%)
  starting transfers between devices  11.9 us (25%)
  Pallas kernels  8.54 us (18%)
    all_to_all x2, blocking collectives, shards(): lax.all_to_all(blocks, ('px', 'py'), split_axis=0, concat_axis=0, tiled=T...  26.2 us
    ppermute x1, starting transfers between devices, source_modes(): outer_got = lax.ppermute(outer_rows, 'py', outer)  3.61 us
    ppermute x1, starting transfers between devices, source_modes(): high_corner = lax.ppermute(corner(0, 1), 'px', down)  3.41 us
    pallas_call x1, Pallas kernels, source_modes(): pl.pallas_call(inner_kernel, out_shape=shapes, in_specs=[smem] + [vmem] *...  2.75 us
    ppermute x1, starting transfers between devices, source_modes(): high = lax.ppermute(leading, 'px', down)  2.25 us
    pallas_call x1, Pallas kernels, solve_planes(): pl.pallas_call(functools.partial(solve_kernel, east_count, north_count, c...  2.05 us
    ppermute x1, starting transfers between devices, source_modes(): low = lax.ppermute(last, 'px', up)  1.58 us
    pallas_call x1, Pallas kernels, source_modes(): pl.pallas_call(outer_kernel, out_shape=shapes, in_specs=[vmem] * 12, out_...  1.55 us
  transfers between devices with their start and end apart: 6, of which 0 were waited for; matrix products, arithmetic and copies ran while one was open for 1% of the time, Pallas kernels for 6%

profile of v3, /device:TPU:0, one launch (start us, length us, event | category | flops | bytes accessed | tf_op | source)
XLA Modules:
  0.0 47.3 jit_solution(11847729285968918707)
XLA Ops:
  0.0 1.2 %pack_winds.1 = (bf16[3,16,16,256]{3,2,1,0:T(8,128)(2,1)S(1)}, bf16[3,16,4,256]{3,2,1,0:T(4,128)(2,1)S(1)}, bf16[3,16,4,256]{3,2,1,0:T(4,128)(2,1)S(1)}, bf16[3,...) custom-call(s32[1]{0:T(128)} %bitcast.place_ref, bf16[16,16,256]{2,1,0:T(8,128)(2,1)} %refs_0_.1, ...), custom_call_target="tpu_custom_call" | custom-call | tf_op jit(solution)/shard_map/pack_winds/pallas_call | solution.py:289
  1.2 0.6 %collective-permute-start.3 = (bf16[3,16,4,256]{3,2,0,1:T(4,128)(2,1)S(1)}, bf16[3,16,4,256]{3,2,0,1:T(4,128)(2,1)S(1)}, u32[]{:S(2)}, u32[]{:S(2)}) collective-permute-start(bf16[3,16,4,256]{3,2,0,1:T(4,128)(2,1)S(1)} %copy.21), channel_id=1, source_target_pairs={{0,1},{1,0},{2,3},{3,2},{4,5},{5,4},{6,7},{7,6},{8,9},{9,8},{10,11... | collective-permute-start | bytes 294920 | tf_op jit(solution)/shard_map/ppermute | solution.py:310
  1.8 3.6 %collective-permute-start.2 = (bf16[3,16,4,256]{3,2,0,1:T(4,128)(2,1)S(1)}, bf16[3,16,4,256]{3,2,0,1:T(4,128)(2,1)S(1)}, u32[]{:S(2)}, u32[]{:S(2)}) collective-permute-start(bf16[3,16,4,256]{3,2,0,1:T(4,128)(2,1)S(1)} %copy.20), channel_id=1, source_target_pairs={{0,7},{1,2},{2,1},{3,4},{4,3},{5,6},{6,5},{7,0},{8,15},{9,10},{10,... | collective-permute-start | bytes 294920 | tf_op jit(solution)/shard_map/ppermute | solution.py:309
  5.5 1.6 %collective-permute-start = (bf16[3,3,16,256]{3,2,1,0:T(8,128)(2,1)S(1)}, bf16[3,3,16,256]{3,2,1,0:T(8,128)(2,1)S(1)}, u32[]{:S(2)}, u32[]{:S(2)}) collective-permute-start(bf16[3,3,16,256]{3,2,1,0:T(8,128)(2,1)S(1)} %get-tuple-element.18), channel_id=1, source_target_pairs={{0,8},{8,16},{16,24},{24,0},{1,9},{9,17},{17,25},{25,1},{2,10},{10... | collective-permute-start | bytes 221192 | tf_op jit(solution)/shard_map/ppermute | solution.py:311
  7.0 2.2 %collective-permute-start.1 = (bf16[3,3,16,256]{3,2,1,0:T(8,128)(2,1)S(1)}, bf16[3,3,16,256]{3,2,1,0:T(8,128)(2,1)S(1)}, u32[]{:S(2)}, u32[]{:S(2)}) collective-permute-start(bf16[3,3,16,256]{3,2,1,0:T(8,128)(2,1)S(1)} %get-tuple-element.19), channel_id=1, source_target_pairs={{8,0},{16,8},{24,16},{0,24},{9,1},{17,9},{25,17},{1,25},{10,2},{18... | collective-permute-start | bytes 221192 | tf_op jit(solution)/shard_map/ppermute | solution.py:312
  9.3 0.0 collective-permute-done.3
  9.3 0.0 collective-permute-done.2
  9.5 0.5 %collective-permute-start.4 = (bf16[3,8,256]{2,1,0:T(8,128)(2,1)S(1)}, bf16[3,8,256]{2,1,0:T(8,128)(2,1)S(1)}, u32[]{:S(2)}, u32[]{:S(2)}) collective-permute-start(bf16[3,8,256]{2,1,0:T(8,128)(2,1)S(1)} %concatenate.6), channel_id=1, source_target_pairs={{0,8},{8,16},{16,24},{24,0},{1,9},{9,17},{17,25},{25,1},{2,10},{10... | collective-permute-start | bytes 36872 | tf_op jit(solution)/shard_map/ppermute | solution.py:322
  10.0 3.4 %collective-permute-start.5 = (bf16[3,8,256]{2,1,0:T(8,128)(2,1)S(1)}, bf16[3,8,256]{2,1,0:T(8,128)(2,1)S(1)}, u32[]{:S(2)}, u32[]{:S(2)}) collective-permute-start(bf16[3,8,256]{2,1,0:T(8,128)(2,1)S(1)} %concatenate.7), channel_id=1, source_target_pairs={{8,0},{16,8},{24,16},{0,24},{9,1},{17,9},{25,17},{1,25},{10,2},{18... | collective-permute-start | bytes 36872 | tf_op jit(solution)/shard_map/ppermute | solution.py:323
  13.5 2.7 %inner_planes.1 = (f32[3,22,24,256]{3,2,1,0:T(8,128)S(1)}, f32[3,22,24,256]{3,2,1,0:T(8,128)S(1)}, f32[3,22,24,256]{3,2,1,0:T(8,128)S(1)}, f32[22,24,256]{2,1,0:...) custom-call(s32[1]{0:T(128)} %bitcast.place_ref, ...), custom_call_target="tpu_custom_call" | custom-call | flops 40000000 | bytes 6000000 | tf_op jit(solution)/shard_map/inner_planes/pallas_call | solution.py:332
  16.3 0.0 collective-permute-done.low_ref
  16.3 0.0 collective-permute-done.1.high_ref
  16.3 0.0 collective-permute-done.4.low_corner_ref
  16.3 0.0 collective-permute-done.5.high_corner_ref
  16.3 0.0 copy-start.2
  16.4 0.0 copy-start.3
  16.4 0.0 copy-start.4
  16.4 0.0 copy-start.5
  16.4 0.0 copy-start.6
  16.4 0.0 copy-start.7
  16.4 0.0 copy-start.8
  16.4 1.5 %outer_planes.1 = (f32[3,22,24,256]{3,2,1,0:T(8,128)S(1)}, f32[3,22,24,256]{3,2,1,0:T(8,128)S(1)}, f32[3,22,24,256]{3,2,1,0:T(8,128)S(1)}, f32[22,24,256]{2,1,0:...) custom-call(bf16[3,3,16,256]{3,2,1,0:T(8,128)(2,1)S(1)} %collective-, ...), custom_call_target="tpu_custom_call", output_to_operand_aliasing={{0}: (5, {}), {1}: (6, {}), {2}: (7, {}), {3}: (8, {}), {4}... | custom-call | tf_op jit(solution)/shard_map/outer_planes/pallas_call | solution.py:342
  18.0 0.0 copy-start.1
  18.0 13.4 %all_to_all.10.in_ref = f32[32,8,256]{2,1,0:T(8,128)S(1)} all-to-all(f32[32,8,256]{2,1,0:T(8,128)S(1)} %bitcast.20), channel_id=1, replica_groups=mesh['px'=4,'py'=8] {'px','py'}, dimensions={0} | all-to-all | bytes 524288 | tf_op jit(solution)/shard_map/all_to_all | solution.py:801
  31.4 0.0 copy-done.5
  31.4 0.0 copy-done.6
  31.4 0.0 copy-done.7
  31.4 0.0 copy-done.8
  31.4 2.0 %solve_planes.1 = f32[32,8,256]{2,1,0:T(8,128)S(1)} custom-call(f32[32,8,256]{2,1,0:T(8,128)S(1)} %all_to_all.10.in_ref, bf16[64,192]{1,0:T(8,128)(2,1)S(1)} %copy-done.6, bf16[64,384]{1,0:T(8,128)(2,1)S(1)} %copy-done.4, bf16[768,128]{1,0:T(8,128)(2,1)S(1)} %copy-done.2, bf16[384,128]{1,0:T(8,128)(2,1)S(1)} %copy-done.3, f32[64,128]{1,0:T(8,128)S(1)} %copy-done.5, ...), custom_call_target="tpu_custom_call" | custom-call | tf_op jit(solution)/shard_map/solve_planes/pallas_call | solution.py:442
  33.5 12.8 %all_to_all.11 = f32[32,8,256]{2,1,0:T(8,128)S(1)} all-to-all(f32[32,8,256]{2,1,0:T(8,128)S(1)} %solve_planes.1), channel_id=1, replica_groups=mesh['px'=4,'py'=8] {'px','py'}, dimensions={0} | all-to-all | bytes 524288 | tf_op jit(solution)/shard_map/all_to_all | solution.py:803
  46.3 0.0 copy-done.1
  46.3 1.0 %pressure_cells.1 = f32[256,256]{1,0:T(8,128)} custom-call(f32[256,256]{1,0:T(8,128)S(1)} %bitcast.21, bf16[768,256]{1,0:T(8,128)(2,1)S(1)} %copy-done.1), custom_call_target="tpu_custom_call" | custom-call | tf_op jit(solution)/shard_map/pressure_cells/pallas_call | solution.py:478
  (21 shorter events, 0.3 us)
Async XLA Ops:
  0.0 13.5 %copy-start = (bf16[256,1536]{1,0:T(8,128)(2,1)S(1)}, bf16[256,1536]{1,0:T(8,128)(2,1)}, u32[]{:S(2)}) copy-start(bf16[256,1536]{1,0:T(8,128)(2,1)} %constant.44.clone.basis_ref) | copy-start | bytes 2359300
  1.2 8.0 %collective-permute-start.3 = (bf16[3,16,4,256]{3,2,0,1:T(4,128)(2,1)S(1)}, bf16[3,16,4,256]{3,2,0,1:T(4,128)(2,1)S(1)}, u32[]{:S(2)}, u32[]{:S(2)}) collective-permute-start(bf16[3,16,4,256]{3,2,0,1:T(4,128)(2,1)S(1)} %copy.21), channel_id=1, source_target_pairs={{0,1},{1,0},{2,3},{3,2},{4,5},{5,4},{6,7},{7,6},{8,9},{9,8},{10,11... | collective-permute-start | bytes 294920 | tf_op jit(solution)/shard_map/ppermute | solution.py:310
  1.8 7.4 %collective-permute-start.2 = (bf16[3,16,4,256]{3,2,0,1:T(4,128)(2,1)S(1)}, bf16[3,16,4,256]{3,2,0,1:T(4,128)(2,1)S(1)}, u32[]{:S(2)}, u32[]{:S(2)}) collective-permute-start(bf16[3,16,4,256]{3,2,0,1:T(4,128)(2,1)S(1)} %copy.20), channel_id=1, source_target_pairs={{0,7},{1,2},{2,1},{3,4},{4,3},{5,6},{6,5},{7,0},{8,15},{9,10},{10,... | collective-permute-start | bytes 294920 | tf_op jit(solution)/shard_map/ppermute | solution.py:309
  5.5 10.8 %collective-permute-start = (bf16[3,3,16,256]{3,2,1,0:T(8,128)(2,1)S(1)}, bf16[3,3,16,256]{3,2,1,0:T(8,128)(2,1)S(1)}, u32[]{:S(2)}, u32[]{:S(2)}) collective-permute-start(bf16[3,3,16,256]{3,2,1,0:T(8,128)(2,1)S(1)} %get-tuple-element.18), channel_id=1, source_target_pairs={{0,8},{8,16},{16,24},{24,0},{1,9},{9,17},{17,25},{25,1},{2,10},{10... | collective-permute-start | bytes 221192 | tf_op jit(solution)/shard_map/ppermute | solution.py:311
  7.0 9.3 %collective-permute-start.1 = (bf16[3,3,16,256]{3,2,1,0:T(8,128)(2,1)S(1)}, bf16[3,3,16,256]{3,2,1,0:T(8,128)(2,1)S(1)}, u32[]{:S(2)}, u32[]{:S(2)}) collective-permute-start(bf16[3,3,16,256]{3,2,1,0:T(8,128)(2,1)S(1)} %get-tuple-element.19), channel_id=1, source_target_pairs={{8,0},{16,8},{24,16},{0,24},{9,1},{17,9},{25,17},{1,25},{10,2},{18... | collective-permute-start | bytes 221192 | tf_op jit(solution)/shard_map/ppermute | solution.py:312
  9.5 6.8 %collective-permute-start.4 = (bf16[3,8,256]{2,1,0:T(8,128)(2,1)S(1)}, bf16[3,8,256]{2,1,0:T(8,128)(2,1)S(1)}, u32[]{:S(2)}, u32[]{:S(2)}) collective-permute-start(bf16[3,8,256]{2,1,0:T(8,128)(2,1)S(1)} %concatenate.6), channel_id=1, source_target_pairs={{0,8},{8,16},{16,24},{24,0},{1,9},{9,17},{17,25},{25,1},{2,10},{10... | collective-permute-start | bytes 36872 | tf_op jit(solution)/shard_map/ppermute | solution.py:322
  10.0 6.3 %collective-permute-start.5 = (bf16[3,8,256]{2,1,0:T(8,128)(2,1)S(1)}, bf16[3,8,256]{2,1,0:T(8,128)(2,1)S(1)}, u32[]{:S(2)}, u32[]{:S(2)}) collective-permute-start(bf16[3,8,256]{2,1,0:T(8,128)(2,1)S(1)} %concatenate.7), channel_id=1, source_target_pairs={{8,0},{16,8},{24,16},{0,24},{9,1},{17,9},{25,17},{1,25},{10,2},{18... | collective-permute-start | bytes 36872 | tf_op jit(solution)/shard_map/ppermute | solution.py:323
  16.3 15.1 %copy-start.2 = (bf16[768,128]{1,0:T(8,128)(2,1)S(1)}, bf16[768,128]{1,0:T(8,128)(2,1)}, u32[]{:S(2)}) copy-start(bf16[768,128]{1,0:T(8,128)(2,1)} %constant.47.clone.qy_ref) | copy-start | bytes 589828
  16.4 15.0 %copy-start.3 = (bf16[384,128]{1,0:T(8,128)(2,1)S(1)}, bf16[384,128]{1,0:T(8,128)(2,1)}, u32[]{:S(2)}) copy-start(bf16[384,128]{1,0:T(8,128)(2,1)} %constant.48.clone.qyt_ref) | copy-start | bytes 294916
  16.4 15.0 %copy-start.4 = (bf16[64,384]{1,0:T(8,128)(2,1)S(1)}, bf16[64,384]{1,0:T(8,128)(2,1)}, u32[]{:S(2)}) copy-start(bf16[64,384]{1,0:T(8,128)(2,1)} %constant.46.clone.qxt_ref) | copy-start | bytes 147460
  16.4 15.0 %copy-start.5 = (f32[64,128]{1,0:T(8,128)S(1)}, f32[64,128]{1,0:T(8,128)}, u32[]{:S(2)}) copy-start(f32[64,128]{1,0:T(8,128)} %constant.49.clone.ex_ref) | copy-start | bytes 98308
  16.4 15.0 %copy-start.6 = (bf16[64,192]{1,0:T(8,128)(2,1)S(1)}, bf16[64,192]{1,0:T(8,128)(2,1)}, u32[]{:S(2)}) copy-start(bf16[64,192]{1,0:T(8,128)(2,1)} %constant.45.clone.qx_ref) | copy-start | bytes 73732
  16.4 15.0 %copy-start.7 = (f32[8,128]{1,0:T(8,128)S(1)}, f32[8,128]{1,0:T(8,128)}, u32[]{:S(2)}) copy-start(f32[8,128]{1,0:T(8,128)} %constant.50.clone.ey_ref) | copy-start | bytes 12292
  16.4 15.0 %copy-start.8 = (f32[256]{0:T(256)S(1)}, f32[256]{0:T(256)}, u32[]{:S(2)}) copy-start(f32[256]{0:T(256)} %constant.51.clone.em_ref) | copy-start | bytes 3076
  18.0 28.3 %copy-start.1 = (bf16[768,256]{1,0:T(8,128)(2,1)S(1)}, bf16[768,256]{1,0:T(8,128)(2,1)}, u32[]{:S(2)}) copy-start(bf16[768,256]{1,0:T(8,128)(2,1)} %constant.52.clone.basis_ref) | copy-start | bytes 1179652

commit v4 on v3

--- a/solution.py
+++ b/solution.py
@@ -210,8 +210,10 @@
     modes[:, half * width : (half + 1) * width] = result
 
 
-def inner_kernel(place_ref, winds_ref, near_ref, far_ref, basis_ref, *refs):
-    wind, above, below, visc, east, part, modes, source = refs
+def inner_kernel(place_ref, winds_ref, near_ref, far_ref, table_ref, *refs):
+    wind, above, below, visc, east, part, modes, basis_ref, source, sem = refs
+    fetch = pltpu.make_async_copy(table_ref, basis_ref, sem)
+    fetch.start()
     cells_x, cells_y, levels = winds_ref.shape[1:]
 
     def load(odd):
@@ -226,10 +228,11 @@
 
         each(0, cells_x, plane, unroll=4)
 
-    by_parity(place_ref[0] % 2, load)
+    by_parity(place_ref[0] // lax.axis_size("px") % 2, load)
     first, last = HALO, HALO + cells_x
     each(first + 1, last - 1, lambda x: visc_plane(x, wind, above, below, visc), unroll=2)
     each(first + 2, last - 2, lambda x: wind_plane(x, wind, above, below, visc, east, part), unroll=2)
+    fetch.wait()
     half_modes(EARLY, source, east, part, basis_ref, modes, 0)
 
 
@@ -276,7 +279,7 @@
                 leading_ref[c, x] = own[:ROWS]
                 last_ref[c, x] = own[cells_y - ROWS :]
 
-    by_parity(place_ref[0] % 2, pack)
+    by_parity(place_ref[0] // lax.axis_size("px") % 2, pack)
     down_ref[...] = winds_ref[:, :HALO]
     up_ref[...] = winds_ref[:, cells_x - HALO :]
 
@@ -301,7 +304,7 @@
     cells_x, cells_y, levels = winds[0].shape
     planes = cells_x + 2 * HALO
     rows = cells_y + 2 * ROWS
-    odd_north = place % 2
+    odd_north = place // lax.axis_size("px") % 2
     place = place.reshape(1)
     stacked, inner_rows, outer_rows, leading, last = pack_winds(winds, place)
     inner, outer = swaps("py")
@@ -328,17 +331,21 @@
     shapes += [pltpu.VMEM((planes, cells_y, levels), F32)] * 2
     shapes += [pltpu.VMEM((levels, cells_x * cells_y), F32)]
     scratch = [pltpu.VMEM((cells_x // 2, cells_y, levels), F32)]
-    basis = on_chip(table_parts(basis_rows * np.float32(0.0625), 1, DCT_PARTS))
+    basis = table_parts(basis_rows * np.float32(0.0625), 1, DCT_PARTS)
     state = pl.pallas_call(
         inner_kernel,
-        out_shape=shapes,
-        in_specs=[smem] + [vmem] * 4,
-        out_specs=[vmem] * 7,
-        scratch_shapes=scratch,
+        out_shape=shapes + [pltpu.VMEM(basis.shape, BF16)],
+        in_specs=[smem] + [vmem] * 3 + [pl.BlockSpec(memory_space=pl.ANY)],
+        out_specs=[vmem] * 8,
+        scratch_shapes=scratch + [pltpu.SemaphoreType.DMA],
         cost_estimate=pl.CostEstimate(flops=40_000_000, bytes_accessed=6_000_000, transcendentals=0),
         compiler_params=KERNEL_VMEM,
         name="inner_planes",
-    )(place, on_chip(stacked), on_chip(inner_got), on_chip(outer_got), basis)
+    )(
+        place,
+        *[on_chip(got) for got in (stacked, inner_got, outer_got)],
+        pltpu.with_memory_space_constraint(basis, pltpu.HBM),
+    )
     results = pl.pallas_call(
         outer_kernel,
         out_shape=shapes,
@@ -353,8 +360,8 @@
         on_chip(high),
         on_chip(low_corner),
         on_chip(high_corner),
-        basis,
-        *[on_chip(part) for part in state],
+        on_chip(state[7]),
+        *[on_chip(part) for part in state[:7]],
     )
     return results[6]
 
@@ -391,7 +398,7 @@
         for a in range(h * east_count // CHUNKS, (h + 1) * east_count // CHUNKS):
             for g in range(groups):
                 lanes = slice(g * total_y, (g + 1) * total_y)
-                got = [in_ref[a * north_count + b, :, lanes] for b in range(north_count)]
+                got = [in_ref[b * east_count + a, :, lanes] for b in range(north_count)]
                 pieces += block_transpose(got, cells_y)
         lines = value_parts(jnp.concatenate(pieces, axis=0), 1, NORTH_PARTS)
         work[h * chunk : (h + 1) * chunk, :] = dot(lines, qy_ref[...], ((1,), (0,)))
@@ -418,7 +425,7 @@
                 pieces = [lines[row + i * block : row + (i + 1) * block] for i in range(north_count)]
                 row += north_count * block
                 for b, piece in enumerate(block_transpose(pieces, cells_y)):
-                    out_ref[a * north_count + b, :, lanes] = piece
+                    out_ref[b * east_count + a, :, lanes] = piece
 
 
 def solve_planes(blocks, place, east_count, north_count, cells_x, cells_y, levels):
@@ -794,13 +801,13 @@
     devices = east_count * north_count
     basis_rows = np.ascontiguousarray(cosine_basis(levels).T)
     north_rank = lax.axis_index("py")
-    place = lax.axis_index("px") * north_count + north_rank
+    place = north_rank * east_count + lax.axis_index("px")
     modes = source_modes((wind_east, wind_north, wind_up), place, basis_rows)
     if levels == 8 * devices and north_count * cells_y == 128 and cells_x % north_count == 0:
         blocks = modes.reshape(devices, levels // devices, cells_x * cells_y)
-        blocks = lax.all_to_all(blocks, ("px", "py"), split_axis=0, concat_axis=0, tiled=True)
+        blocks = lax.all_to_all(blocks, ("py", "px"), split_axis=0, concat_axis=0, tiled=True)
         blocks = solve_planes(blocks, place, east_count, north_count, cells_x, cells_y, levels)
-        blocks = lax.all_to_all(blocks, ("px", "py"), split_axis=0, concat_axis=0, tiled=True)
+        blocks = lax.all_to_all(blocks, ("py", "px"), split_axis=0, concat_axis=0, tiled=True)
         modes = blocks.reshape(levels, cells_x * cells_y)
     else:
         modes = staged(modes, east_count, north_count, cells_x, cells_y)

time: 47.5 us -> 46.9 us (0.987)
  blocking collectives: 26.2 us -> 25.7 us
where the time goes in v4:
time: 46.9 us; the launch traced here: 46.8 us
  blocking collectives  25.7 us (55%)
  starting transfers between devices  11.9 us (25%)
  Pallas kernels  8.5 us (18%)
    all_to_all x2, blocking collectives, shards(): lax.all_to_all(blocks, ('py', 'px'), split_axis=0, concat_axis=0, tiled=T...  25.7 us
    ppermute x1, starting transfers between devices, source_modes(): outer_got = lax.ppermute(outer_rows, 'py', outer)  3.61 us
    ppermute x1, starting transfers between devices, source_modes(): high_corner = lax.ppermute(corner(0, 1), 'px', down)  3.41 us
    pallas_call x1, Pallas kernels, source_modes(): pl.pallas_call(inner_kernel, out_shape=shapes + [pltpu.VMEM(basis.shape,...  2.78 us
    ppermute x1, starting transfers between devices, source_modes(): high = lax.ppermute(leading, 'px', down)  2.25 us
    pallas_call x1, Pallas kernels, solve_planes(): pl.pallas_call(functools.partial(solve_kernel, east_count, north_count, c...  2.05 us
    ppermute x1, starting transfers between devices, source_modes(): low = lax.ppermute(last, 'px', up)  1.58 us
    pallas_call x1, Pallas kernels, source_modes(): pl.pallas_call(outer_kernel, out_shape=shapes, in_specs=[vmem] * 12, out_...  1.55 us
  transfers between devices with their start and end apart: 6, of which 0 were waited for; matrix products, arithmetic and copies ran while one was open for 1% of the time, Pallas kernels for 6%

profile of v4, /device:TPU:0, one launch (start us, length us, event | category | flops | bytes accessed | tf_op | source)
XLA Modules:
  0.0 46.8 jit_solution(13545851241608042437)
XLA Ops:
  0.0 1.1 %pack_winds.1 = (bf16[3,16,16,256]{3,2,1,0:T(8,128)(2,1)S(1)}, bf16[3,16,4,256]{3,2,1,0:T(4,128)(2,1)S(1)}, bf16[3,16,4,256]{3,2,1,0:T(4,128)(2,1)S(1)}, bf16[3,...) custom-call(s32[1]{0:T(128)} %bitcast.place_ref, bf16[16,16,256]{2,1,0:T(8,128)(2,1)} %refs_0_.1, ...), custom_call_target="tpu_custom_call" | custom-call | tf_op jit(solution)/shard_map/pack_winds/pallas_call | solution.py:292
  1.2 0.6 %collective-permute-start.3 = (bf16[3,16,4,256]{3,2,0,1:T(4,128)(2,1)S(1)}, bf16[3,16,4,256]{3,2,0,1:T(4,128)(2,1)S(1)}, u32[]{:S(2)}, u32[]{:S(2)}) collective-permute-start(bf16[3,16,4,256]{3,2,0,1:T(4,128)(2,1)S(1)} %copy.21), channel_id=1, source_target_pairs={{0,1},{1,0},{2,3},{3,2},{4,5},{5,4},{6,7},{7,6},{8,9},{9,8},{10,11... | collective-permute-start | bytes 294920 | tf_op jit(solution)/shard_map/ppermute | solution.py:313
  1.8 3.6 %collective-permute-start.2 = (bf16[3,16,4,256]{3,2,0,1:T(4,128)(2,1)S(1)}, bf16[3,16,4,256]{3,2,0,1:T(4,128)(2,1)S(1)}, u32[]{:S(2)}, u32[]{:S(2)}) collective-permute-start(bf16[3,16,4,256]{3,2,0,1:T(4,128)(2,1)S(1)} %copy.20), channel_id=1, source_target_pairs={{0,7},{1,2},{2,1},{3,4},{4,3},{5,6},{6,5},{7,0},{8,15},{9,10},{10,... | collective-permute-start | bytes 294920 | tf_op jit(solution)/shard_map/ppermute | solution.py:312
  5.4 1.6 %collective-permute-start = (bf16[3,3,16,256]{3,2,1,0:T(8,128)(2,1)S(1)}, bf16[3,3,16,256]{3,2,1,0:T(8,128)(2,1)S(1)}, u32[]{:S(2)}, u32[]{:S(2)}) collective-permute-start(bf16[3,3,16,256]{3,2,1,0:T(8,128)(2,1)S(1)} %get-tuple-element.19), channel_id=1, source_target_pairs={{0,8},{8,16},{16,24},{24,0},{1,9},{9,17},{17,25},{25,1},{2,10},{10... | collective-permute-start | bytes 221192 | tf_op jit(solution)/shard_map/ppermute | solution.py:314
  7.0 2.2 %collective-permute-start.1 = (bf16[3,3,16,256]{3,2,1,0:T(8,128)(2,1)S(1)}, bf16[3,3,16,256]{3,2,1,0:T(8,128)(2,1)S(1)}, u32[]{:S(2)}, u32[]{:S(2)}) collective-permute-start(bf16[3,3,16,256]{3,2,1,0:T(8,128)(2,1)S(1)} %get-tuple-element.20), channel_id=1, source_target_pairs={{8,0},{16,8},{24,16},{0,24},{9,1},{17,9},{25,17},{1,25},{10,2},{18... | collective-permute-start | bytes 221192 | tf_op jit(solution)/shard_map/ppermute | solution.py:315
  9.2 0.0 collective-permute-done.3
  9.2 0.0 collective-permute-done.2
  9.4 0.5 %collective-permute-start.4 = (bf16[3,8,256]{2,1,0:T(8,128)(2,1)S(1)}, bf16[3,8,256]{2,1,0:T(8,128)(2,1)S(1)}, u32[]{:S(2)}, u32[]{:S(2)}) collective-permute-start(bf16[3,8,256]{2,1,0:T(8,128)(2,1)S(1)} %concatenate.6), channel_id=1, source_target_pairs={{0,8},{8,16},{16,24},{24,0},{1,9},{9,17},{17,25},{25,1},{2,10},{10... | collective-permute-start | bytes 36872 | tf_op jit(solution)/shard_map/ppermute | solution.py:325
  10.0 3.4 %collective-permute-start.5 = (bf16[3,8,256]{2,1,0:T(8,128)(2,1)S(1)}, bf16[3,8,256]{2,1,0:T(8,128)(2,1)S(1)}, u32[]{:S(2)}, u32[]{:S(2)}) collective-permute-start(bf16[3,8,256]{2,1,0:T(8,128)(2,1)S(1)} %concatenate.7), channel_id=1, source_target_pairs={{8,0},{16,8},{24,16},{0,24},{9,1},{17,9},{25,17},{1,25},{10,2},{18... | collective-permute-start | bytes 36872 | tf_op jit(solution)/shard_map/ppermute | solution.py:326
  13.5 2.8 %inner_planes.1 = (f32[3,22,24,256]{3,2,1,0:T(8,128)S(1)}, f32[3,22,24,256]{3,2,1,0:T(8,128)S(1)}, f32[3,22,24,256]{3,2,1,0:T(8,128)S(1)}, f32[22,24,256]{2,1,0:...) custom-call(s32[1]{0:T(128)} %bitcast.place_ref, ...), custom_call_target="tpu_custom_call" | custom-call | flops 40000000 | bytes 6000000 | tf_op jit(solution)/shard_map/inner_planes/pallas_call | solution.py:335
  16.2 0.0 collective-permute-done.low_ref
  16.3 0.0 collective-permute-done.1.high_ref
  16.3 0.0 collective-permute-done.4.low_corner_ref
  16.3 0.0 collective-permute-done.5.high_corner_ref
  16.3 0.0 copy-start.1
  16.3 0.0 copy-start.2
  16.3 0.0 copy-start.3
  16.3 0.0 copy-start.4
  16.3 0.0 copy-start.5
  16.3 0.0 copy-start.6
  16.4 0.0 copy-start.7
  16.4 1.5 %outer_planes.1 = (f32[3,22,24,256]{3,2,1,0:T(8,128)S(1)}, f32[3,22,24,256]{3,2,1,0:T(8,128)S(1)}, f32[3,22,24,256]{3,2,1,0:T(8,128)S(1)}, f32[22,24,256]{2,1,0:...) custom-call(bf16[3,3,16,256]{3,2,1,0:T(8,128)(2,1)S(1)} %collective-, ...), custom_call_target="tpu_custom_call", output_to_operand_aliasing={{0}: (5, {}), {1}: (6, {}), {2}: (7, {}), {3}: (8, {}), {4}... | custom-call | tf_op jit(solution)/shard_map/outer_planes/pallas_call | solution.py:349
  17.9 0.0 copy-start
  17.9 13.0 %all_to_all.10.in_ref = f32[32,8,256]{2,1,0:T(8,128)S(1)} all-to-all(f32[32,8,256]{2,1,0:T(8,128)S(1)} %bitcast.20), channel_id=1, replica_groups=mesh['px'=4,'py'=8] {'py','px'}, dimensions={0} | all-to-all | bytes 524288 | tf_op jit(solution)/shard_map/all_to_all | solution.py:808
  31.0 0.0 copy-done.1
  31.0 0.0 copy-done.2
  31.0 0.0 copy-done.3
  31.0 0.0 copy-done.4
  31.0 0.0 copy-done.5
  31.0 2.0 %solve_planes.1 = f32[32,8,256]{2,1,0:T(8,128)S(1)} custom-call(f32[32,8,256]{2,1,0:T(8,128)S(1)} %all_to_all.10.in_ref, bf16[64,192]{1,0:T(8,128)(2,1)S(1)} %copy-done.5, bf16[64,384]{1,0:T(8,128)(2,1)S(1)} %copy-done.3, bf16[768,128]{1,0:T(8,128)(2,1)S(1)} %copy-done.1, bf16[384,128]{1,0:T(8,128)(2,1)S(1)} %copy-done.2, f32[64,128]{1,0:T(8,128)S(1)} %copy-done.4, ...), custom_call_target="tpu_custom_call" | custom-call | tf_op jit(solution)/shard_map/solve_planes/pallas_call | solution.py:449
  33.1 12.7 %all_to_all.11 = f32[32,8,256]{2,1,0:T(8,128)S(1)} all-to-all(f32[32,8,256]{2,1,0:T(8,128)S(1)} %solve_planes.1), channel_id=1, replica_groups=mesh['px'=4,'py'=8] {'py','px'}, dimensions={0} | all-to-all | bytes 524288 | tf_op jit(solution)/shard_map/all_to_all | solution.py:810
  45.8 1.0 %pressure_cells.1 = f32[256,256]{1,0:T(8,128)} custom-call(f32[256,256]{1,0:T(8,128)S(1)} %bitcast.21, bf16[768,256]{1,0:T(8,128)(2,1)S(1)} %copy-done), custom_call_target="tpu_custom_call" | custom-call | tf_op jit(solution)/shard_map/pressure_cells/pallas_call | solution.py:485
  (19 shorter events, 0.3 us)
Async XLA Ops:
  1.2 8.0 %collective-permute-start.3 = (bf16[3,16,4,256]{3,2,0,1:T(4,128)(2,1)S(1)}, bf16[3,16,4,256]{3,2,0,1:T(4,128)(2,1)S(1)}, u32[]{:S(2)}, u32[]{:S(2)}) collective-permute-start(bf16[3,16,4,256]{3,2,0,1:T(4,128)(2,1)S(1)} %copy.21), channel_id=1, source_target_pairs={{0,1},{1,0},{2,3},{3,2},{4,5},{5,4},{6,7},{7,6},{8,9},{9,8},{10,11... | collective-permute-start | bytes 294920 | tf_op jit(solution)/shard_map/ppermute | solution.py:313
  1.8 7.4 %collective-permute-start.2 = (bf16[3,16,4,256]{3,2,0,1:T(4,128)(2,1)S(1)}, bf16[3,16,4,256]{3,2,0,1:T(4,128)(2,1)S(1)}, u32[]{:S(2)}, u32[]{:S(2)}) collective-permute-start(bf16[3,16,4,256]{3,2,0,1:T(4,128)(2,1)S(1)} %copy.20), channel_id=1, source_target_pairs={{0,7},{1,2},{2,1},{3,4},{4,3},{5,6},{6,5},{7,0},{8,15},{9,10},{10,... | collective-permute-start | bytes 294920 | tf_op jit(solution)/shard_map/ppermute | solution.py:312
  5.4 10.9 %collective-permute-start = (bf16[3,3,16,256]{3,2,1,0:T(8,128)(2,1)S(1)}, bf16[3,3,16,256]{3,2,1,0:T(8,128)(2,1)S(1)}, u32[]{:S(2)}, u32[]{:S(2)}) collective-permute-start(bf16[3,3,16,256]{3,2,1,0:T(8,128)(2,1)S(1)} %get-tuple-element.19), channel_id=1, source_target_pairs={{0,8},{8,16},{16,24},{24,0},{1,9},{9,17},{17,25},{25,1},{2,10},{10... | collective-permute-start | bytes 221192 | tf_op jit(solution)/shard_map/ppermute | solution.py:314
  7.0 9.3 %collective-permute-start.1 = (bf16[3,3,16,256]{3,2,1,0:T(8,128)(2,1)S(1)}, bf16[3,3,16,256]{3,2,1,0:T(8,128)(2,1)S(1)}, u32[]{:S(2)}, u32[]{:S(2)}) collective-permute-start(bf16[3,3,16,256]{3,2,1,0:T(8,128)(2,1)S(1)} %get-tuple-element.20), channel_id=1, source_target_pairs={{8,0},{16,8},{24,16},{0,24},{9,1},{17,9},{25,17},{1,25},{10,2},{18... | collective-permute-start | bytes 221192 | tf_op jit(solution)/shard_map/ppermute | solution.py:315
  9.4 6.9 %collective-permute-start.4 = (bf16[3,8,256]{2,1,0:T(8,128)(2,1)S(1)}, bf16[3,8,256]{2,1,0:T(8,128)(2,1)S(1)}, u32[]{:S(2)}, u32[]{:S(2)}) collective-permute-start(bf16[3,8,256]{2,1,0:T(8,128)(2,1)S(1)} %concatenate.6), channel_id=1, source_target_pairs={{0,8},{8,16},{16,24},{24,0},{1,9},{9,17},{17,25},{25,1},{2,10},{10... | collective-permute-start | bytes 36872 | tf_op jit(solution)/shard_map/ppermute | solution.py:325
  10.0 6.3 %collective-permute-start.5 = (bf16[3,8,256]{2,1,0:T(8,128)(2,1)S(1)}, bf16[3,8,256]{2,1,0:T(8,128)(2,1)S(1)}, u32[]{:S(2)}, u32[]{:S(2)}) collective-permute-start(bf16[3,8,256]{2,1,0:T(8,128)(2,1)S(1)} %concatenate.7), channel_id=1, source_target_pairs={{8,0},{16,8},{24,16},{0,24},{9,1},{17,9},{25,17},{1,25},{10,2},{18... | collective-permute-start | bytes 36872 | tf_op jit(solution)/shard_map/ppermute | solution.py:326
  16.3 14.7 %copy-start.1 = (bf16[768,128]{1,0:T(8,128)(2,1)S(1)}, bf16[768,128]{1,0:T(8,128)(2,1)}, u32[]{:S(2)}) copy-start(bf16[768,128]{1,0:T(8,128)(2,1)} %constant.59.clone.qy_ref) | copy-start | bytes 589828
  16.3 14.7 %copy-start.2 = (bf16[384,128]{1,0:T(8,128)(2,1)S(1)}, bf16[384,128]{1,0:T(8,128)(2,1)}, u32[]{:S(2)}) copy-start(bf16[384,128]{1,0:T(8,128)(2,1)} %constant.60.clone.qyt_ref) | copy-start | bytes 294916
  16.3 14.7 %copy-start.3 = (bf16[64,384]{1,0:T(8,128)(2,1)S(1)}, bf16[64,384]{1,0:T(8,128)(2,1)}, u32[]{:S(2)}) copy-start(bf16[64,384]{1,0:T(8,128)(2,1)} %constant.58.clone.qxt_ref) | copy-start | bytes 147460
  16.3 14.7 %copy-start.4 = (f32[64,128]{1,0:T(8,128)S(1)}, f32[64,128]{1,0:T(8,128)}, u32[]{:S(2)}) copy-start(f32[64,128]{1,0:T(8,128)} %constant.61.clone.ex_ref) | copy-start | bytes 98308
  16.3 14.7 %copy-start.5 = (bf16[64,192]{1,0:T(8,128)(2,1)S(1)}, bf16[64,192]{1,0:T(8,128)(2,1)}, u32[]{:S(2)}) copy-start(bf16[64,192]{1,0:T(8,128)(2,1)} %constant.57.clone.qx_ref) | copy-start | bytes 73732
  16.3 14.7 %copy-start.6 = (f32[8,128]{1,0:T(8,128)S(1)}, f32[8,128]{1,0:T(8,128)}, u32[]{:S(2)}) copy-start(f32[8,128]{1,0:T(8,128)} %constant.62.clone.ey_ref) | copy-start | bytes 12292
  16.4 14.7 %copy-start.7 = (f32[256]{0:T(256)S(1)}, f32[256]{0:T(256)}, u32[]{:S(2)}) copy-start(f32[256]{0:T(256)} %constant.63.clone.em_ref) | copy-start | bytes 3076
  17.9 27.8 %copy-start = (bf16[768,256]{1,0:T(8,128)(2,1)S(1)}, bf16[768,256]{1,0:T(8,128)(2,1)}, u32[]{:S(2)}) copy-start(bf16[768,256]{1,0:T(8,128)(2,1)} %constant.64.clone.basis_ref) | copy-start | bytes 1179652

commit v5 on v4

--- a/solution.py
+++ b/solution.py
@@ -171,6 +171,8 @@
         return total - whole[:rows] * u[:rows]
 
     east[x] = one(0, cells)
+    if part is None:
+        return
     north = one(1, nu.shape[0])
     up = one(2, cells)
     edge = centre[2][:cells]
@@ -179,11 +181,21 @@
     part[x] = (y_next(north) - y_prev(north))[:cells] + (z_next(up, top) - z_prev(up, bottom))
 
 
-def store_plane(c, x, plane, wind, above, below):
-    none = jnp.zeros((plane.shape[0], LANES), F32)
-    wind[c, x] = plane
-    above[c, x] = z_next(plane, none)
-    below[c, x] = z_prev(plane, none)
+def shift_table(levels):
+    level = lax.broadcasted_iota(jnp.int32, (levels, levels), 0)
+    moved = lax.broadcasted_iota(jnp.int32, (levels, levels), 1)
+    tables = [jnp.where(level == moved + step, 1.0, 0.0) for step in (1, -1)]
+    return jnp.concatenate(tables, axis=1).astype(BF16)
+
+
+def store_planes(places, planes, table, wind, above, below):
+    rows, levels = planes[0].shape
+    stacked = jnp.concatenate(planes, axis=0).astype(BF16)
+    moved = dot(stacked, table, ((1,), (0,)))
+    for i, ((c, x), plane) in enumerate(zip(places, planes)):
+        wind[c, x] = plane
+        above[c, x] = moved[i * rows : (i + 1) * rows, :levels]
+        below[c, x] = moved[i * rows : (i + 1) * rows, levels:]
 
 
 def by_parity(odd, body):
@@ -211,20 +223,24 @@
 
 
 def inner_kernel(place_ref, winds_ref, near_ref, far_ref, table_ref, *refs):
-    wind, above, below, visc, east, part, modes, basis_ref, source, sem = refs
+    wind, above, below, visc, east, part, modes, basis_ref, table, source, sem = refs
     fetch = pltpu.make_async_copy(table_ref, basis_ref, sem)
     fetch.start()
     cells_x, cells_y, levels = winds_ref.shape[1:]
 
+    table[...] = shift_table(levels)
+
     def load(odd):
         after_ref, before_ref = (far_ref, near_ref) if odd else (near_ref, far_ref)
 
         def plane(x):
             for c in range(3):
                 pieces = [winds_ref[c, x], after_ref[c, x], before_ref[c, x]]
-                own, after, before = [piece.astype(F32) for piece in pieces]
-                whole = jnp.concatenate([own, after, before], axis=0)
-                store_plane(c, x + HALO, whole, wind, above, below)
+                whole = jnp.concatenate([piece.astype(F32) for piece in pieces], axis=0)
+                none = jnp.zeros((whole.shape[0], LANES), F32)
+                wind[c, x + HALO] = whole
+                above[c, x + HALO] = z_next(whole, none)
+                below[c, x + HALO] = z_prev(whole, none)
 
         each(0, cells_x, plane, unroll=4)
 
@@ -236,27 +252,32 @@
     half_modes(EARLY, source, east, part, basis_ref, modes, 0)
 
 
-def outer_kernel(low_ref, high_ref, low_corner_ref, high_corner_ref, basis_ref, *refs):
-    wind, above, below, visc, east, part, modes, source = refs[7:]
+def side_kernel(side, planes_ref, corner_ref, table, *refs):
+    if side:
+        wind, above, below, visc, east, part, modes, source = refs[8:]
+        basis_ref = refs[0]
+    else:
+        wind, above, below, visc, east, part = refs[6:]
     levels = wind.shape[3]
-    cells_x = skip = wind.shape[1] - 2 * HALO
+    cells_x = wind.shape[1] - 2 * HALO
     row = lax.broadcasted_iota(jnp.int32, (8, levels), 0)
 
-    def load(c):
-        for side, ref, corner_ref in ((0, low_ref, low_corner_ref), (1, high_ref, high_corner_ref)):
-            nearest = corner_ref[c].astype(F32)
-            second = jnp.where(row < 4, pltpu.roll(nearest, 6, 0), pltpu.roll(nearest, 2, 0))
-            for i, rest in enumerate((nearest, second, jnp.zeros_like(nearest))):
-                index = i if side else HALO - 1 - i
-                plane = jnp.concatenate([ref[c, index].astype(F32), rest], axis=0)
-                start = HALO + cells_x if side else 0
-                store_plane(c, start + index, plane, wind, above, below)
-
-    each(0, 3, load)
-    each(1, 7, lambda x: visc_plane(x, wind, above, below, visc), 3, skip - 2, unroll=2)
-    each(2, 8, lambda x: wind_plane(x, wind, above, below, visc, east, part), 3, skip - 4, unroll=2)
-
-    half_modes(cells_x - EARLY, source, east, part, basis_ref, modes, 1)
+    places, planes = [], []
+    for c in range(3):
+        nearest = corner_ref[c].astype(F32)
+        second = jnp.where(row < 4, pltpu.roll(nearest, 6, 0), pltpu.roll(nearest, 2, 0))
+        for i, rest in enumerate((nearest, second, jnp.zeros_like(nearest))):
+            index = i if side else HALO - 1 - i
+            planes.append(jnp.concatenate([planes_ref[c, index].astype(F32), rest], axis=0))
+            places.append((c, index + (HALO + cells_x if side else 0)))
+    store_planes(places, planes, table[...], wind, above, below)
+    skip = cells_x + 1 if side else 0
+    each(1 + skip, 4 + skip, lambda x: visc_plane(x, wind, above, below, visc), unroll=3)
+    first = cells_x + 1 if side else HALO
+    each(first, first + 2, lambda x: wind_plane(x, wind, above, below, visc, east, part), unroll=2)
+    wind_plane(HALO + cells_x if side else 2, wind, above, below, visc, east, None)
+    if side:
+        half_modes(cells_x - EARLY, source, east, part, basis_ref, modes, 1)
 
 
 def pack_kernel(place_ref, *refs):
@@ -334,9 +355,9 @@
     basis = table_parts(basis_rows * np.float32(0.0625), 1, DCT_PARTS)
     state = pl.pallas_call(
         inner_kernel,
-        out_shape=shapes + [pltpu.VMEM(basis.shape, BF16)],
+        out_shape=shapes + [pltpu.VMEM(basis.shape, BF16), pltpu.VMEM((levels, 2 * levels), BF16)],
         in_specs=[smem] + [vmem] * 3 + [pl.BlockSpec(memory_space=pl.ANY)],
-        out_specs=[vmem] * 8,
+        out_specs=[vmem] * 9,
         scratch_shapes=scratch + [pltpu.SemaphoreType.DMA],
         cost_estimate=pl.CostEstimate(flops=40_000_000, bytes_accessed=6_000_000, transcendentals=0),
         compiler_params=KERNEL_VMEM,
@@ -346,23 +367,26 @@
         *[on_chip(got) for got in (stacked, inner_got, outer_got)],
         pltpu.with_memory_space_constraint(basis, pltpu.HBM),
     )
+    low_state = pl.pallas_call(
+        functools.partial(side_kernel, 0),
+        out_shape=shapes[:6],
+        in_specs=[vmem] * 9,
+        out_specs=[vmem] * 6,
+        input_output_aliases={3 + i: i for i in range(6)},
+        cost_estimate=pl.CostEstimate(flops=8_000_000, bytes_accessed=2_000_000, transcendentals=0),
+        compiler_params=KERNEL_VMEM,
+        name="low_planes",
+    )(*[on_chip(got) for got in (low, low_corner, state[8], *state[:6])])
     results = pl.pallas_call(
-        outer_kernel,
+        functools.partial(side_kernel, 1),
         out_shape=shapes,
-        in_specs=[vmem] * 12,
+        in_specs=[vmem] * 11,
         out_specs=[vmem] * 7,
-        input_output_aliases={5 + i: i for i in range(7)},
+        input_output_aliases={4 + i: i for i in range(7)},
         scratch_shapes=scratch,
         compiler_params=KERNEL_VMEM,
-        name="outer_planes",
-    )(
-        on_chip(low),
-        on_chip(high),
-        on_chip(low_corner),
-        on_chip(high_corner),
-        on_chip(state[7]),
-        *[on_chip(part) for part in state[:7]],
-    )
+        name="high_planes",
+    )(*[on_chip(got) for got in (high, high_corner, state[8], state[7], *low_state, state[6])])
     return results[6]
 
 

time: 46.9 us -> 46.2 us (0.985)
    ppermute x1, starting transfers between devices: 1.58 us -> 0.01 us  [source_modes(): low = lax.ppermute(last, 'px', up)]
    ppermute x1, starting transfers between devices: 2.25 us -> 3.6 us  [source_modes(): high = lax.ppermute(leading, 'px', down)]
    pallas_call x1 -> x2, Pallas kernels: 1.55 us -> 1.14 us  [the longest x1 0.75 us: source_modes(): pl.pallas_call(functools.partial(side_kernel, 1), out_shape=shapes, in_sp...]
  transfers between devices with their start and end apart: 6 -> 6, of which waited for: 0 -> 0; matrix products, arithmetic and copies ran while one was open for 1% -> 1% of each run, Pallas kernels for 6% -> 7%
where the time goes in v5:
time: 46.2 us; the launch traced here: 46 us
  blocking collectives  25.5 us (55%)
  starting transfers between devices  11.7 us (25%)
  Pallas kernels  8.12 us (18%)
    all_to_all x2, blocking collectives, shards(): lax.all_to_all(blocks, ('py', 'px'), split_axis=0, concat_axis=0, tiled=T...  25.5 us
    ppermute x1, starting transfers between devices, source_modes(): outer_got = lax.ppermute(outer_rows, 'py', outer)  3.61 us
    ppermute x1, starting transfers between devices, source_modes(): high = lax.ppermute(leading, 'px', down)  3.6 us
    ppermute x1, starting transfers between devices, source_modes(): high_corner = lax.ppermute(corner(0, 1), 'px', down)  3.22 us
    pallas_call x1, Pallas kernels, source_modes(): pl.pallas_call(inner_kernel, out_shape=shapes + [pltpu.VMEM(basis.shape,...  2.81 us
    pallas_call x1, Pallas kernels, solve_planes(): pl.pallas_call(functools.partial(solve_kernel, east_count, north_count, c...  2.05 us
    pallas_call x1, Pallas kernels, pack_winds(): pl.pallas_call(pack_kernel, out_shape=[pltpu.VMEM((3, cells_x, cells_y, l...  1.12 us
    pallas_call x1, Pallas kernels, pressure_cells(): pl.pallas_call(functools.partial(pressure_kernel, shift), out_shape=jax.S...  1.01 us
  transfers between devices with their start and end apart: 6, of which 0 were waited for; matrix products, arithmetic and copies ran while one was open for 1% of the time, Pallas kernels for 7%

profile of v5, /device:TPU:0, one launch (start us, length us, event | category | flops | bytes accessed | tf_op | source)
XLA Modules:
  0.0 46.0 jit_solution(6423505166983184333)
XLA Ops:
  0.0 1.1 %pack_winds.1 = (bf16[3,16,16,256]{3,2,1,0:T(8,128)(2,1)S(1)}, bf16[3,16,4,256]{3,2,1,0:T(4,128)(2,1)S(1)}, bf16[3,16,4,256]{3,2,1,0:T(4,128)(2,1)S(1)}, bf16[3,...) custom-call(s32[1]{0:T(128)} %bitcast.place_ref, bf16[16,16,256]{2,1,0:T(8,128)(2,1)} %refs_0_.1, ...), custom_call_target="tpu_custom_call" | custom-call | tf_op jit(solution)/shard_map/pack_winds/pallas_call | solution.py:313
  1.2 0.6 %collective-permute-start.2 = (bf16[3,16,4,256]{3,2,0,1:T(4,128)(2,1)S(1)}, bf16[3,16,4,256]{3,2,0,1:T(4,128)(2,1)S(1)}, u32[]{:S(2)}, u32[]{:S(2)}) collective-permute-start(bf16[3,16,4,256]{3,2,0,1:T(4,128)(2,1)S(1)} %copy.27), channel_id=1, source_target_pairs={{0,1},{1,0},{2,3},{3,2},{4,5},{5,4},{6,7},{7,6},{8,9},{9,8},{10,11... | collective-permute-start | bytes 294920 | tf_op jit(solution)/shard_map/ppermute | solution.py:334
  1.8 3.6 %collective-permute-start.1 = (bf16[3,16,4,256]{3,2,0,1:T(4,128)(2,1)S(1)}, bf16[3,16,4,256]{3,2,0,1:T(4,128)(2,1)S(1)}, u32[]{:S(2)}, u32[]{:S(2)}) collective-permute-start(bf16[3,16,4,256]{3,2,0,1:T(4,128)(2,1)S(1)} %copy.26), channel_id=1, source_target_pairs={{0,7},{1,2},{2,1},{3,4},{4,3},{5,6},{6,5},{7,0},{8,15},{9,10},{10,... | collective-permute-start | bytes 294920 | tf_op jit(solution)/shard_map/ppermute | solution.py:333
  5.4 3.6 %collective-permute-start = (bf16[3,3,16,256]{3,2,1,0:T(8,128)(2,1)S(1)}, bf16[3,3,16,256]{3,2,1,0:T(8,128)(2,1)S(1)}, u32[]{:S(2)}, u32[]{:S(2)}) collective-permute-start(bf16[3,3,16,256]{3,2,1,0:T(8,128)(2,1)S(1)} %get-tuple-element.26), channel_id=1, source_target_pairs={{8,0},{16,8},{24,16},{0,24},{9,1},{17,9},{25,17},{1,25},{10,2},{18... | collective-permute-start | bytes 221192 | tf_op jit(solution)/shard_map/ppermute | solution.py:336
  9.0 0.0 collective-permute-start.4
  9.0 0.0 collective-permute-done.2
  9.0 0.0 collective-permute-done.1
  9.1 0.7 %collective-permute-start.5 = (bf16[3,8,256]{2,1,0:T(8,128)(2,1)S(1)}, bf16[3,8,256]{2,1,0:T(8,128)(2,1)S(1)}, u32[]{:S(2)}, u32[]{:S(2)}) collective-permute-start(bf16[3,8,256]{2,1,0:T(8,128)(2,1)S(1)} %concatenate.7), channel_id=1, source_target_pairs={{0,8},{8,16},{16,24},{24,0},{1,9},{9,17},{17,25},{25,1},{2,10},{10... | collective-permute-start | bytes 36872 | tf_op jit(solution)/shard_map/ppermute | solution.py:346
  10.0 3.2 %collective-permute-start.3 = (bf16[3,8,256]{2,1,0:T(8,128)(2,1)S(1)}, bf16[3,8,256]{2,1,0:T(8,128)(2,1)S(1)}, u32[]{:S(2)}, u32[]{:S(2)}) collective-permute-start(bf16[3,8,256]{2,1,0:T(8,128)(2,1)S(1)} %concatenate.6), channel_id=1, source_target_pairs={{8,0},{16,8},{24,16},{0,24},{9,1},{17,9},{25,17},{1,25},{10,2},{18... | collective-permute-start | bytes 36872 | tf_op jit(solution)/shard_map/ppermute | solution.py:347
  13.3 2.8 %inner_planes.1 = (f32[3,22,24,256]{3,2,1,0:T(8,128)S(1)}, f32[3,22,24,256]{3,2,1,0:T(8,128)S(1)}, f32[3,22,24,256]{3,2,1,0:T(8,128)S(1)}, f32[22,24,256]{2,1,0:...) custom-call(s32[1]{0:T(128)} %bitcast.place_ref, ...), custom_call_target="tpu_custom_call" | custom-call | flops 40000000 | bytes 6000000 | tf_op jit(solution)/shard_map/inner_planes/pallas_call | solution.py:356
  16.1 0.0 collective-permute-done.4.planes_ref
  16.1 0.0 collective-permute-done.5.corner_ref
  16.1 0.4 low_planes.1
  16.5 0.0 collective-permute-done.planes_ref
  16.5 0.0 collective-permute-done.3.corner_ref
  16.5 0.0 copy-start.1
  16.5 0.0 copy-start.2
  16.5 0.0 copy-start.3
  16.5 0.0 copy-start.4
  16.6 0.0 copy-start.5
  16.6 0.0 copy-start.6
  16.6 0.0 copy-start.7
  16.6 0.8 %high_planes.1 = (f32[3,22,24,256]{3,2,1,0:T(8,128)S(1)}, f32[3,22,24,256]{3,2,1,0:T(8,128)S(1)}, f32[3,22,24,256]{3,2,1,0:T(8,128)S(1)}, f32[22,24,256]{2,1,0:T...) custom-call(bf16[3,3,16,256]{3,2,1,0:T(8,128)(2,1)S(1)} %collective-, ...), custom_call_target="tpu_custom_call", output_to_operand_aliasing={{0}: (4, {}), {1}: (5, {}), {2}: (6, {}), {3}: (7, {}), {4}... | custom-call | tf_op jit(solution)/shard_map/high_planes/pallas_call | solution.py:380
  17.4 0.0 copy-start
  17.4 12.8 %all_to_all.10.in_ref = f32[32,8,256]{2,1,0:T(8,128)S(1)} all-to-all(f32[32,8,256]{2,1,0:T(8,128)S(1)} %bitcast.20), channel_id=1, replica_groups=mesh['px'=4,'py'=8] {'py','px'}, dimensions={0} | all-to-all | bytes 524288 | tf_op jit(solution)/shard_map/all_to_all | solution.py:832
  30.2 0.0 copy-done.1
  30.2 0.0 copy-done.2
  30.2 0.0 copy-done.3
  30.2 0.0 copy-done.4
  30.2 2.0 %solve_planes.1 = f32[32,8,256]{2,1,0:T(8,128)S(1)} custom-call(f32[32,8,256]{2,1,0:T(8,128)S(1)} %all_to_all.10.in_ref, bf16[64,192]{1,0:T(8,128)(2,1)S(1)} %copy-done.5, bf16[64,384]{1,0:T(8,128)(2,1)S(1)} %copy-done.3, bf16[768,128]{1,0:T(8,128)(2,1)S(1)} %copy-done.1, bf16[384,128]{1,0:T(8,128)(2,1)S(1)} %copy-done.2, f32[64,128]{1,0:T(8,128)S(1)} %copy-done.4, ...), custom_call_target="tpu_custom_call" | custom-call | tf_op jit(solution)/shard_map/solve_planes/pallas_call | solution.py:473
  32.3 12.7 %all_to_all.11 = f32[32,8,256]{2,1,0:T(8,128)S(1)} all-to-all(f32[32,8,256]{2,1,0:T(8,128)S(1)} %solve_planes.1), channel_id=1, replica_groups=mesh['px'=4,'py'=8] {'py','px'}, dimensions={0} | all-to-all | bytes 524288 | tf_op jit(solution)/shard_map/all_to_all | solution.py:834
  45.0 1.0 %pressure_cells.1 = f32[256,256]{1,0:T(8,128)} custom-call(f32[256,256]{1,0:T(8,128)S(1)} %bitcast.21, bf16[768,256]{1,0:T(8,128)(2,1)S(1)} %copy-done), custom_call_target="tpu_custom_call" | custom-call | tf_op jit(solution)/shard_map/pressure_cells/pallas_call | solution.py:509
  (20 shorter events, 0.3 us)
Async XLA Ops:
  1.2 7.8 %collective-permute-start.2 = (bf16[3,16,4,256]{3,2,0,1:T(4,128)(2,1)S(1)}, bf16[3,16,4,256]{3,2,0,1:T(4,128)(2,1)S(1)}, u32[]{:S(2)}, u32[]{:S(2)}) collective-permute-start(bf16[3,16,4,256]{3,2,0,1:T(4,128)(2,1)S(1)} %copy.27), channel_id=1, source_target_pairs={{0,1},{1,0},{2,3},{3,2},{4,5},{5,4},{6,7},{7,6},{8,9},{9,8},{10,11... | collective-permute-start | bytes 294920 | tf_op jit(solution)/shard_map/ppermute | solution.py:334
  1.8 7.2 %collective-permute-start.1 = (bf16[3,16,4,256]{3,2,0,1:T(4,128)(2,1)S(1)}, bf16[3,16,4,256]{3,2,0,1:T(4,128)(2,1)S(1)}, u32[]{:S(2)}, u32[]{:S(2)}) collective-permute-start(bf16[3,16,4,256]{3,2,0,1:T(4,128)(2,1)S(1)} %copy.26), channel_id=1, source_target_pairs={{0,7},{1,2},{2,1},{3,4},{4,3},{5,6},{6,5},{7,0},{8,15},{9,10},{10,... | collective-permute-start | bytes 294920 | tf_op jit(solution)/shard_map/ppermute | solution.py:333
  5.4 11.1 %collective-permute-start = (bf16[3,3,16,256]{3,2,1,0:T(8,128)(2,1)S(1)}, bf16[3,3,16,256]{3,2,1,0:T(8,128)(2,1)S(1)}, u32[]{:S(2)}, u32[]{:S(2)}) collective-permute-start(bf16[3,3,16,256]{3,2,1,0:T(8,128)(2,1)S(1)} %get-tuple-element.26), channel_id=1, source_target_pairs={{8,0},{16,8},{24,16},{0,24},{9,1},{17,9},{25,17},{1,25},{10,2},{18... | collective-permute-start | bytes 221192 | tf_op jit(solution)/shard_map/ppermute | solution.py:336
  9.0 7.1 %collective-permute-start.4 = (bf16[3,3,16,256]{3,2,1,0:T(8,128)(2,1)S(1)}, bf16[3,3,16,256]{3,2,1,0:T(8,128)(2,1)S(1)}, u32[]{:S(2)}, u32[]{:S(2)}) collective-permute-start(bf16[3,3,16,256]{3,2,1,0:T(8,128)(2,1)S(1)} %get-tuple-element.32), channel_id=1, source_target_pairs={{0,8},{8,16},{16,24},{24,0},{1,9},{9,17},{17,25},{25,1},{2,10},{10... | collective-permute-start | bytes 221192 | tf_op jit(solution)/shard_map/ppermute | solution.py:335
  9.1 6.9 %collective-permute-start.5 = (bf16[3,8,256]{2,1,0:T(8,128)(2,1)S(1)}, bf16[3,8,256]{2,1,0:T(8,128)(2,1)S(1)}, u32[]{:S(2)}, u32[]{:S(2)}) collective-permute-start(bf16[3,8,256]{2,1,0:T(8,128)(2,1)S(1)} %concatenate.7), channel_id=1, source_target_pairs={{0,8},{8,16},{16,24},{24,0},{1,9},{9,17},{17,25},{25,1},{2,10},{10... | collective-permute-start | bytes 36872 | tf_op jit(solution)/shard_map/ppermute | solution.py:346
  10.0 6.5 %collective-permute-start.3 = (bf16[3,8,256]{2,1,0:T(8,128)(2,1)S(1)}, bf16[3,8,256]{2,1,0:T(8,128)(2,1)S(1)}, u32[]{:S(2)}, u32[]{:S(2)}) collective-permute-start(bf16[3,8,256]{2,1,0:T(8,128)(2,1)S(1)} %concatenate.6), channel_id=1, source_target_pairs={{8,0},{16,8},{24,16},{0,24},{9,1},{17,9},{25,17},{1,25},{10,2},{18... | collective-permute-start | bytes 36872 | tf_op jit(solution)/shard_map/ppermute | solution.py:347
  16.5 13.7 %copy-start.1 = (bf16[768,128]{1,0:T(8,128)(2,1)S(1)}, bf16[768,128]{1,0:T(8,128)(2,1)}, u32[]{:S(2)}) copy-start(bf16[768,128]{1,0:T(8,128)(2,1)} %constant.59.clone.qy_ref) | copy-start | bytes 589828
  16.5 13.7 %copy-start.2 = (bf16[384,128]{1,0:T(8,128)(2,1)S(1)}, bf16[384,128]{1,0:T(8,128)(2,1)}, u32[]{:S(2)}) copy-start(bf16[384,128]{1,0:T(8,128)(2,1)} %constant.60.clone.qyt_ref) | copy-start | bytes 294916
  16.5 13.6 %copy-start.3 = (bf16[64,384]{1,0:T(8,128)(2,1)S(1)}, bf16[64,384]{1,0:T(8,128)(2,1)}, u32[]{:S(2)}) copy-start(bf16[64,384]{1,0:T(8,128)(2,1)} %constant.58.clone.qxt_ref) | copy-start | bytes 147460
  16.5 13.6 %copy-start.4 = (f32[64,128]{1,0:T(8,128)S(1)}, f32[64,128]{1,0:T(8,128)}, u32[]{:S(2)}) copy-start(f32[64,128]{1,0:T(8,128)} %constant.61.clone.ex_ref) | copy-start | bytes 98308
  16.6 13.6 %copy-start.5 = (bf16[64,192]{1,0:T(8,128)(2,1)S(1)}, bf16[64,192]{1,0:T(8,128)(2,1)}, u32[]{:S(2)}) copy-start(bf16[64,192]{1,0:T(8,128)(2,1)} %constant.57.clone.qx_ref) | copy-start | bytes 73732
  16.6 13.6 %copy-start.6 = (f32[8,128]{1,0:T(8,128)S(1)}, f32[8,128]{1,0:T(8,128)}, u32[]{:S(2)}) copy-start(f32[8,128]{1,0:T(8,128)} %constant.62.clone.ey_ref) | copy-start | bytes 12292
  16.6 13.6 %copy-start.7 = (f32[256]{0:T(256)S(1)}, f32[256]{0:T(256)}, u32[]{:S(2)}) copy-start(f32[256]{0:T(256)} %constant.63.clone.em_ref) | copy-start | bytes 3076
  17.4 27.6 %copy-start = (bf16[768,256]{1,0:T(8,128)(2,1)S(1)}, bf16[768,256]{1,0:T(8,128)(2,1)}, u32[]{:S(2)}) copy-start(bf16[768,256]{1,0:T(8,128)(2,1)} %constant.64.clone.basis_ref) | copy-start | bytes 1179652
